TPU v7x, 1024 devices: a whole 8x8x8 slice. The times are simulated.
1024 devices in a mesh: py: 64 (over z, y), pz: 16 (over x, core).
Axes of the slice: x: 8, y: 8, z: 8, core: 2. Of those that a mesh axis runs over, the one named last changes fastest.
Arguments:
- velocity: float32 [3, 256, 128, 512], P(None, 'py', 'pz'), may hold values from -24 to 24
- fraction: float32 [256, 128, 512], P('py', 'pz'), may hold values from 0 to 1
- wall_flags: int32 [2, 256, 128], P(None, 'py', 'pz'), may hold values from 0 to 1
Outputs:
- velocity_next: float32 [3, 256, 128, 512], P(None, 'py', 'pz')
- pressure_step: float32 [256, 128, 512], P('py', 'pz')
Inputs may be any that keep to these rules, and one draw needn't show every extreme that they name: `wall_flags`: 1 marks a free-slip wall, 0 a no-slip wall.
All inputs are finite; a program needn't handle non-finite values.
Results may differ from a plain program's by a relative error of at most 0.0003.
Values sent between devices are 32-bit elements; how exact they have to be, the bound alone decides.
No kernel may reach another device: no remote copies, remote signals or barrier semaphores. Data moves between devices by JAX's collectives and lax.ppermute only.
A program may use at most 32 MiB of HBM per device.

v0:
```python
import math

import jax
import jax.numpy as jnp
from jax import lax
from jax.sharding import PartitionSpec as P

NX = 512
ITERS = 2


time_step = 0.05
heavy_density = 8.0
light_viscosity = 0.3
heavy_viscosity = 0.6
compressibility = 0.001
mean_inverse = 0.5
weno_epsilon = 1e-06
highest = lax.Precision.HIGHEST


def with_halo(cells, sides, width):
    for axis, dim in sides:
        count = lax.axis_size(axis)
        ends = count - 1
        head = lax.slice_in_dim(cells, 0, width, axis=dim)
        tail = lax.slice_in_dim(cells, cells.shape[dim] - width, cells.shape[dim], axis=dim)
        cells = jnp.concatenate(
            [
                lax.ppermute(tail, axis, [(i, (i + 1) % count) for i in range(ends)]),
                cells,
                lax.ppermute(head, axis, [((i + 1) % count, i) for i in range(ends)]),
            ],
            axis=dim,
        )
    return cells


def weno_blend(slope_one, slope_two, slope_three, slope_four, slope_five):
    smooth_one = (
        13.0 / 12.0 * (slope_one - 2.0 * slope_two + slope_three) ** 2
        + 0.25 * (slope_one - 4.0 * slope_two + 3.0 * slope_three) ** 2
    )
    smooth_two = (
        13.0 / 12.0 * (slope_two - 2.0 * slope_three + slope_four) ** 2
        + 0.25 * (slope_two - slope_four) ** 2
    )
    smooth_three = (
        13.0 / 12.0 * (slope_three - 2.0 * slope_four + slope_five) ** 2
        + 0.25 * (3.0 * slope_three - 4.0 * slope_four + slope_five) ** 2
    )
    alpha_one = 0.1 / (weno_epsilon + smooth_one) ** 2
    alpha_two = 0.6 / (weno_epsilon + smooth_two) ** 2
    alpha_three = 0.3 / (weno_epsilon + smooth_three) ** 2
    weight_sum = alpha_one + alpha_two + alpha_three
    blended = alpha_one * (slope_one / 3.0 - 7.0 * slope_two / 6.0 + 11.0 * slope_three / 6.0)
    blended = blended + alpha_two * (-slope_two / 6.0 + 5.0 * slope_three / 6.0 + slope_four / 3.0)
    blended = blended + alpha_three * (
        slope_three / 3.0 + 5.0 * slope_four / 6.0 - slope_five / 6.0
    )
    return blended / weight_sum


def upwind_derivative(padded, direction_axis, advecting):
    length = padded.shape[direction_axis] - 6
    differences = jnp.diff(padded, axis=direction_axis)

    def window(offset):
        return lax.slice_in_dim(differences, offset, offset + length, axis=direction_axis)

    lower_side = weno_blend(window(0), window(1), window(2), window(3), window(4))
    upper_side = weno_blend(window(5), window(4), window(3), window(2), window(1))
    return jnp.where(advecting > 0, lower_side, upper_side)


def predicted(center, along_x, along_y, along_z, fraction):
    slope_x = upwind_derivative(along_x, 3, center[0][None])
    slope_y = upwind_derivative(along_y, 1, center[1][None])
    slope_z = upwind_derivative(along_z, 2, center[2][None])
    transport = center[0] * slope_x + center[1] * slope_y + center[2] * slope_z
    spread = along_x[..., 4:-2] + along_x[..., 2:-4] - 2.0 * center
    spread = spread + (along_y[:, 4:-2] + along_y[:, 2:-4] - 2.0 * center)
    spread = spread + (along_z[:, :, 4:-2] + along_z[:, :, 2:-4] - 2.0 * center)
    density = 1.0 + (heavy_density - 1.0) * fraction
    kinematic = (light_viscosity + (heavy_viscosity - light_viscosity) * fraction) / density
    return center + time_step * (kinematic * spread - transport)


def wall_ghosts(velocity, wall_flags):
    tangential = 2.0 * wall_flags.astype(jnp.float32) - 1.0
    normal = -jnp.ones_like(tangential)
    mirror_signs = jnp.stack([normal, tangential, tangential])
    lower_ghost = velocity[..., :3][..., ::-1] * mirror_signs[:, 0, :, :, None]
    upper_ghost = velocity[..., -3:][..., ::-1] * mirror_signs[:, 1, :, :, None]
    return jnp.concatenate([lower_ghost, velocity, upper_ghost], axis=-1)


def faces(stacked):
    return with_halo(stacked, (("py", 1), ("pz", 2)), 1)


def face_weights(fraction_rim, row_start, col_start, total_rows, total_cols):
    density_rim = 1.0 + (heavy_density - 1.0) * fraction_rim
    density = density_rim[3:-3, 3:-3]
    rows_local, cols_local = (density.shape[0], density.shape[1])
    inner_x = 2.0 / (density[:, :, 1:] + density[:, :, :-1])
    plus_x = jnp.concatenate([inner_x, jnp.zeros_like(density[:, :, :1])], axis=2)
    global_row = row_start + jnp.arange(rows_local, dtype=jnp.int32)[:, None, None]
    global_col = col_start + jnp.arange(cols_local, dtype=jnp.int32)[None, :, None]
    plus_y = jnp.where(global_row == total_rows - 1, 0.0, 2.0 / (density + density_rim[4:-2, 3:-3]))
    minus_y = jnp.where(global_row == 0, 0.0, 2.0 / (density + density_rim[2:-4, 3:-3]))
    plus_z = jnp.where(global_col == total_cols - 1, 0.0, 2.0 / (density + density_rim[3:-3, 4:-2]))
    minus_z = jnp.where(global_col == 0, 0.0, 2.0 / (density + density_rim[3:-3, 2:-4]))
    return (plus_x, plus_y, minus_y, plus_z, minus_z)


def face_fluxes(values, weights):
    plus_x, plus_y, minus_y, plus_z, minus_z = weights
    rimmed = faces(values[None])[0]
    forward_x = plus_x * (jnp.roll(values, -1, axis=2) - values)
    backward_x = jnp.roll(forward_x, 1, axis=2)
    forward_y = plus_y * (rimmed[2:, 1:-1] - values)
    backward_y = minus_y * (values - rimmed[:-2, 1:-1])
    forward_z = plus_z * (rimmed[1:-1, 2:] - values)
    backward_z = minus_z * (values - rimmed[1:-1, :-2])
    return (forward_x, backward_x, forward_y, backward_y, forward_z, backward_z)


def apply_operator(values, weights):
    forward_x, backward_x, forward_y, backward_y, forward_z, backward_z = face_fluxes(
        values, weights
    )
    return compressibility * values - (
        forward_x - backward_x + (forward_y - backward_y) + (forward_z - backward_z)
    )


def divergence_source(provisional):
    normal_x = provisional[0]
    forward_x = jnp.concatenate([normal_x[:, :, 1:], -normal_x[:, :, -1:]], axis=2)
    backward_x = jnp.concatenate([-normal_x[:, :, :1], normal_x[:, :, :-1]], axis=2)
    rimmed = faces(provisional[1:])
    spread_x = 0.5 * (forward_x - backward_x)
    spread_y = 0.5 * (rimmed[0, 2:, 1:-1] - rimmed[0, :-2, 1:-1])
    spread_z = 0.5 * (rimmed[1, 1:-1, 2:] - rimmed[1, 1:-1, :-2])
    return -(spread_x + spread_y + spread_z)


def cosine_table(length):
    wave_index = jnp.arange(length, dtype=jnp.int32)[:, None]
    position = jnp.arange(length, dtype=jnp.int32)[None, :]
    phase_count = wave_index * (2 * position + 1) % (4 * length)
    phase_angle = math.pi / (2 * length) * phase_count.astype(jnp.float32)
    weight = jnp.where(wave_index == 0, math.sqrt(1.0 / length), math.sqrt(2.0 / length))
    return weight * jnp.cos(phase_angle)


def eigenvalue(wave_index, length):
    return 2.0 - 2.0 * jnp.cos(math.pi / length * wave_index.astype(jnp.float32))


def residual_inner(left_field, right_field):
    return lax.psum(jnp.sum(left_field * right_field), ("py", "pz"))


def curvature_inner(left_field, right_field):
    return lax.psum(jnp.sum(left_field * right_field), ("py", "pz"))


def on_device(velocity, fraction, wall_flags):
    rows_local, cols_local = (fraction.shape[0], fraction.shape[1])
    rows_devices = lax.axis_size("py")
    cols_devices = lax.axis_size("pz")
    total_rows = rows_local * rows_devices
    total_cols = cols_local * cols_devices
    row_index = lax.axis_index("py")
    col_index = lax.axis_index("pz")
    bundle = jnp.concatenate([velocity, fraction[None]], axis=0)
    rimmed = with_halo(bundle, (("py", 1), ("pz", 2)), 3)
    provisional = predicted(
        velocity,
        wall_ghosts(velocity, wall_flags),
        rimmed[:3, :, 3:-3],
        rimmed[:3, 3:-3, :],
        fraction,
    )
    weights = face_weights(
        rimmed[3], row_index * rows_local, col_index * cols_local, total_rows, total_cols
    )
    source = divergence_source(provisional)
    table_x = cosine_table(NX)
    table_y = cosine_table(total_rows)
    table_z = cosine_table(total_cols)
    part_x = NX // rows_devices
    part_y = total_rows // cols_devices
    wave_y = col_index * part_y + jnp.arange(part_y, dtype=jnp.int32)
    wave_z = jnp.arange(total_cols, dtype=jnp.int32)
    wave_x = row_index * part_x + jnp.arange(part_x, dtype=jnp.int32)
    denominator = compressibility + mean_inverse * (
        eigenvalue(wave_y, total_rows)[:, None, None]
        + eigenvalue(wave_z, total_cols)[None, :, None]
        + eigenvalue(wave_x, NX)[None, None, :]
    )

    def precondition(values):
        spectral = jnp.einsum("yzm,km->yzk", values, table_x, precision=highest)
        spectral = lax.all_to_all(spectral, "py", split_axis=2, concat_axis=0, tiled=True)
        spectral = jnp.dot(table_y, spectral.reshape(total_rows, -1), precision=highest)
        spectral = lax.all_to_all(spectral, "pz", split_axis=0, concat_axis=1, tiled=True)
        spectral = jnp.einsum(
            "kz,yzx->ykx", table_z, spectral.reshape(part_y, total_cols, part_x), precision=highest
        )
        spectral = spectral / denominator
        spectral = jnp.einsum("kz,ykx->yzx", table_z, spectral, precision=highest).reshape(
            part_y, -1
        )
        spectral = lax.all_to_all(spectral, "pz", split_axis=1, concat_axis=0, tiled=True)
        spectral = jnp.einsum("ky,kc->yc", table_y, spectral, precision=highest)
        spectral = lax.all_to_all(
            spectral.reshape(total_rows, cols_local, part_x),
            "py",
            split_axis=0,
            concat_axis=2,
            tiled=True,
        )
        return jnp.einsum("yzk,km->yzm", spectral, table_x, precision=highest)

    solution = jnp.zeros_like(source)
    residual = source
    search = precondition(residual)
    aligned = residual_inner(residual, search)
    direction = search
    for iteration in range(ITERS):
        applied = apply_operator(direction, weights)
        step_size = aligned / curvature_inner(direction, applied)
        solution = solution + step_size * direction
        if iteration + 1 < ITERS:
            residual = residual - step_size * applied
            search = precondition(residual)
            renewed = residual_inner(residual, search)
            direction = search + renewed / aligned * direction
            aligned = renewed
    forward_x, backward_x, forward_y, backward_y, forward_z, backward_z = face_fluxes(
        solution, weights
    )
    correction = jnp.stack(
        [
            0.5 * (forward_x + backward_x),
            0.5 * (forward_y + backward_y),
            0.5 * (forward_z + backward_z),
        ]
    )
    return (provisional - correction, solution)


def solution(mesh):
    in_specs = (P(None, "py", "pz", None), P("py", "pz", None), P(None, "py", "pz"))
    out_specs = (P(None, "py", "pz", None), P("py", "pz", None))
    return jax.shard_map(
        on_device, mesh=mesh, in_specs=in_specs, out_specs=out_specs, check_vma=False
    )
```

profile of v0, /device:TPU:1, one launch (start us, length us, event | category | flops | bytes accessed | tf_op | source)
XLA Modules:
  0.0 627.6 jit_solution(12384922500222754246)
XLA Ops:
  1.7 4.1 collective-permute-start.1
  12.5 14.3 %collective-permute-start.2 = (f32[4,10,3,512]{3,2,1,0:T(4,128)S(1)}, f32[4,10,3,512]{3,2,1,0:T(4,128)S(1)}, u32[]{:S(2)}, u32[]{:S(2)}) collective-permute-start(f32[4,10,3,512]{3,2,1,0:T(4,128)S(1)} %get-tuple-element.11), channel_id=1, source_target_pairs={{1,0},{2,1},{3,2},{4,3},{5,4},{6,5},{7,6},{8,7},{9,8},{10,9},{11,1... | collective-permute-start | bytes 737288 | tf_op jit(solution)/shard_map/ppermute | solution.py:32
  28.8 3.9 collective-permute-done.3
  44.0 5.7 collective-permute-start.7
  50.7 4.9 fusion.17
  57.7 16.6 %all-to-all-start = ((f32[64,1,256]{2,1,0:T(1,128)}), f32[64,1,256]{2,1,0:T(1,128)S(1)}, u32[]{:S(2)}, u32[]{:S(2)}) async-start(f32[64,1,256]{2,1,0:T(1,128)} %reshape.236), calls=%async_computation | async-start | bytes 131072 | tf_op jit(solution)/shard_map/all_to_all | solution.py:207
  74.3 11.1 %all-to-all-done = f32[64,1,256]{2,1,0:T(1,128)S(1)} async-done(((f32[64,1,256]{2,1,0:T(1,128)}), f32[64,1,256]{2,1,0:T(1,128)S(1)}, u32[]{:S(2)}, u32[]{:S(2)}) %all-to-all-start) | async-done | bytes 65568 | tf_op jit(solution)/shard_map/all_to_all | solution.py:207
  90.8 11.8 %all-to-all-start.1 = ((f32[16,1,1024]{2,1,0:T(1,128)}), f32[16,1,1024]{2,1,0:T(1,128)S(1)}, u32[]{:S(2)}, u32[]{:S(2)}) async-start(f32[16,1,1024]{2,1,0:T(1,128)} %reshape.238), calls=%async_computation.1 | async-start | bytes 131072 | tf_op jit(solution)/shard_map/all_to_all | solution.py:209
  102.7 7.7 %all-to-all-done.1 = f32[16,1,1024]{2,1,0:T(1,128)S(1)} async-done(((f32[16,1,1024]{2,1,0:T(1,128)}), f32[16,1,1024]{2,1,0:T(1,128)S(1)}, u32[]{:S(2)}, u32[]{:S(2)}) %all-to-all-start.1) | async-done | bytes 65568 | tf_op jit(solution)/shard_map/all_to_all | solution.py:209
  117.3 7.8 %all-to-all-done.2 = f32[16,1,1024]{2,1,0:T(1,128)S(1)} async-done(((f32[16,1,1024]{2,1,0:T(1,128)}), f32[16,1,1024]{2,1,0:T(1,128)S(1)}, u32[]{:S(2)}, u32[]{:S(2)}) %all-to-all-start.2) | async-done | bytes 65568 | tf_op jit(solution)/shard_map/all_to_all | solution.py:217
  128.9 5.0 all-to-all-start.3
  134.8 10.3 %all-to-all-done.3 = f32[64,1,256]{2,1,0:T(1,128)S(1)} async-done(((f32[64,1,256]{2,1,0:T(1,128)}), f32[64,1,256]{2,1,0:T(1,128)S(1)}, u32[]{:S(2)}, u32[]{:S(2)}) %all-to-all-start.3) | async-done | bytes 65568 | tf_op jit(solution)/shard_map/all_to_all | solution.py:219
  147.5 4.6 fusion.15
  159.0 4.8 collective-permute-start.10
  169.7 113.4 %all-reduce.1 = (f32[]{:T(128)}, f32[]{:T(128)}) all-reduce(f32[]{:T(128)} %get-tuple-element.3, f32[]{:T(128)} %get-tuple-element.2), channel_id=1, replica_groups=mesh['py'=64,'pz'=16] {'py','pz'}, use_global_device_ids=true, to_apply=%region_1.2 | all-reduce | flops 2 | bytes 16 | tf_op jit(solution)/shard_map/psum | solution.py:163
  284.3 4.9 fusion.13
  290.7 17.0 %all_to_all.130 = f32[64,1,256]{2,1,0:T(1,128)S(1)} all-to-all(f32[64,1,256]{2,1,0:T(1,128)S(1)} %reshape.244), channel_id=1, replica_groups=mesh['py'=64,'pz'=16] {'py'}, dimensions={0} | all-to-all | bytes 131072 | tf_op jit(solution)/shard_map/all_to_all | solution.py:207
  311.9 14.9 %all_to_all.131 = f32[16,1,1024]{2,1,0:T(1,128)S(1)} all-to-all(f32[16,1,1024]{2,1,0:T(1,128)S(1)} %reshape.246), channel_id=1, replica_groups=mesh['py'=64,'pz'=16] {'pz'}, dimensions={0} | all-to-all | bytes 131072 | tf_op jit(solution)/shard_map/all_to_all | solution.py:209
  329.7 10.3 %all_to_all.132 = f32[16,1,1024]{2,1,0:T(1,128)S(1)} all-to-all(f32[16,1,1024]{2,1,0:T(1,128)S(1)} %reshape.248), channel_id=1, replica_groups=mesh['py'=64,'pz'=16] {'pz'}, dimensions={0} | all-to-all | bytes 131072 | tf_op jit(solution)/shard_map/all_to_all | solution.py:217
  343.2 14.9 %all_to_all.133 = f32[64,1,256]{2,1,0:T(1,128)S(1)} all-to-all(f32[64,1,256]{2,1,0:T(1,128)S(1)} %reshape.250), channel_id=1, replica_groups=mesh['py'=64,'pz'=16] {'py'}, dimensions={0} | all-to-all | bytes 131072 | tf_op jit(solution)/shard_map/all_to_all | solution.py:219
  360.6 5.2 multiply_reduce_fusion
  365.8 110.2 %psum.30 = f32[]{:T(128)} all-reduce(f32[]{:T(128)} %get-tuple-element.48), channel_id=1, replica_groups=mesh['py'=64,'pz'=16] {'py','pz'}, use_global_device_ids=true, to_apply=%region_5.6 | all-reduce | flops 1 | bytes 8 | tf_op jit(solution)/shard_map/psum | solution.py:163
  493.5 113.9 %psum.31 = f32[]{:T(128)} all-reduce(f32[]{:T(128)} %fusion.115), channel_id=1, replica_groups=mesh['py'=64,'pz'=16] {'py','pz'}, use_global_device_ids=true, to_apply=%region_7.8 | all-reduce | flops 1 | bytes 8 | tf_op jit(solution)/shard_map/psum | solution.py:167
  614.8 5.6 collective-permute-start.18
  (173 shorter events, 99.0 us)
Async XLA Ops:
  1.7 7.9 %collective-permute-start.1 = (f32[4,3,8,512]{3,2,1,0:T(8,128)S(1)}, f32[4,3,8,512]{3,2,1,0:T(8,128)S(1)}, u32[]{:S(2)}, u32[]{:S(2)}) collective-permute-start(f32[4,3,8,512]{3,2,1,0:T(8,128)S(1)} %get-tuple-element.15), channel_id=1, source_target_pairs={{0,16},{16,32},{32,48},{48,64},{64,80},{80,96},{96,112},{112,128},... | collective-permute-start | bytes 589832 | tf_op jit(solution)/shard_map/ppermute | solution.py:30
  5.9 6.4 %collective-permute-start = (f32[4,3,8,512]{3,2,1,0:T(8,128)S(1)}, f32[4,3,8,512]{3,2,1,0:T(8,128)S(1)}, u32[]{:S(2)}, u32[]{:S(2)}) collective-permute-start(f32[4,3,8,512]{3,2,1,0:T(8,128)S(1)} %get-tuple-element.16), channel_id=1, source_target_pairs={{16,0},{32,16},{48,32},{64,48},{80,64},{96,80},{112,96},{128,112},... | collective-permute-start | bytes 589832 | tf_op jit(solution)/shard_map/ppermute | solution.py:32
  12.5 16.3 %collective-permute-start.2 = (f32[4,10,3,512]{3,2,1,0:T(4,128)S(1)}, f32[4,10,3,512]{3,2,1,0:T(4,128)S(1)}, u32[]{:S(2)}, u32[]{:S(2)}) collective-permute-start(f32[4,10,3,512]{3,2,1,0:T(4,128)S(1)} %get-tuple-element.11), channel_id=1, source_target_pairs={{1,0},{2,1},{3,2},{4,3},{5,4},{6,5},{7,6},{8,7},{9,8},{10,9},{11,1... | collective-permute-start | bytes 737288 | tf_op jit(solution)/shard_map/ppermute | solution.py:32
  26.8 5.9 collective-permute-start.3
  36.0 2.7 collective-permute-start.5
  37.3 4.7 collective-permute-start.4
  42.0 7.7 %collective-permute-start.6 = (f32[2,6,1,512]{3,2,1,0:T(1,128)S(1)}, f32[2,6,1,512]{3,2,1,0:T(1,128)S(1)}, u32[]{:S(2)}, u32[]{:S(2)}) collective-permute-start(f32[2,6,1,512]{3,2,1,0:T(1,128)S(1)} %get-tuple-element.17), channel_id=1, source_target_pairs={{1,0},{2,1},{3,2},{4,3},{5,4},{6,5},{7,6},{8,7},{9,8},{10,9},{11,1... | collective-permute-start | bytes 73736 | tf_op jit(solution)/shard_map/ppermute | solution.py:32
  44.0 6.6 %collective-permute-start.7 = (f32[2,6,1,512]{3,2,1,0:T(1,128)S(1)}, f32[2,6,1,512]{3,2,1,0:T(1,128)S(1)}, u32[]{:S(2)}, u32[]{:S(2)}) collective-permute-start(f32[2,6,1,512]{3,2,1,0:T(1,128)S(1)} %get-tuple-element.18), channel_id=1, source_target_pairs={{0,1},{1,2},{2,3},{3,4},{4,5},{5,6},{6,7},{7,8},{8,9},{9,10},{10,1... | collective-permute-start | bytes 73736 | tf_op jit(solution)/shard_map/ppermute | solution.py:30
  57.7 27.7 %all-to-all-start = ((f32[64,1,256]{2,1,0:T(1,128)}), f32[64,1,256]{2,1,0:T(1,128)S(1)}, u32[]{:S(2)}, u32[]{:S(2)}) async-start(f32[64,1,256]{2,1,0:T(1,128)} %reshape.236), calls=%async_computation | async-start | bytes 131072 | tf_op jit(solution)/shard_map/all_to_all | solution.py:207
  90.8 19.6 %all-to-all-start.1 = ((f32[16,1,1024]{2,1,0:T(1,128)}), f32[16,1,1024]{2,1,0:T(1,128)S(1)}, u32[]{:S(2)}, u32[]{:S(2)}) async-start(f32[16,1,1024]{2,1,0:T(1,128)} %reshape.238), calls=%async_computation.1 | async-start | bytes 131072 | tf_op jit(solution)/shard_map/all_to_all | solution.py:209
  113.9 11.2 %all-to-all-start.2 = ((f32[16,1,1024]{2,1,0:T(1,128)}), f32[16,1,1024]{2,1,0:T(1,128)S(1)}, u32[]{:S(2)}, u32[]{:S(2)}) async-start(f32[16,1,1024]{2,1,0:T(1,128)} %reshape.240), calls=%async_computation.2 | async-start | bytes 131072 | tf_op jit(solution)/shard_map/all_to_all | solution.py:217
  128.9 16.1 %all-to-all-start.3 = ((f32[64,1,256]{2,1,0:T(1,128)}), f32[64,1,256]{2,1,0:T(1,128)S(1)}, u32[]{:S(2)}, u32[]{:S(2)}) async-start(f32[64,1,256]{2,1,0:T(1,128)} %reshape.242), calls=%async_computation.3 | async-start | bytes 131072 | tf_op jit(solution)/shard_map/all_to_all | solution.py:219
  152.2 3.8 collective-permute-start.8
  154.5 4.5 collective-permute-start.9
  159.0 6.9 %collective-permute-start.10 = (f32[1,6,1,512]{3,2,1,0:T(1,128)S(1)}, f32[1,6,1,512]{3,2,1,0:T(1,128)S(1)}, u32[]{:S(2)}, u32[]{:S(2)}) collective-permute-start(f32[1,6,1,512]{3,2,1,0:T(1,128)S(1)} %get-tuple-element.33), channel_id=1, source_target_pairs={{0,1},{1,2},{2,3},{3,4},{4,5},{5,6},{6,7},{7,8},{8,9},{9,10},{10,1... | collective-permute-start | bytes 36872 | tf_op jit(solution)/shard_map/ppermute | solution.py:30
  163.8 5.0 collective-permute-start.11
  477.3 3.7 collective-permute-start.12
  479.6 4.5 collective-permute-start.13
  484.1 5.8 collective-permute-start.14
  487.8 5.0 collective-permute-start.15
  608.7 2.9 collective-permute-start.16
  610.3 4.5 collective-permute-start.17
  614.8 7.6 %collective-permute-start.18 = (f32[1,6,1,512]{3,2,1,0:T(1,128)S(1)}, f32[1,6,1,512]{3,2,1,0:T(1,128)S(1)}, u32[]{:S(2)}, u32[]{:S(2)}) collective-permute-start(f32[1,6,1,512]{3,2,1,0:T(1,128)S(1)} %get-tuple-element.29), channel_id=1, source_target_pairs={{0,1},{1,2},{2,3},{3,4},{4,5},{5,6},{6,7},{7,8},{8,9},{9,10},{10,1... | collective-permute-start | bytes 36872 | tf_op jit(solution)/shard_map/ppermute | solution.py:30
  620.4 5.0 collective-permute-start.19
  (7 other events, 36.9 us)
where the time goes:
time: 637 us; the launch traced here: 628 us
  blocking collectives  395 us (62%)
  starting transfers between devices  98.6 us (15%)
  waiting for transfers between devices  65.6 us (10%)
  matrix products  26.8 us (4%)
  local copies, waits for them, and re-layouts  21 us (3%)
  other arithmetic  15.3 us (2%)
    psum x2, blocking collectives, residual_inner(): return lax.psum(jnp.sum(left_field * right_field), ('py', 'pz'))  224 us
    psum x1, blocking collectives, curvature_inner(): return lax.psum(jnp.sum(left_field * right_field), ('py', 'pz'))  114 us
    ppermute x10, starting transfers between devices, with_halo(): lax.ppermute(tail, axis, [(i, (i + 1) % count) for i in range(ends)])  33.3 us
    ppermute x10, starting transfers between devices, with_halo(): lax.ppermute(head, axis, [((i + 1) % count, i) for i in range(ends)])  28.5 us
    ppermute x10, waiting for transfers between devices, with_halo(): lax.ppermute(head, axis, [((i + 1) % count, i) for i in range(ends)])  24 us
    all_to_all x1, blocking collectives, precondition(): lax.all_to_all(spectral, 'py', split_axis=2, concat_axis=0, tiled=True)  17 us
    all_to_all x1, starting transfers between devices, precondition(): lax.all_to_all(spectral, 'py', split_axis=2, concat_axis=0, tiled=True)  16.6 us
    all_to_all x1, blocking collectives, precondition(): lax.all_to_all(spectral, 'pz', split_axis=0, concat_axis=1, tiled=True)  14.9 us
  transfers between devices with their start and end apart: 24, of which 14 were waited for; matrix products, arithmetic and copies ran while one was open for 0% of the time, Pallas kernels for 0%

commit v1 on v0

v1 whole, which is shorter than its diff:
```python
import math

import jax
import jax.numpy as jnp
import numpy as np
from jax import lax
from jax.sharding import PartitionSpec as P

NX = 512
ITERS = 2


time_step = 0.05
heavy_density = 8.0
light_viscosity = 0.3
heavy_viscosity = 0.6
compressibility = 0.001
mean_inverse = 0.5
weno_epsilon = 1e-06
highest = lax.Precision.HIGHEST


def weno_blend(slope_one, slope_two, slope_three, slope_four, slope_five):
    smooth_one = (
        13.0 / 12.0 * (slope_one - 2.0 * slope_two + slope_three) ** 2
        + 0.25 * (slope_one - 4.0 * slope_two + 3.0 * slope_three) ** 2
    )
    smooth_two = (
        13.0 / 12.0 * (slope_two - 2.0 * slope_three + slope_four) ** 2
        + 0.25 * (slope_two - slope_four) ** 2
    )
    smooth_three = (
        13.0 / 12.0 * (slope_three - 2.0 * slope_four + slope_five) ** 2
        + 0.25 * (3.0 * slope_three - 4.0 * slope_four + slope_five) ** 2
    )
    alpha_one = 0.1 / (weno_epsilon + smooth_one) ** 2
    alpha_two = 0.6 / (weno_epsilon + smooth_two) ** 2
    alpha_three = 0.3 / (weno_epsilon + smooth_three) ** 2
    weight_sum = alpha_one + alpha_two + alpha_three
    blended = alpha_one * (slope_one / 3.0 - 7.0 * slope_two / 6.0 + 11.0 * slope_three / 6.0)
    blended = blended + alpha_two * (-slope_two / 6.0 + 5.0 * slope_three / 6.0 + slope_four / 3.0)
    blended = blended + alpha_three * (
        slope_three / 3.0 + 5.0 * slope_four / 6.0 - slope_five / 6.0
    )
    return blended / weight_sum


def upwind_derivative(padded, direction_axis, advecting):
    length = padded.shape[direction_axis] - 6
    differences = jnp.diff(padded, axis=direction_axis)

    def window(offset):
        return lax.slice_in_dim(differences, offset, offset + length, axis=direction_axis)

    lower_side = weno_blend(window(0), window(1), window(2), window(3), window(4))
    upper_side = weno_blend(window(5), window(4), window(3), window(2), window(1))
    return jnp.where(advecting > 0, lower_side, upper_side)


def predicted(center, along_x, along_y, along_z, fraction):
    slope_x = upwind_derivative(along_x, 3, center[0][None])
    slope_y = upwind_derivative(along_y, 1, center[1][None])
    slope_z = upwind_derivative(along_z, 2, center[2][None])
    transport = center[0] * slope_x + center[1] * slope_y + center[2] * slope_z
    spread = along_x[..., 4:-2] + along_x[..., 2:-4] - 2.0 * center
    spread = spread + (along_y[:, 4:-2] + along_y[:, 2:-4] - 2.0 * center)
    spread = spread + (along_z[:, :, 4:-2] + along_z[:, :, 2:-4] - 2.0 * center)
    density = 1.0 + (heavy_density - 1.0) * fraction
    kinematic = (light_viscosity + (heavy_viscosity - light_viscosity) * fraction) / density
    return center + time_step * (kinematic * spread - transport)


def wall_ghosts(velocity, wall_flags):
    tangential = 2.0 * wall_flags.astype(jnp.float32) - 1.0
    normal = -jnp.ones_like(tangential)
    mirror_signs = jnp.stack([normal, tangential, tangential])
    lower_ghost = velocity[..., :3][..., ::-1] * mirror_signs[:, 0, :, :, None]
    upper_ghost = velocity[..., -3:][..., ::-1] * mirror_signs[:, 1, :, :, None]
    return jnp.concatenate([lower_ghost, velocity, upper_ghost], axis=-1)


def shifted_pair(head, tail, axis):
    count = lax.axis_size(axis)
    up = [(i, i + 1) for i in range(count - 1)]
    down = [(i + 1, i) for i in range(count - 1)]
    return lax.ppermute(tail, axis, up), lax.ppermute(head, axis, down)


def cosine_table(length):
    wave_index = np.arange(length)[:, None]
    position = np.arange(length)[None, :]
    angle = np.pi / (2 * length) * (wave_index * (2 * position + 1) % (4 * length))
    weight = np.where(wave_index == 0, np.sqrt(1.0 / length), np.sqrt(2.0 / length))
    return weight * np.cos(angle)


def central_table(length):
    return 0.5 * (np.eye(length, k=1) - np.eye(length, k=-1))


def with_rims(table, blocks):
    length = table.shape[0]
    inverse = np.concatenate([np.zeros((1, length)), table.T, np.zeros((1, length))])
    size = length // blocks
    return np.concatenate([inverse[i * size : i * size + size + 2] for i in range(blocks)])


def eigenvalue(wave_index, length):
    return 2.0 - 2.0 * jnp.cos(math.pi / length * wave_index.astype(jnp.float32))


def face_weights(density, y_low, y_high, z_low, z_high, edges):
    inner_x = 2.0 / (density[:, :, 1:] + density[:, :, :-1])
    plus_x = jnp.concatenate([inner_x, jnp.zeros_like(density[:, :, :1])], axis=2)
    along_y = jnp.concatenate([y_low, density, y_high], axis=0)
    along_z = jnp.concatenate([z_low, density, z_high], axis=1)
    first_y, last_y, first_z, last_z = edges
    beta_y = 2.0 / (along_y[1:] + along_y[:-1])
    beta_z = 2.0 / (along_z[:, 1:] + along_z[:, :-1])
    rows, cols = density.shape[:2]
    face_y = jnp.arange(rows + 1, dtype=jnp.int32)[:, None, None]
    face_z = jnp.arange(cols + 1, dtype=jnp.int32)[None, :, None]
    wall_y = (first_y & (face_y == 0)) | (last_y & (face_y == rows))
    wall_z = (first_z & (face_z == 0)) | (last_z & (face_z == cols))
    return plus_x, jnp.where(wall_y, 0.0, beta_y), jnp.where(wall_z, 0.0, beta_z)


def face_fluxes(rimmed, weights):
    plus_x, beta_y, beta_z = weights
    values = rimmed[1:-1, 1:-1]
    forward_x = plus_x * (jnp.roll(values, -1, axis=2) - values)
    backward_x = jnp.roll(forward_x, 1, axis=2)
    flux_y = beta_y * (rimmed[1:, 1:-1] - rimmed[:-1, 1:-1])
    flux_z = beta_z * (rimmed[1:-1, 1:] - rimmed[1:-1, :-1])
    return forward_x, backward_x, flux_y[1:], flux_y[:-1], flux_z[:, 1:], flux_z[:, :-1]


def apply_operator(rimmed, weights):
    forward_x, backward_x, forward_y, backward_y, forward_z, backward_z = face_fluxes(
        rimmed, weights
    )
    return compressibility * rimmed[1:-1, 1:-1] - (
        forward_x - backward_x + (forward_y - backward_y) + (forward_z - backward_z)
    )


def exchange(message, axis):
    return lax.all_to_all(message, axis, split_axis=0, concat_axis=0, tiled=True)


def packed(rows, extras, width):
    count = rows.shape[0]
    tail = jnp.broadcast_to(jnp.stack(extras)[None], (count, len(extras))) if extras else rows[:, :0]
    fill = jnp.zeros((count, width - rows.shape[1] - len(extras)), rows.dtype)
    return jnp.concatenate([rows, tail, fill], axis=1).reshape(count, width // 128, 128)


def summed(partials):
    row = jnp.concatenate([jnp.stack(partials), jnp.zeros((128 - len(partials),), jnp.float32)])
    for axis in ("py", "pz"):
        count = lax.axis_size(axis)
        parts = exchange(jnp.broadcast_to(row[None, None], (count, 1, 128)), axis)
        row = jnp.sum(parts[:, 0], axis=0)
    return [row[i] for i in range(len(partials))]


def dot(left, right):
    return jnp.dot(left, right, precision=highest)


def on_device(velocity, fraction, wall_flags):
    rows, cols = (fraction.shape[0], fraction.shape[1])
    rows_devices = lax.axis_size("py")
    cols_devices = lax.axis_size("pz")
    total_rows = rows * rows_devices
    total_cols = cols * cols_devices
    row_index = lax.axis_index("py")
    col_index = lax.axis_index("pz")
    edges = (row_index == 0, row_index == rows_devices - 1, col_index == 0, col_index == cols_devices - 1)

    def y_layers(part, width):
        return part.reshape(3 * width, cols, NX)

    y_head = jnp.concatenate([y_layers(velocity[:, :3], 3), fraction[:1]], axis=0)
    y_tail = jnp.concatenate([y_layers(velocity[:, -3:], 3), fraction[-1:]], axis=0)
    y_low, y_high = shifted_pair(y_head, y_tail, "py")

    def z_layers(first, only):
        lanes = jnp.transpose(velocity[:, :, first : first + 3], (0, 2, 1, 3)).reshape(9, rows, NX)
        return jnp.concatenate([lanes, fraction[:, only][None]], axis=0)

    z_low, z_high = shifted_pair(z_layers(0, 0), z_layers(cols - 3, cols - 1), "pz")

    def unlayered(z_rim):
        return jnp.transpose(z_rim[:9].reshape(3, 3, rows, NX), (0, 2, 1, 3))

    provisional = predicted(
        velocity,
        wall_ghosts(velocity, wall_flags),
        jnp.concatenate([y_low[:9].reshape(3, 3, cols, NX), velocity, y_high[:9].reshape(3, 3, cols, NX)], axis=1),
        jnp.concatenate([unlayered(z_low), velocity, unlayered(z_high)], axis=2),
        fraction,
    )

    def density_of(part):
        return 1.0 + (heavy_density - 1.0) * part

    weights = face_weights(
        density_of(fraction),
        density_of(y_low[9:]),
        density_of(y_high[9:]),
        density_of(z_low[9][:, None]),
        density_of(z_high[9][:, None]),
        edges,
    )
    normal_x = provisional[0]
    forward_x = jnp.concatenate([normal_x[:, :, 1:], -normal_x[:, :, -1:]], axis=2)
    backward_x = jnp.concatenate([-normal_x[:, :, :1], normal_x[:, :, :-1]], axis=2)
    source_x = -0.5 * (forward_x - backward_x)

    plain_x = cosine_table(NX)
    plain_y = cosine_table(total_rows)
    plain_z = cosine_table(total_cols)

    def constant(table):
        return jnp.asarray(table, dtype=jnp.float32)

    table_x = constant(plain_x)
    table_y = constant(plain_y)
    table_z = constant(plain_z)
    source_y = constant(np.concatenate([plain_y, -plain_y @ central_table(total_rows)], axis=1))
    source_z = constant(np.concatenate([plain_z, -plain_z @ central_table(total_cols)], axis=1))
    back_y = constant(with_rims(plain_y, rows_devices))
    back_z = constant(with_rims(plain_z, cols_devices))

    part_x = NX // rows_devices
    part_y = total_rows // cols_devices
    wave_y = col_index * part_y + jnp.arange(part_y, dtype=jnp.int32)
    wave_z = jnp.arange(total_cols, dtype=jnp.int32)
    wave_x = row_index * part_x + jnp.arange(part_x, dtype=jnp.int32)
    modes = (eigenvalue(wave_y, total_rows)[:, None] + eigenvalue(wave_x, NX)[None, :]).reshape(1, -1)
    denominator = compressibility + mean_inverse * (modes + eigenvalue(wave_z, total_cols)[:, None])
    block = rows * cols * part_x

    def along_x(fields):
        count = fields.shape[0]
        spectral = lax.dot_general(
            table_x, fields.reshape(-1, NX), (((1,), (1,)), ((), ())), precision=highest
        )
        return spectral.reshape(rows_devices, -1), count

    def to_rows(message, count):
        cells = message.reshape(rows_devices, part_x, count, rows, cols)
        return jnp.transpose(cells, (2, 0, 3, 1, 4)).reshape(count, total_rows, part_x * cols)

    def to_cols(message, count):
        cells = message.reshape(cols_devices, count, part_y, part_x, cols)
        return jnp.transpose(cells, (1, 0, 4, 2, 3)).reshape(count * total_cols, part_y * part_x)

    def back(spectral):
        wide = dot(back_z, spectral).reshape(cols_devices, -1)
        wide = exchange(packed(wide, [], wide.shape[1]), "pz").reshape(
            cols_devices, cols + 2, part_y, part_x
        )
        wide = jnp.transpose(wide, (0, 2, 1, 3)).reshape(total_rows, -1)
        wide = dot(back_y, wide).reshape(rows_devices, -1)
        size = wide.shape[1]
        wide = exchange(packed(wide, [], 512), "py").reshape(rows_devices, 512)[:, :size]
        wide = wide.reshape(rows_devices, (rows + 2) * (cols + 2), part_x)
        wide = jnp.transpose(wide, (1, 0, 2)).reshape((rows + 2) * (cols + 2), NX)
        return dot(wide, table_x).reshape(rows + 2, cols + 2, NX)

    fields = jnp.stack([source_x, provisional[1], provisional[2]])
    message, count = along_x(fields)
    message = exchange(packed(message, [], 1024), "py").reshape(rows_devices, -1)[:, : count * block]
    cells = to_rows(message, count)
    joined = dot(source_y, cells[:2].reshape(2 * total_rows, -1))
    third = dot(table_y, cells[2])
    message = jnp.stack(
        [joined.reshape(cols_devices, -1), third.reshape(cols_devices, -1)], axis=1
    ).reshape(cols_devices, -1)
    message = exchange(packed(message, [], message.shape[1]), "pz")
    residual = dot(source_z, to_cols(message, 2))
    search = residual / denominator
    aligned = jnp.sum(residual * search)

    first = back(search)
    applied = apply_operator(first, weights)
    curvature = jnp.sum(first[1:-1, 1:-1] * applied)

    message, count = along_x(applied[None])
    message = exchange(packed(message, [aligned, curvature], 512), "py").reshape(rows_devices, 512)
    totals = jnp.sum(message[:, block : block + 2], axis=0)
    image = dot(table_y, to_rows(message[:, :block], 1)[0]).reshape(cols_devices, -1)
    size = image.shape[1]
    message = exchange(packed(image, [totals[0], totals[1]], size + 128), "pz").reshape(cols_devices, -1)
    totals = jnp.sum(message[:, size : size + 2], axis=0)
    aligned, curvature = totals[0], totals[1]
    image = dot(table_z, to_cols(message[:, :size], 1))
    first_step = aligned / curvature
    residual = residual - first_step * image
    search = residual / denominator
    renewed = jnp.sum(residual * search)

    second = back(search)
    core = second[1:-1, 1:-1]
    bent = jnp.sum(core * apply_operator(second, weights))
    crossed = jnp.sum(core * applied)
    renewed, bent, crossed = summed([renewed, bent, crossed])
    ratio = renewed / aligned
    second_step = renewed / (bent + 2.0 * ratio * crossed + ratio * ratio * curvature)
    solution = first_step * first + second_step * (second + ratio * first)
    forward_x, backward_x, forward_y, backward_y, forward_z, backward_z = face_fluxes(
        solution, weights
    )
    correction = jnp.stack(
        [
            0.5 * (forward_x + backward_x),
            0.5 * (forward_y + backward_y),
            0.5 * (forward_z + backward_z),
        ]
    )
    return (provisional - correction, solution[1:-1, 1:-1])


def solution(mesh):
    in_specs = (P(None, "py", "pz", None), P("py", "pz", None), P(None, "py", "pz"))
    out_specs = (P(None, "py", "pz", None), P("py", "pz", None))
    return jax.shard_map(
        on_device, mesh=mesh, in_specs=in_specs, out_specs=out_specs, check_vma=False
    )
```

time: 637 us -> 246 us (0.39); the launches traced: 628 us -> 245 us
  blocking collectives: 395 us -> 83.2 us
  starting transfers between devices: 98.6 us -> 50.4 us
  waiting for transfers between devices: 65.6 us -> 42.3 us
  matrix products: 26.8 us -> 9.93 us
  local copies, waits for them, and re-layouts: 21 us -> 32.2 us
    psum x3 -> x0, blocking collectives: 337 us -> none  [the longest x2 224 us: residual_inner(): return lax.psum(jnp.sum(left_field * right_field), ('py', 'pz'))]
    ppermute x20 -> x4, starting transfers between devices: 61.8 us -> 19.9 us  [shifted_pair(): return (lax.ppermute(tail, axis, up), lax.ppermute(head, axis, down))]
    all_to_all x4 -> x6, blocking collectives: 57.1 us -> 83.2 us  [exchange(): lax.all_to_all(message, axis, split_axis=0, concat_axis=0, tiled=True)]
    ppermute x20 -> x4, waiting for transfers between devices: 28.8 us -> 5.09 us  [shifted_pair(): return (lax.ppermute(tail, axis, up), lax.ppermute(head, axis, down))]
    dot_general x12 -> x13, matrix products: 26.8 us -> 9.93 us  [the longest x11 8 us: dot(): return jnp.dot(left, right, precision=highest)]
    unnamed x30 -> x75, local copies, waits for them, and re-layouts: 12.6 us -> 2.21 us
    transpose x2 -> x12, local copies, waits for them, and re-layouts: 0.49 us -> 9.78 us  [the longest x4 4.57 us: back(): wide = jnp.transpose(wide, (1, 0, 2)).reshape((rows + 2) * (cols + 2), NX)]
  transfers between devices with their start and end apart: 24 -> 8, of which waited for: 14 -> 6; matrix products, arithmetic and copies ran while one was open for 0% -> 4% of each run, Pallas kernels for 0% -> 0%
where the time goes in v1:
time: 246 us; the launch traced here: 245 us
  blocking collectives  83.2 us (34%)
  starting transfers between devices  50.4 us (20%)
  waiting for transfers between devices  42.3 us (17%)
  local copies, waits for them, and re-layouts  32.2 us (13%)
  other arithmetic  19.4 us (8%)
  matrix products  9.93 us (4%)
  between operations  6.99 us (3%)
    all_to_all x6, blocking collectives, exchange(): lax.all_to_all(message, axis, split_axis=0, concat_axis=0, tiled=True)  83.2 us
    all_to_all x4, waiting for transfers between devices, exchange(): lax.all_to_all(message, axis, split_axis=0, concat_axis=0, tiled=True)  37.2 us
    all_to_all x4, starting transfers between devices, exchange(): lax.all_to_all(message, axis, split_axis=0, concat_axis=0, tiled=True)  30.5 us
    ppermute x4, starting transfers between devices, shifted_pair(): return (lax.ppermute(tail, axis, up), lax.ppermute(head, axis, down))  19.9 us
    dot_general x11, matrix products, dot(): return jnp.dot(left, right, precision=highest)  8 us
    ppermute x4, waiting for transfers between devices, shifted_pair(): return (lax.ppermute(tail, axis, up), lax.ppermute(head, axis, down))  5.09 us
    add x4, other arithmetic, density_of(): return 1.0 + (heavy_density - 1.0) * part  4.94 us
  transfers between devices with their start and end apart: 8, of which 6 were waited for; matrix products, arithmetic and copies ran while one was open for 4% of the time, Pallas kernels for 0%

profile of v1, /device:TPU:1, one launch (start us, length us, event | category | flops | bytes accessed | tf_op | source)
XLA Modules:
  0.0 244.5 jit_solution(6437423391129510817)
XLA Ops:
  2.8 4.5 %collective-permute-start.3 = (f32[10,4,512]{2,0,1:T(8,128)S(1)}, f32[10,4,512]{2,0,1:T(8,128)S(1)}, u32[]{:S(2)}, u32[]{:S(2)}) collective-permute-start(f32[10,4,512]{2,0,1:T(8,128)S(1)} %pad_maximum_fusion.13), channel_id=1, source_target_pairs={{0,1},{1,2},{2,3},{3,4},{4,5},{5,6},{6,7},{7,8},{8,9},{9,10},{10,1... | collective-permute-start | bytes 245768 | tf_op jit(solution)/shard_map/ppermute | solution.py:86
  7.4 12.8 %collective-permute-start.2 = (f32[10,4,512]{2,0,1:T(8,128)S(1)}, f32[10,4,512]{2,0,1:T(8,128)S(1)}, u32[]{:S(2)}, u32[]{:S(2)}) collective-permute-start(f32[10,4,512]{2,0,1:T(8,128)S(1)} %pad_maximum_fusion.12), channel_id=1, source_target_pairs={{1,0},{2,1},{3,2},{4,3},{5,4},{6,5},{7,6},{8,7},{9,8},{10,9},{11,1... | collective-permute-start | bytes 245768 | tf_op jit(solution)/shard_map/ppermute | solution.py:86
  26.9 4.2 %collective-permute-done = f32[10,8,512]{2,1,0:T(8,128)S(1)} collective-permute-done((f32[10,8,512]{2,1,0:T(8,128)S(1)}, f32[10,8,512]{2,1,0:T(8,128)S(1)}, u32[]{:S(2)}, u32[]{:S(2)}) %collective-permute-start) | collective-permute-done | bytes 163872 | tf_op jit(solution)/shard_map/ppermute | solution.py:86
  31.3 3.1 %fusion.8 = f32[3,4,8,512]{3,2,1,0:T(8,128)S(1)} fusion(f32[3,4,8,512]{3,2,1,0:T(8,128)S(1)} %copy-done, f32[3,4,3,512]{3,2,1,0:T(4,128)S(1)} %bitcast.179, f32[3,4,3,512]{3,2,1,0:T(4,128)S(1)} %bitcast.181, f32[3,3,8,512]{3,2,1,0:T(8,128)S(1)} %bitcast.173, f32[3,3,8,512]{3,2,1,0:T(8,128)S(1)} %bitcast.175, f32[3,4,8,3]{3,2,1,0:T(8,128)S(1)} %get-tuple-element.41, ...), kind=kLoop, calls=%fused_computation.19 | loop fusion | flops 19611648 | bytes 4688128 | tf_op jit(solution)/shard_map/add | solution.py:70
  36.6 13.2 %all-to-all-start = ((f32[64,8,128]{2,1,0:T(8,128)}), f32[64,8,128]{2,1,0:T(8,128)S(1)}, u32[]{:S(2)}, u32[]{:S(2)}) async-start(f32[64,8,128]{2,1,0:T(8,128)} %bitcast.79), calls=%async_computation | async-start | bytes 524288 | tf_op jit(solution)/shard_map/all_to_all | solution.py:148
  50.6 13.3 %all-to-all-done = f32[64,8,128]{2,1,0:T(8,128)S(1)} async-done(((f32[64,8,128]{2,1,0:T(8,128)}), f32[64,8,128]{2,1,0:T(8,128)S(1)}, u32[]{:S(2)}, u32[]{:S(2)}) %all-to-all-start) | async-done | bytes 262176 | tf_op jit(solution)/shard_map/all_to_all | solution.py:148
  65.9 1.8 copy.135
  69.8 9.3 %all-to-all-start.1 = ((f32[16,16,128]{2,1,0:T(8,128)}), f32[16,16,128]{2,1,0:T(8,128)S(1)}, u32[]{:S(2)}, u32[]{:S(2)}) async-start(f32[16,16,128]{2,1,0:T(8,128)} %reshape_reshape.9), calls=%async_computation.1 | async-start | bytes 262144 | tf_op jit(solution)/shard_map/all_to_all | solution.py:148
  81.8 6.2 %all-to-all-done.1 = f32[16,16,128]{2,1,0:T(8,128)S(1)} async-done(((f32[16,16,128]{2,1,0:T(8,128)}), f32[16,16,128]{2,1,0:T(8,128)S(1)}, u32[]{:S(2)}, u32[]{:S(2)}) %all-to-all-start.1) | async-done | bytes 131104 | tf_op jit(solution)/shard_map/all_to_all | solution.py:148
  88.3 1.8 copy.141
  93.6 3.4 %all-to-all-start.2 = ((f32[16,10,128]{2,1,0:T(8,128)}), f32[16,10,128]{2,1,0:T(8,128)S(1)}, u32[]{:S(2)}, u32[]{:S(2)}) async-start(f32[16,10,128]{2,1,0:T(8,128)} %reshape_reshape.10), calls=%async_computation.2 | async-start | bytes 262144 | tf_op jit(solution)/shard_map/all_to_all | solution.py:148
  98.5 7.5 %all-to-all-done.2 = f32[16,10,128]{2,1,0:T(8,128)S(1)} async-done(((f32[16,10,128]{2,1,0:T(8,128)}), f32[16,10,128]{2,1,0:T(8,128)S(1)}, u32[]{:S(2)}, u32[]{:S(2)}) %all-to-all-start.2) | async-done | bytes 81952 | tf_op jit(solution)/shard_map/all_to_all | solution.py:148
  108.1 4.6 %all-to-all-start.3 = ((f32[64,4,128]{2,1,0:T(4,128)}), f32[64,4,128]{2,1,0:T(4,128)S(1)}, u32[]{:S(2)}, u32[]{:S(2)}) async-start(f32[64,4,128]{2,1,0:T(4,128)} %reshape.327), calls=%async_computation.3 | async-start | bytes 262144 | tf_op jit(solution)/shard_map/all_to_all | solution.py:148
  114.7 10.3 %all-to-all-done.3 = f32[64,4,128]{2,1,0:T(4,128)S(1)} async-done(((f32[64,4,128]{2,1,0:T(4,128)}), f32[64,4,128]{2,1,0:T(4,128)S(1)}, u32[]{:S(2)}, u32[]{:S(2)}) %all-to-all-start.3) | async-done | bytes 131104 | tf_op jit(solution)/shard_map/all_to_all | solution.py:148
  127.5 1.8 dot_general.75
  129.3 1.8 fusion.80
  136.0 15.4 %all_to_all.50 = f32[64,4,128]{2,1,0:T(4,128)S(1)} all-to-all(f32[64,4,128]{2,1,0:T(4,128)S(1)} %reshape.331), channel_id=1, replica_groups=mesh['py'=64,'pz'=16] {'py'}, dimensions={0} | all-to-all | bytes 262144 | tf_op jit(solution)/shard_map/all_to_all | solution.py:148
  153.6 14.0 %all_to_all.51 = f32[16,9,128]{2,1,0:T(8,128)S(1)} all-to-all(f32[16,9,128]{2,1,0:T(8,128)S(1)} %reshape.335), channel_id=1, replica_groups=mesh['py'=64,'pz'=16] {'pz'}, dimensions={0} | all-to-all | bytes 147456 | tf_op jit(solution)/shard_map/all_to_all | solution.py:148
  172.5 11.3 %all_to_all.52 = f32[16,10,128]{2,1,0:T(8,128)S(1)} all-to-all(f32[16,10,128]{2,1,0:T(8,128)S(1)} %reshape_reshape.11), channel_id=1, replica_groups=mesh['py'=64,'pz'=16] {'pz'}, dimensions={0} | all-to-all | bytes 163840 | tf_op jit(solution)/shard_map/all_to_all | solution.py:148
  185.2 15.9 %all_to_all.53 = f32[64,4,128]{2,1,0:T(4,128)S(1)} all-to-all(f32[64,4,128]{2,1,0:T(4,128)S(1)} %reshape.342), channel_id=1, replica_groups=mesh['py'=64,'pz'=16] {'py'}, dimensions={0} | all-to-all | bytes 262144 | tf_op jit(solution)/shard_map/all_to_all | solution.py:148
  203.5 1.8 dot_general.86
  209.6 1.9 pad_maximum_fusion.17
  211.5 14.8 %all_to_all.54 = f32[64,1,128]{2,1,0:T(1,128)S(1)} all-to-all(f32[64,1,128]{2,1,0:T(1,128)S(1)} %broadcast_in_dim.104), channel_id=1, replica_groups=mesh['py'=64,'pz'=16] {'py'}, dimensions={0} | all-to-all | bytes 65536 | tf_op jit(solution)/shard_map/all_to_all | solution.py:148
  226.3 11.9 %all_to_all.55 = f32[16,1,128]{2,1,0:T(1,128)S(1)} all-to-all(f32[16,1,128]{2,1,0:T(1,128)S(1)} %broadcast_in_dim.105), channel_id=1, replica_groups=mesh['py'=64,'pz'=16] {'pz'}, dimensions={0} | all-to-all | bytes 16384 | tf_op jit(solution)/shard_map/all_to_all | solution.py:148
  (233 shorter events, 51.2 us)
Async XLA Ops:
  0.6 24.2 %copy-start.12 = (f32[4,8,512]{2,1,0:T(8,128)S(1)}, f32[4,8,512]{2,1,0:T(8,128)}, u32[]{:S(2)}) copy-start(f32[4,8,512]{2,1,0:T(8,128)} %param.11) | copy-start | bytes 196612
  0.6 24.1 %copy-start = (f32[3,4,8,512]{3,2,1,0:T(8,128)S(1)}, f32[3,4,8,512]{3,2,1,0:T(8,128)}, u32[]{:S(2)}) copy-start(f32[3,4,8,512]{3,2,1,0:T(8,128)} %param.10) | copy-start | bytes 589828
  0.7 24.3 %copy-start.28 = (s32[2,4,8]{2,1,0:T(4,128)S(1)}, s32[2,4,8]{2,1,0:T(4,128)}, u32[]{:S(2)}) copy-start(s32[2,4,8]{2,1,0:T(4,128)} %param.12) | copy-start | bytes 772
  2.8 22.9 %collective-permute-start.3 = (f32[10,4,512]{2,0,1:T(8,128)S(1)}, f32[10,4,512]{2,0,1:T(8,128)S(1)}, u32[]{:S(2)}, u32[]{:S(2)}) collective-permute-start(f32[10,4,512]{2,0,1:T(8,128)S(1)} %pad_maximum_fusion.13), channel_id=1, source_target_pairs={{0,1},{1,2},{2,3},{3,4},{4,5},{5,6},{6,7},{7,8},{8,9},{9,10},{10,1... | collective-permute-start | bytes 245768 | tf_op jit(solution)/shard_map/ppermute | solution.py:86
  7.4 18.4 %collective-permute-start.2 = (f32[10,4,512]{2,0,1:T(8,128)S(1)}, f32[10,4,512]{2,0,1:T(8,128)S(1)}, u32[]{:S(2)}, u32[]{:S(2)}) collective-permute-start(f32[10,4,512]{2,0,1:T(8,128)S(1)} %pad_maximum_fusion.12), channel_id=1, source_target_pairs={{1,0},{2,1},{3,2},{4,3},{5,4},{6,5},{7,6},{8,7},{9,8},{10,9},{11,1... | collective-permute-start | bytes 245768 | tf_op jit(solution)/shard_map/ppermute | solution.py:86
  22.0 4.9 %collective-permute-start.1 = (f32[10,8,512]{2,1,0:T(8,128)S(1)}, f32[10,8,512]{2,1,0:T(8,128)S(1)}, u32[]{:S(2)}, u32[]{:S(2)}) collective-permute-start(f32[10,8,512]{2,1,0:T(8,128)S(1)} %pad_maximum_fusion.11), channel_id=1, source_target_pairs={{0,16},{16,32},{32,48},{48,64},{64,80},{80,96},{96,112},{112,128},... | collective-permute-start | bytes 491528 | tf_op jit(solution)/shard_map/ppermute | solution.py:86
  23.3 7.8 %collective-permute-start = (f32[10,8,512]{2,1,0:T(8,128)S(1)}, f32[10,8,512]{2,1,0:T(8,128)S(1)}, u32[]{:S(2)}, u32[]{:S(2)}) collective-permute-start(f32[10,8,512]{2,1,0:T(8,128)S(1)} %pad_maximum_fusion.10), channel_id=1, source_target_pairs={{16,0},{32,16},{48,32},{64,48},{80,64},{96,80},{112,96},{128,112},... | collective-permute-start | bytes 491528 | tf_op jit(solution)/shard_map/ppermute | solution.py:86
  24.7 67.4 %copy-start.31 = (f32[128]{0:T(128)}, f32[128]{0:T(128)S(1)}, u32[]{:S(2)}) copy-start(f32[128]{0:T(128)S(1)} %multiply_subtract_fusion.1) | copy-start | bytes 1540
  36.6 27.2 %all-to-all-start = ((f32[64,8,128]{2,1,0:T(8,128)}), f32[64,8,128]{2,1,0:T(8,128)S(1)}, u32[]{:S(2)}, u32[]{:S(2)}) async-start(f32[64,8,128]{2,1,0:T(8,128)} %bitcast.79), calls=%async_computation | async-start | bytes 524288 | tf_op jit(solution)/shard_map/all_to_all | solution.py:148
  69.8 18.2 %all-to-all-start.1 = ((f32[16,16,128]{2,1,0:T(8,128)}), f32[16,16,128]{2,1,0:T(8,128)S(1)}, u32[]{:S(2)}, u32[]{:S(2)}) async-start(f32[16,16,128]{2,1,0:T(8,128)} %reshape_reshape.9), calls=%async_computation.1 | async-start | bytes 262144 | tf_op jit(solution)/shard_map/all_to_all | solution.py:148
  91.2 15.6 %copy-start.4 = (f32[384,256]{1,0:T(8,128)S(1)}, f32[384,256]{1,0:T(8,128)}, u32[]{:S(2)}) copy-start(f32[384,256]{1,0:T(8,128)} %constant.176.clone) | copy-start | bytes 1179652
  93.6 12.3 %all-to-all-start.2 = ((f32[16,10,128]{2,1,0:T(8,128)}), f32[16,10,128]{2,1,0:T(8,128)S(1)}, u32[]{:S(2)}, u32[]{:S(2)}) async-start(f32[16,10,128]{2,1,0:T(8,128)} %reshape_reshape.10), calls=%async_computation.2 | async-start | bytes 262144 | tf_op jit(solution)/shard_map/all_to_all | solution.py:148
  108.1 17.0 %all-to-all-start.3 = ((f32[64,4,128]{2,1,0:T(4,128)}), f32[64,4,128]{2,1,0:T(4,128)S(1)}, u32[]{:S(2)}, u32[]{:S(2)}) async-start(f32[64,4,128]{2,1,0:T(4,128)} %reshape.327), calls=%async_computation.3 | async-start | bytes 262144 | tf_op jit(solution)/shard_map/all_to_all | solution.py:148
  134.5 18.4 %copy-start.7 = (f32[256,256]{1,0:T(8,128)S(1)}, f32[256,256]{1,0:T(8,128)}, u32[]{:S(2)}) copy-start(f32[256,256]{1,0:T(8,128)} %constant.172.clone) | copy-start | bytes 786436
  153.4 17.9 %copy-start.23 = (f32[128,128]{1,0:T(8,128)S(1)}, f32[128,128]{1,0:T(8,128)}, u32[]{:S(2)}) copy-start(f32[128,128]{1,0:T(8,128)} %copy-done.22) | copy-start | bytes 196612
  153.4 17.9 %copy-start.30 = (f32[128]{0:T(128)S(1)}, f32[128]{0:T(128)}, u32[]{:S(2)}) copy-start(f32[128]{0:T(128)} %copy-done.29) | copy-start | bytes 1540
  153.5 17.9 %copy-start.32 = (f32[128]{0:T(128)S(1)}, f32[128]{0:T(128)}, u32[]{:S(2)}) copy-start(f32[128]{0:T(128)} %copy-done.31) | copy-start | bytes 1540
  153.5 17.9 %copy-start.35 = (f32[128,128]{1,0:T(8,128)S(1)}, f32[128,128]{1,0:T(8,128)}, u32[]{:S(2)}) copy-start(f32[128,128]{1,0:T(8,128)} %constant.173.clone) | copy-start | bytes 196612
  153.6 18.6 %copy-start.34 = (f32[160,128]{1,0:T(8,128)S(1)}, f32[160,128]{1,0:T(8,128)}, u32[]{:S(2)}) copy-start(f32[160,128]{1,0:T(8,128)} %constant.177.clone) | copy-start | bytes 245764
  205.3 37.4 %copy-start.11 = (f32[1,8,512]{2,1,0:T(8,128)S(1)}, f32[1,8,512]{2,1,0:T(8,128)}, u32[]{:S(2)}) copy-start(f32[1,8,512]{2,1,0:T(8,128)} %fusion.59) | copy-start | bytes 49156
  205.3 37.4 %copy-start.27 = (pred[5]{0:T(512)(128)(4,1)S(1)}, pred[5]{0:T(512)(128)(4,1)}, u32[]{:S(2)}) copy-start(pred[5]{0:T(512)(128)(4,1)} %and_or_fusion.1) | copy-start | bytes 19
  205.3 37.5 %copy-start.18 = (f32[4,1,512]{2,1,0:T(1,128)S(1)}, f32[4,1,512]{2,1,0:T(1,128)}, u32[]{:S(2)}) copy-start(f32[4,1,512]{2,1,0:T(1,128)} %fusion.63) | copy-start | bytes 24580
  205.3 37.5 %copy-start.20 = (f32[4,1,512]{2,1,0:T(1,128)S(1)}, f32[4,1,512]{2,1,0:T(1,128)}, u32[]{:S(2)}) copy-start(f32[4,1,512]{2,1,0:T(1,128)} %fusion.65) | copy-start | bytes 24580
  205.3 37.5 %copy-start.26 = (pred[9]{0:T(512)(128)(4,1)S(1)}, pred[9]{0:T(512)(128)(4,1)}, u32[]{:S(2)}) copy-start(pred[9]{0:T(512)(128)(4,1)} %and_or_fusion) | copy-start | bytes 31
  (20 other events, 84.9 us)

commit v2 on v1

v2 whole, which is shorter than its diff:
```python
import math

import jax
import jax.numpy as jnp
import numpy as np
from jax import lax
from jax.experimental import pallas as pl
from jax.experimental.pallas import tpu as pltpu
from jax.sharding import PartitionSpec as P

NX = 512
ITERS = 2


time_step = 0.05
heavy_density = 8.0
light_viscosity = 0.3
heavy_viscosity = 0.6
compressibility = 0.001
mean_inverse = 0.5
weno_epsilon = 1e-06
highest = lax.Precision.HIGHEST


def weno_blend(slope_one, slope_two, slope_three, slope_four, slope_five):
    smooth_one = (
        13.0 / 12.0 * (slope_one - 2.0 * slope_two + slope_three) ** 2
        + 0.25 * (slope_one - 4.0 * slope_two + 3.0 * slope_three) ** 2
    )
    smooth_two = (
        13.0 / 12.0 * (slope_two - 2.0 * slope_three + slope_four) ** 2
        + 0.25 * (slope_two - slope_four) ** 2
    )
    smooth_three = (
        13.0 / 12.0 * (slope_three - 2.0 * slope_four + slope_five) ** 2
        + 0.25 * (3.0 * slope_three - 4.0 * slope_four + slope_five) ** 2
    )
    alpha_one = 0.1 / (weno_epsilon + smooth_one) ** 2
    alpha_two = 0.6 / (weno_epsilon + smooth_two) ** 2
    alpha_three = 0.3 / (weno_epsilon + smooth_three) ** 2
    weight_sum = alpha_one + alpha_two + alpha_three
    blended = alpha_one * (slope_one / 3.0 - 7.0 * slope_two / 6.0 + 11.0 * slope_three / 6.0)
    blended = blended + alpha_two * (-slope_two / 6.0 + 5.0 * slope_three / 6.0 + slope_four / 3.0)
    blended = blended + alpha_three * (
        slope_three / 3.0 + 5.0 * slope_four / 6.0 - slope_five / 6.0
    )
    return blended / weight_sum


def upwind_derivative(padded, direction_axis, advecting):
    length = padded.shape[direction_axis] - 6
    differences = jnp.diff(padded, axis=direction_axis)

    def window(offset):
        return lax.slice_in_dim(differences, offset, offset + length, axis=direction_axis)

    lower_side = weno_blend(window(0), window(1), window(2), window(3), window(4))
    upper_side = weno_blend(window(5), window(4), window(3), window(2), window(1))
    return jnp.where(advecting > 0, lower_side, upper_side)


def predicted(center, along_x, along_y, along_z, fraction):
    slope_x = upwind_derivative(along_x, 3, center[0][None])
    slope_y = upwind_derivative(along_y, 1, center[1][None])
    slope_z = upwind_derivative(along_z, 2, center[2][None])
    transport = center[0] * slope_x + center[1] * slope_y + center[2] * slope_z
    spread = along_x[..., 4:-2] + along_x[..., 2:-4] - 2.0 * center
    spread = spread + (along_y[:, 4:-2] + along_y[:, 2:-4] - 2.0 * center)
    spread = spread + (along_z[:, :, 4:-2] + along_z[:, :, 2:-4] - 2.0 * center)
    density = 1.0 + (heavy_density - 1.0) * fraction
    kinematic = (light_viscosity + (heavy_viscosity - light_viscosity) * fraction) / density
    return center + time_step * (kinematic * spread - transport)


def wall_ghosts(velocity, wall_flags):
    tangential = 2.0 * wall_flags.astype(jnp.float32) - 1.0
    normal = -jnp.ones_like(tangential)
    mirror_signs = jnp.stack([normal, tangential, tangential])
    lower_ghost = velocity[..., :3][..., ::-1] * mirror_signs[:, 0, :, :, None]
    upper_ghost = velocity[..., -3:][..., ::-1] * mirror_signs[:, 1, :, :, None]
    return jnp.concatenate([lower_ghost, velocity, upper_ghost], axis=-1)


def shifted_pair(head, tail, axis):
    count = lax.axis_size(axis)
    up = [(i, i + 1) for i in range(count - 1)]
    down = [(i + 1, i) for i in range(count - 1)]
    return lax.ppermute(tail, axis, up), lax.ppermute(head, axis, down)


def cosine_table(length):
    wave_index = np.arange(length)[:, None]
    position = np.arange(length)[None, :]
    angle = np.pi / (2 * length) * (wave_index * (2 * position + 1) % (4 * length))
    weight = np.where(wave_index == 0, np.sqrt(1.0 / length), np.sqrt(2.0 / length))
    return weight * np.cos(angle)


def half_eigenvalue(length):
    return mean_inverse * 4.0 * np.sin(np.pi * np.arange(length) / (2 * length)) ** 2


def exchange(message, axis):
    return lax.all_to_all(message, axis, split_axis=0, concat_axis=0, tiled=True)


def dot(left, right):
    return lax.dot_general(
        left, right, (((1,), (0,)), ((), ())), precision=highest, preferred_element_type=jnp.float32
    )


def dot_nt(left, right):
    return lax.dot_general(
        left, right, (((1,), (1,)), ((), ())), precision=highest, preferred_element_type=jnp.float32
    )


def rolled(values, shift, axis):
    return pltpu.roll(values, shift % values.shape[axis], axis)


def moved(values, step):
    row = lax.broadcasted_iota(jnp.int32, values.shape, 0)
    edge = 0 if step == 1 else values.shape[0] - 1
    return jnp.where(row == edge, 0.0, rolled(values, step, 0))


def picked(values, source):
    lane = lax.broadcasted_iota(jnp.int32, (values.shape[1], source.shape[1]), 0)
    chosen = jnp.where(lane == source, 1.0, 0.0).astype(jnp.bfloat16)
    total = None
    rest = values
    for _ in range(3):
        piece = rest.astype(jnp.bfloat16)
        rest = rest - piece.astype(jnp.float32)
        term = jnp.dot(piece, chosen, preferred_element_type=jnp.float32)
        total = term if total is None else total + term
    return total


def from_tiles(tiles, count):
    return jnp.concatenate([tiles[:, t, :] for t in range(count)], axis=1)


def into_tiles(ref, values):
    for t in range(values.shape[1] // 128):
        ref[:, t, :] = values[:, 128 * t : 128 * t + 128]


def to_message(rows, table_x):
    spectral = dot_nt(table_x, rows)
    devices = spectral.shape[0] // 8
    return jnp.concatenate([spectral[devices * k : devices * k + devices] for k in range(8)], axis=1)


def row_blocks(message, source):
    ordered = picked(message, source)
    return [ordered[:, 64 * y : 64 * y + 64] for y in range(4)]


def to_modes(blocks, table_y):
    return dot(jnp.concatenate(blocks, axis=0).T, table_y)


def moments(rows, rho):
    upward = rows[0:8]
    for z in range(1, 8):
        upward = rho * upward + rows[8 * z : 8 * z + 8]
    downward = rows[56:64]
    for z in range(6, -1, -1):
        downward = rho * downward + rows[8 * z : 8 * z + 8]
    return upward, downward


def incoming(upward, downward, weights):
    low = jnp.sum(weights[0] * upward + weights[1] * downward, axis=0)
    high = jnp.sum(weights[2] * upward + weights[3] * downward, axis=0)
    return low, high


def solved(rows, low, high, rho, scale):
    inverse = 1.0 / rho
    cells = [rows[8 * z : 8 * z + 8] for z in range(8)]
    wave = low * inverse
    forward = [wave]
    for z in range(8):
        wave = rho * wave + cells[z]
        forward.append(wave)
    forward.append(rho * wave)
    wave = high
    backward = [high * inverse, high]
    for z in range(7, -1, -1):
        wave = rho * (wave + cells[z])
        backward.append(wave)
    backward = backward[::-1]
    return jnp.concatenate([scale * (f + b) for f, b in zip(forward, backward)], axis=0)


def to_rims(modes, table_y, source):
    rows = dot_nt(table_y, modes)
    devices = rows.shape[0] // 4
    blocks = [rows[devices * y : devices * y + devices] for y in range(4)]
    blocks = [moved(blocks[3], 1), *blocks, moved(blocks[0], -1)]
    return picked(jnp.concatenate(blocks, axis=1), source)


def from_rims(message, table_x):
    stacked = jnp.concatenate([message[:, 64 * k : 64 * k + 64] for k in range(8)], axis=0)
    return dot(stacked.T, table_x)


def fluxes(slots, beta_x, beta_y, beta_z):
    tiles = [slots[8 * y : 8 * y + 8] for y in range(6)]
    flux_y = [beta_y[y] * (tiles[y + 1] - tiles[y]) for y in range(5)]
    layer = lax.broadcasted_iota(jnp.int32, tiles[0].shape, 0)
    results = []
    for y in range(4):
        cells = tiles[y + 1]
        forward_x = beta_x[y] * (rolled(cells, -1, 1) - cells)
        above = jnp.where(layer == 7, slots[52 + y : 53 + y], rolled(cells, -1, 0))
        below = jnp.where(layer == 0, slots[48 + y : 49 + y], rolled(cells, 1, 0))
        results.append(
            (
                cells,
                forward_x,
                rolled(forward_x, 1, 1),
                flux_y[y + 1],
                flux_y[y],
                beta_z[0, y] * (above - cells),
                beta_z[1, y] * (cells - below),
            )
        )
    return results


def applied_rows(slots, beta_x, beta_y, beta_z):
    rows = []
    for cells, fx, bx, fy, by, fz, bz in fluxes(slots, beta_x, beta_y, beta_z):
        rows.append(compressibility * cells - (fx - bx + (fy - by) + (fz - bz)))
    return jnp.concatenate(rows, axis=0)


def total(values):
    return jnp.sum(jnp.sum(values, axis=0, keepdims=True), axis=1, keepdims=True)


def lane_row(values):
    lane = lax.broadcasted_iota(jnp.int32, (1, 128), 1)
    row = jnp.zeros((1, 128), jnp.float32)
    for index, value in enumerate(values):
        row = jnp.where(lane == index, value, row)
    return row


def send_fields(fields_ref, table_ref, out_ref):
    table = table_ref[...]
    for c in range(3):
        message = to_message(fields_ref[c].reshape(32, NX), table)
        out_ref[:, 2 * c, :] = message[:, :128]
        out_ref[:, 2 * c + 1, :] = message[:, 128:]


def read_fields(message_ref, table_ref, source_ref, rho_ref, gather_ref, rows_ref):
    tiles = message_ref[...]
    source = source_ref[...]
    parts = []
    for c in range(3):
        pair = jnp.concatenate([tiles[:, 2 * c, :], tiles[:, 2 * c + 1, :]], axis=1)
        parts.append(row_blocks(pair, source))
    across, along_y, along_z = parts
    after = [*along_y[1:], moved(along_y[0], -1)]
    before = [moved(along_y[3], 1), *along_y[:3]]
    table = table_ref[...]
    joined = to_modes([s - 0.5 * (a - b) for s, a, b in zip(across, after, before)], table)
    third = to_modes(along_z, table)
    zero = jnp.zeros_like(third[:8])
    above = jnp.concatenate([third[8:], zero], axis=0)
    below = jnp.concatenate([zero, third[:-8]], axis=0)
    rows = joined - 0.5 * (above - below)
    rho = rho_ref[...]
    upward, downward = moments(rows, rho)
    gather_ref[0:8] = upward
    gather_ref[8:16] = downward
    gather_ref[16:24] = third[0:8]
    gather_ref[24:32] = third[56:64]
    rows_ref[...] = rows


def first_solve(gather_ref, rows_ref, edge_ref, rho_ref, scale_ref, weights_ref, table_ref, source_ref,
                out_ref, residual_ref, waves_ref, aligned_ref):
    rho = rho_ref[...]
    power = rho * rho
    power = power * power * power * rho
    gathered = gather_ref[...]
    first, last = gathered[:, 16:24], gathered[:, 24:32]
    zero = jnp.zeros_like(first[:1])
    under = 0.5 * jnp.concatenate([zero, last[:-1]], axis=0)
    over = -0.5 * jnp.concatenate([first[1:], zero], axis=0)
    upward = gathered[:, 0:8] + power * under + over
    downward = gathered[:, 8:16] + under + power * over
    low, high = incoming(upward, downward, weights_ref[...])
    mine = edge_ref[...]
    rows = rows_ref[...]
    rows = jnp.concatenate(
        [
            rows[:8] + jnp.sum(mine * under, axis=0),
            rows[8:56],
            rows[56:] + jnp.sum(mine * over, axis=0),
        ],
        axis=0,
    )
    modes = solved(rows, low, high, rho, scale_ref[...])
    aligned_ref[...] = lane_row([total(rows * modes[8:72])])
    residual_ref[...] = rows
    waves_ref[0:8] = low
    waves_ref[8:16] = high
    into_tiles(out_ref, to_rims(modes, table_ref[...], source_ref[...]))


def first_image(message_ref, aligned_ref, table_ref, beta_x_ref, beta_y_ref, beta_z_ref, out_ref, slots_ref, applied_ref):
    table = table_ref[...]
    slots = from_rims(from_tiles(message_ref[...], 4), table)
    applied = applied_rows(slots, beta_x_ref[...], beta_y_ref[...], beta_z_ref[...])
    slots_ref[...] = slots
    applied_ref[...] = applied
    message = to_message(applied, table)
    curvature = total(slots[8:40] * applied)
    out_ref[:, 0, :] = message[:, :128]
    out_ref[:, 1, :] = message[:, 128:]
    row = lane_row([aligned_ref[...][:, :1], curvature])
    out_ref[:, 2, :] = jnp.broadcast_to(row, (message.shape[0], 128))
    out_ref[:, 3, :] = jnp.zeros((message.shape[0], 128), jnp.float32)


def read_image(message_ref, table_ref, source_ref, rho_ref, gather_ref, rows_ref):
    tiles = message_ref[...]
    rows = to_modes(row_blocks(from_tiles(tiles, 2), source_ref[...]), table_ref[...])
    sums = jnp.sum(tiles[:, 2, :], axis=0, keepdims=True)
    upward, downward = moments(rows, rho_ref[...])
    gather_ref[0:8] = upward
    gather_ref[8:16] = downward
    gather_ref[16:24] = jnp.broadcast_to(jnp.concatenate([sums, sums], axis=1), (8, 256))
    rows_ref[...] = rows


def second_solve(gather_ref, rows_ref, residual_ref, waves_ref, rho_ref, scale_ref, weights_ref, table_ref, source_ref,
                 out_ref, scalars_ref):
    gathered = gather_ref[...]
    sums = jnp.sum(gathered[:, 16:17, :128], axis=0)
    aligned, curvature = sums[:, 0:1], sums[:, 1:2]
    step = aligned / curvature
    low, high = incoming(gathered[:, 0:8], gathered[:, 8:16], weights_ref[...])
    waves = waves_ref[...]
    rows = residual_ref[...] - step * rows_ref[...]
    modes = solved(rows, waves[0:8] - step * low, waves[8:16] - step * high, rho_ref[...], scale_ref[...])
    scalars_ref[...] = lane_row([total(rows * modes[8:72]), aligned, curvature])
    into_tiles(out_ref, to_rims(modes, table_ref[...], source_ref[...]))


def second_image(message_ref, scalars_ref, applied_ref, table_ref, beta_x_ref, beta_y_ref, beta_z_ref, slots_ref, out_ref):
    slots = from_rims(from_tiles(message_ref[...], 4), table_ref[...])
    slots_ref[...] = slots
    bent = total(slots[8:40] * applied_rows(slots, beta_x_ref[...], beta_y_ref[...], beta_z_ref[...]))
    crossed = total(slots[8:40] * applied_ref[...])
    row = lane_row([scalars_ref[...][:, 0:1], bent, crossed])
    out_ref[...] = jnp.broadcast_to(row[None], out_ref.shape)


def add_parts(parts_ref, out_ref):
    row = jnp.sum(parts_ref[...], axis=0)
    out_ref[...] = jnp.broadcast_to(row[None], out_ref.shape)


def finish(parts_ref, scalars_ref, first_ref, second_ref, beta_x_ref, beta_y_ref, beta_z_ref, provisional_ref, next_ref, pressure_ref):
    sums = jnp.sum(parts_ref[...], axis=0)
    renewed, bent, crossed = sums[:, 0:1], sums[:, 1:2], sums[:, 2:3]
    scalars = scalars_ref[...]
    aligned, curvature = scalars[:, 1:2], scalars[:, 2:3]
    ratio = renewed / aligned
    second_step = renewed / (bent + 2.0 * ratio * crossed + ratio * ratio * curvature)
    first = first_ref[...]
    slots = (aligned / curvature) * first + second_step * (second_ref[...] + ratio * first)
    parts = fluxes(slots, beta_x_ref[...], beta_y_ref[...], beta_z_ref[...])
    for y, (cells, fx, bx, fy, by, fz, bz) in enumerate(parts):
        pressure_ref[y] = cells
        next_ref[0, y] = provisional_ref[0, y] - 0.5 * (fx + bx)
        next_ref[1, y] = provisional_ref[1, y] - 0.5 * (fy + by)
        next_ref[2, y] = provisional_ref[2, y] - 0.5 * (fz + bz)


def run(kernel, outs, *arrays):
    shapes = [jax.ShapeDtypeStruct(shape, jnp.float32) for shape in outs]
    whole = pl.BlockSpec(memory_space=pltpu.VMEM)
    return pl.pallas_call(
        kernel,
        out_shape=shapes,
        in_specs=[whole] * len(arrays),
        out_specs=[whole] * len(outs),
        name=kernel.__name__,
    )(*arrays)


def rim_slots():
    places = [(0, z + 1) for z in range(8)]
    places += [(y + 1, z + 1) for y in range(4) for z in range(8)]
    places += [(5, z + 1) for z in range(8)]
    places += [(y + 1, 0) for y in range(4)] + [(y + 1, 9) for y in range(4)]
    lanes = [[(y * 10 + z) * 8 + k for y, z in places] + [-1] * (64 - len(places)) for k in range(8)]
    return np.array(lanes, np.int32).reshape(1, -1)


def wave_weights(index, rho, count):
    block = jnp.arange(count, dtype=jnp.int32)
    period = 16 * count
    behind = 8 * (index - block) - 7 + jnp.where(block < index, 0, period)
    ahead = 8 * (block - index) - 7 + jnp.where(block > index, 0, period)
    mirrored_low = 8 * (index + block) + 1
    mirrored_high = period - 15 - 8 * (index + block)
    exponents = jnp.stack([behind, mirrored_low, mirrored_high, ahead]).astype(jnp.float32)
    log_rho = jnp.log(rho)
    powers = jnp.exp(exponents[:, :, None, None] * log_rho)
    return powers / (1.0 - jnp.exp(period * log_rho))


def on_device(velocity, fraction, wall_flags):
    rows, cols = (fraction.shape[0], fraction.shape[1])
    rows_devices = lax.axis_size("py")
    cols_devices = lax.axis_size("pz")
    total_rows = rows * rows_devices
    row_index = lax.axis_index("py")
    col_index = lax.axis_index("pz")

    def y_layers(part):
        return part.reshape(9, cols, NX)

    y_head = jnp.concatenate([y_layers(velocity[:, :3]), fraction[:1]], axis=0)
    y_tail = jnp.concatenate([y_layers(velocity[:, -3:]), fraction[-1:]], axis=0)
    y_low, y_high = shifted_pair(y_head, y_tail, "py")

    def z_layers(first, only):
        lanes = jnp.transpose(velocity[:, :, first : first + 3], (0, 2, 1, 3)).reshape(9, rows, NX)
        return jnp.concatenate([lanes, fraction[:, only][None]], axis=0)

    z_low, z_high = shifted_pair(z_layers(0, 0), z_layers(cols - 3, cols - 1), "pz")

    def unlayered(z_rim):
        return jnp.transpose(z_rim[:9].reshape(3, 3, rows, NX), (0, 2, 1, 3))

    provisional = predicted(
        velocity,
        wall_ghosts(velocity, wall_flags),
        jnp.concatenate([y_low[:9].reshape(3, 3, cols, NX), velocity, y_high[:9].reshape(3, 3, cols, NX)], axis=1),
        jnp.concatenate([unlayered(z_low), velocity, unlayered(z_high)], axis=2),
        fraction,
    )

    def density_of(part):
        return 1.0 + (heavy_density - 1.0) * part

    density = density_of(fraction)
    inner_x = 2.0 / (density[:, :, 1:] + density[:, :, :-1])
    beta_x = jnp.concatenate([inner_x, jnp.zeros_like(density[:, :, :1])], axis=2)
    along_y = jnp.concatenate([density_of(y_low[9:]), density, density_of(y_high[9:])], axis=0)
    face = row_index * rows + jnp.arange(rows + 1, dtype=jnp.int32)[:, None, None]
    wall = (face == 0) | (face == total_rows)
    beta_y = jnp.where(wall, 0.0, 2.0 / (along_y[1:] + along_y[:-1]))
    over = jnp.concatenate([density[:, 1:], density_of(z_high[9][:, None])], axis=1)
    under = jnp.concatenate([density_of(z_low[9][:, None]), density[:, :-1]], axis=1)
    layer = col_index * cols + jnp.arange(cols, dtype=jnp.int32)[None, :, None]
    plus_z = jnp.where(layer == cols_devices * cols - 1, 0.0, 2.0 / (density + over))
    minus_z = jnp.where(layer == 0, 0.0, 2.0 / (density + under))
    betas = (beta_x, beta_y, jnp.stack([plus_z, minus_z]))

    normal_x = provisional[0]
    forward_x = jnp.concatenate([normal_x[:, :, 1:], -normal_x[:, :, -1:]], axis=2)
    backward_x = jnp.concatenate([-normal_x[:, :, :1], normal_x[:, :, :-1]], axis=2)
    source_x = -0.5 * (forward_x - backward_x)
    fields = jnp.stack([source_x, provisional[1], provisional[2]])

    part_x = NX // rows_devices
    plain_x = cosine_table(NX).reshape(rows_devices, part_x, NX).transpose(1, 0, 2).reshape(NX, NX)
    plain_y = cosine_table(total_rows).T.reshape(rows_devices, rows, total_rows)
    plain_y = plain_y.transpose(1, 0, 2).reshape(total_rows, total_rows)
    table_x = jnp.asarray(plain_x, dtype=jnp.float32)
    table_y = jnp.asarray(plain_y, dtype=jnp.float32)
    inner = np.arange(256)
    row_source = jnp.asarray((inner % 8 * 32 + inner // 64 * 8 + inner // 8 % 8)[None].astype(np.int32))
    rim_source = jnp.asarray(rim_slots())

    half_x = lax.dynamic_slice(
        jnp.asarray(half_eigenvalue(NX), dtype=jnp.float32), (row_index * part_x,), (part_x,)
    )
    half_y = jnp.asarray(half_eigenvalue(total_rows), dtype=jnp.float32)
    shift = compressibility + half_x[:, None] + half_y[None, :]
    root = jnp.sqrt(shift * (shift + 2.0))
    rho = 1.0 / (1.0 + shift + root)
    scale = 1.0 / root
    weights = wave_weights(col_index, rho, cols_devices)
    here = jnp.arange(cols_devices, dtype=jnp.int32) == col_index
    edge = jnp.broadcast_to(here.astype(jnp.float32)[:, None, None], (cols_devices, part_x, total_rows))

    modes_shape = (64, total_rows)
    wide = (rows_devices, 8, 128)
    narrow = (rows_devices, 4, 128)
    (message,) = run(send_fields, [wide], fields, table_x)
    message = exchange(message, "py")
    gather, modes = run(
        read_fields, [(32, total_rows), modes_shape], message, table_y, row_source, rho
    )
    gather = lax.all_gather(gather, "pz")
    message, residual, waves, aligned = run(
        first_solve,
        [narrow, modes_shape, (16, total_rows), (1, 128)],
        gather, modes, edge, rho, scale, weights, table_y, rim_source,
    )
    message = exchange(message, "py")
    message, first, applied = run(
        first_image, [narrow, (64, NX), (32, NX)], message, aligned, table_x, *betas
    )
    message = exchange(message, "py")
    gather, modes = run(
        read_image, [(24, total_rows), modes_shape], message, table_y, row_source, rho
    )
    gather = lax.all_gather(gather, "pz")
    message, scalars = run(
        second_solve,
        [narrow, (1, 128)],
        gather, modes, residual, waves, rho, scale, weights, table_y, rim_source,
    )
    message = exchange(message, "py")
    second, parts = run(
        second_image, [(64, NX), (rows_devices, 1, 128)], message, scalars, applied, table_x, *betas
    )
    (parts,) = run(add_parts, [(cols_devices, 1, 128)], exchange(parts, "py"))
    parts = exchange(parts, "pz")
    next_velocity, pressure = run(
        finish,
        [velocity.shape, fraction.shape],
        parts, scalars, first, second, *betas, provisional,
    )
    return next_velocity, pressure


def solution(mesh):
    in_specs = (P(None, "py", "pz", None), P("py", "pz", None), P(None, "py", "pz"))
    out_specs = (P(None, "py", "pz", None), P("py", "pz", None))
    return jax.shard_map(
        on_device, mesh=mesh, in_specs=in_specs, out_specs=out_specs, check_vma=False
    )
```

time: 246 us -> 218 us (0.89)
  Pallas kernels: 0 us -> 27.2 us
  blocking collectives: 83.2 us -> 108 us
  local copies, waits for them, and re-layouts: 32.2 us -> 7.54 us
  waiting for transfers between devices: 42.3 us -> 26.1 us
  starting transfers between devices: 50.4 us -> 38.5 us
  other arithmetic: 19.4 us -> 8.7 us
  matrix products: 9.93 us -> 0 us
  between operations: 6.99 us -> 1.08 us
    all_gather x0 -> x2, blocking collectives: none -> 42.4 us  [on_device(): gather = lax.all_gather(gather, 'pz')]
    pallas_call x0 -> x9, Pallas kernels: none -> 27.2 us  [run(): pl.pallas_call(kernel, out_shape=shapes, in_specs=[whole] * len(arrays),...]
    all_to_all x6 -> x4, blocking collectives: 83.2 us -> 65.7 us  [exchange(): lax.all_to_all(message, axis, split_axis=0, concat_axis=0, tiled=True)]
    all_to_all x4 -> x2, waiting for transfers between devices: 37.2 us -> 23.8 us  [exchange(): lax.all_to_all(message, axis, split_axis=0, concat_axis=0, tiled=True)]
    all_to_all x4 -> x2, starting transfers between devices: 30.5 us -> 18.5 us  [exchange(): lax.all_to_all(message, axis, split_axis=0, concat_axis=0, tiled=True)]
    dot_general x13 -> x0, matrix products: 9.93 us -> none  [the longest x11 8 us: dot(): return jnp.dot(left, right, precision=highest)]
    transpose x9 -> x1, local copies, waits for them, and re-layouts: 8.66 us -> 0.08 us  [unlayered(): return jnp.transpose(z_rim[:9].reshape(3, 3, rows, NX), (0, 2, 1, 3))]
    slice x21 -> x3, local copies, waits for them, and re-layouts: 6.41 us -> 0.04 us  [the longest x2 0.03 us: on_device(): y_head = jnp.concatenate([y_layers(velocity[:, :3]), fraction[:1]], axis=0)]
  transfers between devices with their start and end apart: 8 -> 6, of which waited for: 6 -> 3; matrix products, arithmetic and copies ran while one was open for 4% -> 3% of each run, Pallas kernels for 0% -> 0%
where the time goes in v2:
time: 218 us; the launch traced here: 217 us
  blocking collectives  108 us (50%)
  starting transfers between devices  38.5 us (18%)
  Pallas kernels  27.2 us (12%)
  waiting for transfers between devices  26.1 us (12%)
  other arithmetic  8.7 us (4%)
  local copies, waits for them, and re-layouts  7.54 us (3%)
    all_to_all x4, blocking collectives, exchange(): lax.all_to_all(message, axis, split_axis=0, concat_axis=0, tiled=True)  65.7 us
    all_gather x2, blocking collectives, on_device(): gather = lax.all_gather(gather, 'pz')  42.4 us
    pallas_call x9, Pallas kernels, run(): pl.pallas_call(kernel, out_shape=shapes, in_specs=[whole] * len(arrays),...  27.2 us
    all_to_all x2, waiting for transfers between devices, exchange(): lax.all_to_all(message, axis, split_axis=0, concat_axis=0, tiled=True)  23.8 us
    ppermute x4, starting transfers between devices, shifted_pair(): return (lax.ppermute(tail, axis, up), lax.ppermute(head, axis, down))  20 us
    all_to_all x2, starting transfers between devices, exchange(): lax.all_to_all(message, axis, split_axis=0, concat_axis=0, tiled=True)  18.5 us
  transfers between devices with their start and end apart: 6, of which 3 were waited for; matrix products, arithmetic and copies ran while one was open for 3% of the time, Pallas kernels for 0%

profile of v2, /device:TPU:1, one launch (start us, length us, event | category | flops | bytes accessed | tf_op | source)
XLA Modules:
  0.0 217.2 jit_solution(311461019588662051)
XLA Ops:
  2.7 4.5 %collective-permute-start.3 = (f32[10,4,512]{2,0,1:T(8,128)S(1)}, f32[10,4,512]{2,0,1:T(8,128)S(1)}, u32[]{:S(2)}, u32[]{:S(2)}) collective-permute-start(f32[10,4,512]{2,0,1:T(8,128)S(1)} %pad_maximum_fusion.13), channel_id=1, source_target_pairs={{0,1},{1,2},{2,3},{3,4},{4,5},{5,6},{6,7},{7,8},{8,9},{9,10},{10,1... | collective-permute-start | bytes 245768 | tf_op jit(solution)/shard_map/ppermute | solution.py:88
  7.4 13.0 %collective-permute-start.2 = (f32[10,4,512]{2,0,1:T(8,128)S(1)}, f32[10,4,512]{2,0,1:T(8,128)S(1)}, u32[]{:S(2)}, u32[]{:S(2)}) collective-permute-start(f32[10,4,512]{2,0,1:T(8,128)S(1)} %pad_maximum_fusion.12), channel_id=1, source_target_pairs={{1,0},{2,1},{3,2},{4,3},{5,4},{6,5},{7,6},{8,7},{9,8},{10,9},{11,1... | collective-permute-start | bytes 245768 | tf_op jit(solution)/shard_map/ppermute | solution.py:88
  20.4 1.3 collective-permute-start.1
  27.3 2.3 %collective-permute-done = f32[10,8,512]{2,1,0:T(8,128)S(1)} collective-permute-done((f32[10,8,512]{2,1,0:T(8,128)S(1)}, f32[10,8,512]{2,1,0:T(8,128)S(1)}, u32[]{:S(2)}, u32[]{:S(2)}) %collective-permute-start) | collective-permute-done | bytes 163872 | tf_op jit(solution)/shard_map/ppermute | solution.py:88
  29.6 3.1 %fusion.6.provisional_ref = f32[3,4,8,512]{3,2,1,0:T(8,128)S(1)} fusion(f32[3,4,8,512]{3,2,1,0:T(8,128)S(1)} %copy-done, f32[3,4,3,512]{3,2,1,0:T(4,128)S(1)} %get-tuple-element.65, f32[3,4,3,512]{3,2,1,0:T(4,128)S(1)} %get-tuple-element.66, f32[3,3,8,512]{3,2,1,0:T(8,128)S(1)} %bitcast.64, f32[3,3,8,512]{3,2,1,0:T(8,128)S(1)} %bitcast.66, ...), kind=kLoop, calls=%fused_computation.14 | loop fusion | flops 19611648 | bytes 4688128 | tf_op jit(solution)/shard_map/add | solution.py:72
  35.2 4.8 %send_fields.1 = f32[64,8,128]{2,1,0:T(8,128)} custom-call(f32[3,4,8,512]{3,2,1,0:T(8,128)} %pad_maximum_fusion.9.fields_ref, f32[512,512]{1,0:T(8,128)} %constant.163.clone.table_ref), custom_call_target="tpu_custom_call" | custom-call | tf_op jit(solution)/shard_map/send_fields/pallas_call | solution.py:395
  40.0 13.9 %all-to-all-start = ((f32[64,8,128]{2,1,0:T(8,128)}), f32[64,8,128]{2,1,0:T(8,128)S(1)}, u32[]{:S(2)}, u32[]{:S(2)}) async-start(f32[64,8,128]{2,1,0:T(8,128)} %send_fields.1), calls=%async_computation | async-start | bytes 524288 | tf_op jit(solution)/shard_map/all_to_all | solution.py:104
  55.5 12.7 %all-to-all-done.message_ref = f32[64,8,128]{2,1,0:T(8,128)S(1)} async-done(((f32[64,8,128]{2,1,0:T(8,128)}), f32[64,8,128]{2,1,0:T(8,128)S(1)}, u32[]{:S(2)}, u32[]{:S(2)}) %all-to-all-start) | async-done | bytes 262176 | tf_op jit(solution)/shard_map/all_to_all | solution.py:104
  68.9 2.7 %read_fields.1 = (f32[32,256]{1,0:T(8,128)}, f32[64,256]{1,0:T(8,128)}) custom-call(f32[64,8,128]{2,1,0:T(8,128)} %copy-done.2, f32[256,256]{1,0:T(8,128)} %constant.164.clone.table_ref, s32[1,256]{1,0:T(1,128)} %constant.165.clone.source_ref, f32[8,256]{1,0:T(8,128)} %get-tuple-element.62.rho_ref), custom_call_target="tpu_custom_call" | custom-call | tf_op jit(solution)/shard_map/read_fields/pallas_call | solution.py:395
  71.6 21.6 %all-gather = f32[512,256]{1,0:T(8,128)} all-gather(f32[32,256]{1,0:T(8,128)} %get-tuple-element.17), channel_id=2, replica_groups=mesh['py'=64,'pz'=16] {'pz'}, dimensions={0}, use_global_device_ids=true | all-gather | bytes 557056 | tf_op jit(solution)/shard_map/all_gather | solution.py:511
  94.0 3.3 %first_solve.1 = (f32[64,4,128]{2,1,0:T(4,128)}, f32[64,256]{1,0:T(8,128)}, f32[16,256]{1,0:T(8,128)}, f32[1,128]{1,0:T(1,128)}) custom-call(f32[16,32,256]{2,1,0:T(8,128)} %bitcast.61, f32[64,256]{1,0:T(8,128)} %get-tuple-element.18.rows_ref, f32[16,8,256]{2,1,0:T(8,128)} %broadcast_in_dim.85.edge_ref, f32[8,256]{1,0:T(8,128)} %get-tuple-element.62.rho_ref, ...), custom_call_target="tpu_custom_call" | custom-call | tf_op jit(solution)/shard_map/first_solve/pallas_call | solution.py:395
  97.3 4.6 %all-to-all-start.1 = ((f32[64,4,128]{2,1,0:T(4,128)}), f32[64,4,128]{2,1,0:T(4,128)S(1)}, u32[]{:S(2)}, u32[]{:S(2)}) async-start(f32[64,4,128]{2,1,0:T(4,128)} %get-tuple-element.19), calls=%async_computation.1 | async-start | bytes 262144 | tf_op jit(solution)/shard_map/all_to_all | solution.py:104
  102.6 11.1 %all-to-all-done.1.message_ref = f32[64,4,128]{2,1,0:T(4,128)S(1)} async-done(((f32[64,4,128]{2,1,0:T(4,128)}), f32[64,4,128]{2,1,0:T(4,128)S(1)}, u32[]{:S(2)}, u32[]{:S(2)}) %all-to-all-start.1) | async-done | bytes 131104 | tf_op jit(solution)/shard_map/all_to_all | solution.py:104
  114.3 4.1 %first_image.1 = (f32[64,4,128]{2,1,0:T(4,128)}, f32[64,512]{1,0:T(8,128)}, f32[32,512]{1,0:T(8,128)}) custom-call(f32[64,4,128]{2,1,0:T(4,128)} %copy-done.3, f32[1,128]{1,0:T(1,128)} %get-tuple-element.20.aligned_ref, f32[512,512]{1,0:T(8,128)} %constant.163.clone.table_ref, f32[4,8,512]{2,1,0:T(8,128)} %concatenate.106.beta_x_ref, ...), custom_call_target="tpu_custom_call" | custom-call | tf_op jit(solution)/shard_map/first_image/pallas_call | solution.py:395
  118.4 17.1 %all_to_all.30.message_ref = f32[64,4,128]{2,1,0:T(4,128)} all-to-all(f32[64,4,128]{2,1,0:T(4,128)} %get-tuple-element.21), channel_id=1, replica_groups=mesh['py'=64,'pz'=16] {'py'}, dimensions={0} | all-to-all | bytes 262144 | tf_op jit(solution)/shard_map/all_to_all | solution.py:104
  135.5 2.3 %read_image.1 = (f32[24,256]{1,0:T(8,128)}, f32[64,256]{1,0:T(8,128)}) custom-call(f32[64,4,128]{2,1,0:T(4,128)} %all_to_all.30.message_ref, f32[256,256]{1,0:T(8,128)} %constant.164.clone.table_ref, s32[1,256]{1,0:T(1,128)} %constant.165.clone.source_ref, f32[8,256]{1,0:T(8,128)} %get-tuple-element.62.rho_ref), custom_call_target="tpu_custom_call" | custom-call | tf_op jit(solution)/shard_map/read_image/pallas_call | solution.py:395
  137.7 20.8 %all-gather.1 = f32[384,256]{1,0:T(8,128)} all-gather(f32[24,256]{1,0:T(8,128)} %get-tuple-element.22), channel_id=3, replica_groups=mesh['py'=64,'pz'=16] {'pz'}, dimensions={0}, use_global_device_ids=true | all-gather | bytes 417792 | tf_op jit(solution)/shard_map/all_gather | solution.py:525
  158.6 3.3 %second_solve.1 = (f32[64,4,128]{2,1,0:T(4,128)}, f32[1,128]{1,0:T(1,128)}) custom-call(f32[16,24,256]{2,1,0:T(8,128)} %bitcast.62, f32[64,256]{1,0:T(8,128)} %get-tuple-element.23.rows_ref, f32[64,256]{1,0:T(8,128)} %get-tuple-element.24.residual_ref, f32[16,256]{1,0:T(8,128)} %get-tuple-element.25.waves_ref, f32[8,256]{1,0:T(8,128)} %get-tuple-element.62.rho_ref, ...), custom_call_target="tpu_custom_call" | custom-call | tf_op jit(solution)/shard_map/second_solve/pallas_call | solution.py:395
  161.8 17.1 %all_to_all.31.message_ref = f32[64,4,128]{2,1,0:T(4,128)} all-to-all(f32[64,4,128]{2,1,0:T(4,128)} %get-tuple-element.26), channel_id=1, replica_groups=mesh['py'=64,'pz'=16] {'py'}, dimensions={0} | all-to-all | bytes 262144 | tf_op jit(solution)/shard_map/all_to_all | solution.py:104
  179.0 3.0 %second_image.1 = (f32[64,512]{1,0:T(8,128)}, f32[64,1,128]{2,1,0:T(1,128)}) custom-call(f32[64,4,128]{2,1,0:T(4,128)} %all_to_all.31.message_ref, f32[1,128]{1,0:T(1,128)} %get-tuple-element.27.scalars_ref, f32[32,512]{1,0:T(8,128)} %get-tuple-element.28.applied_ref, f32[512,512]{1,0:T(8,128)} %constant.163.clone.table_ref, ...), custom_call_target="tpu_custom_call" | custom-call | tf_op jit(solution)/shard_map/second_image/pallas_call | solution.py:395
  182.0 16.0 %all_to_all.32.parts_ref = f32[64,1,128]{2,1,0:T(1,128)} all-to-all(f32[64,1,128]{2,1,0:T(1,128)} %get-tuple-element.29), channel_id=1, replica_groups=mesh['py'=64,'pz'=16] {'py'}, dimensions={0} | all-to-all | bytes 65536 | tf_op jit(solution)/shard_map/all_to_all | solution.py:104
  197.9 1.4 add_parts.1
  199.4 15.5 %all_to_all.33.parts_ref = f32[16,1,128]{2,1,0:T(1,128)} all-to-all(f32[16,1,128]{2,1,0:T(1,128)} %add_parts.1), channel_id=1, replica_groups=mesh['py'=64,'pz'=16] {'pz'}, dimensions={0} | all-to-all | bytes 16384 | tf_op jit(solution)/shard_map/all_to_all | solution.py:104
  214.9 2.3 %finish.1 = (f32[3,4,8,512]{3,2,1,0:T(8,128)}, f32[4,8,512]{2,1,0:T(8,128)}) custom-call(f32[16,1,128]{2,1,0:T(1,128)} %all_to_all.33.parts_ref, f32[1,128]{1,0:T(1,128)} %get-tuple-element.27.scalars_ref, f32[64,512]{1,0:T(8,128)} %get-tuple-element.30.first_ref, f32[64,512]{1,0:T(8,128)} %get-tuple-element.31.second_ref, ...), custom_call_target="tpu_custom_call" | custom-call | tf_op jit(solution)/shard_map/finish/pallas_call | solution.py:395
  (79 shorter events, 14.5 us)
Async XLA Ops:
  2.7 24.0 %collective-permute-start.3 = (f32[10,4,512]{2,0,1:T(8,128)S(1)}, f32[10,4,512]{2,0,1:T(8,128)S(1)}, u32[]{:S(2)}, u32[]{:S(2)}) collective-permute-start(f32[10,4,512]{2,0,1:T(8,128)S(1)} %pad_maximum_fusion.13), channel_id=1, source_target_pairs={{0,1},{1,2},{2,3},{3,4},{4,5},{5,6},{6,7},{7,8},{8,9},{9,10},{10,1... | collective-permute-start | bytes 245768 | tf_op jit(solution)/shard_map/ppermute | solution.py:88
  7.3 13.0 %copy-start = (f32[3,4,8,512]{3,2,1,0:T(8,128)S(1)}, f32[3,4,8,512]{3,2,1,0:T(8,128)}, u32[]{:S(2)}) copy-start(f32[3,4,8,512]{3,2,1,0:T(8,128)} %param.9) | copy-start | bytes 589828
  7.3 13.0 %copy-start.4 = (f32[4,8,512]{2,1,0:T(8,128)S(1)}, f32[4,8,512]{2,1,0:T(8,128)}, u32[]{:S(2)}) copy-start(f32[4,8,512]{2,1,0:T(8,128)} %param.10) | copy-start | bytes 196612
  7.4 19.4 %collective-permute-start.2 = (f32[10,4,512]{2,0,1:T(8,128)S(1)}, f32[10,4,512]{2,0,1:T(8,128)S(1)}, u32[]{:S(2)}, u32[]{:S(2)}) collective-permute-start(f32[10,4,512]{2,0,1:T(8,128)S(1)} %pad_maximum_fusion.12), channel_id=1, source_target_pairs={{1,0},{2,1},{3,2},{4,3},{5,4},{6,5},{7,6},{8,7},{9,8},{10,9},{11,1... | collective-permute-start | bytes 245768 | tf_op jit(solution)/shard_map/ppermute | solution.py:88
  20.4 6.8 %collective-permute-start.1 = (f32[10,8,512]{2,1,0:T(8,128)S(1)}, f32[10,8,512]{2,1,0:T(8,128)S(1)}, u32[]{:S(2)}, u32[]{:S(2)}) collective-permute-start(f32[10,8,512]{2,1,0:T(8,128)S(1)} %pad_maximum_fusion.11), channel_id=1, source_target_pairs={{0,16},{16,32},{32,48},{48,64},{64,80},{80,96},{96,112},{112,128},... | collective-permute-start | bytes 491528 | tf_op jit(solution)/shard_map/ppermute | solution.py:88
  21.7 7.8 %collective-permute-start = (f32[10,8,512]{2,1,0:T(8,128)S(1)}, f32[10,8,512]{2,1,0:T(8,128)S(1)}, u32[]{:S(2)}, u32[]{:S(2)}) collective-permute-start(f32[10,8,512]{2,1,0:T(8,128)S(1)} %pad_maximum_fusion.10), channel_id=1, source_target_pairs={{16,0},{32,16},{48,32},{64,48},{80,64},{96,80},{112,96},{128,112},... | collective-permute-start | bytes 491528 | tf_op jit(solution)/shard_map/ppermute | solution.py:88
  23.4 0.7 copy-start.5
  24.6 0.8 copy-start.6
  32.7 0.7 copy-start.1
  33.6 0.9 slice-start
  40.0 28.2 %all-to-all-start = ((f32[64,8,128]{2,1,0:T(8,128)}), f32[64,8,128]{2,1,0:T(8,128)S(1)}, u32[]{:S(2)}, u32[]{:S(2)}) async-start(f32[64,8,128]{2,1,0:T(8,128)} %send_fields.1), calls=%async_computation | async-start | bytes 524288 | tf_op jit(solution)/shard_map/all_to_all | solution.py:104
  68.2 0.7 copy-start.2
  97.3 16.4 %all-to-all-start.1 = ((f32[64,4,128]{2,1,0:T(4,128)}), f32[64,4,128]{2,1,0:T(4,128)S(1)}, u32[]{:S(2)}, u32[]{:S(2)}) async-start(f32[64,4,128]{2,1,0:T(4,128)} %get-tuple-element.19), calls=%async_computation.1 | async-start | bytes 262144 | tf_op jit(solution)/shard_map/all_to_all | solution.py:104
  113.7 0.7 copy-start.3

commit v3 on v2

--- a/solution.py
+++ b/solution.py
@@ -1,5 +1,3 @@
-import math
-
 import jax
 import jax.numpy as jnp
 import numpy as np
@@ -9,7 +7,6 @@
 from jax.sharding import PartitionSpec as P
 
 NX = 512
-ITERS = 2
 
 
 time_step = 0.05
@@ -148,19 +145,29 @@
         ref[:, t, :] = values[:, 128 * t : 128 * t + 128]
 
 
-def to_message(rows, table_x):
+def to_messages(rows, table_x):
     spectral = dot_nt(table_x, rows)
     devices = spectral.shape[0] // 8
-    return jnp.concatenate([spectral[devices * k : devices * k + devices] for k in range(8)], axis=1)
-
-
-def row_blocks(message, source):
-    ordered = picked(message, source)
-    return [ordered[:, 64 * y : 64 * y + 64] for y in range(4)]
-
-
-def to_modes(blocks, table_y):
-    return dot(jnp.concatenate(blocks, axis=0).T, table_y)
+    blocks = [spectral[devices * k : devices * k + devices] for k in range(8)]
+    return [
+        jnp.concatenate([block[:, 32 * c : 32 * c + 32] for block in blocks], axis=1)
+        for c in range(rows.shape[0] // 32)
+    ]
+
+
+def row_blocks(messages, source):
+    ordered = picked(jnp.concatenate(messages, axis=0), source)
+    devices = messages[0].shape[0]
+    return [
+        [ordered[devices * c : devices * c + devices, 64 * y : 64 * y + 64] for y in range(4)]
+        for c in range(len(messages))
+    ]
+
+
+def to_modes(fields, table_y):
+    cells = [jnp.concatenate(blocks, axis=0).T for blocks in fields]
+    modes = dot(jnp.concatenate(cells, axis=0), table_y)
+    return [modes[64 * c : 64 * c + 64] for c in range(len(fields))]
 
 
 def moments(rows, rho):
@@ -253,27 +260,28 @@
     return row
 
 
-def send_fields(fields_ref, table_ref, out_ref):
-    table = table_ref[...]
-    for c in range(3):
-        message = to_message(fields_ref[c].reshape(32, NX), table)
+def send_fields(provisional_ref, table_ref, out_ref):
+    normal = provisional_ref[0].reshape(32, NX)
+    lane = lax.broadcasted_iota(jnp.int32, normal.shape, 1)
+    after = jnp.where(lane == NX - 1, -normal, rolled(normal, -1, 1))
+    before = jnp.where(lane == 0, -normal, rolled(normal, 1, 1))
+    rows = [-0.5 * (after - before)]
+    rows += [provisional_ref[c].reshape(32, NX) for c in (1, 2)]
+    for c, message in enumerate(to_messages(jnp.concatenate(rows, axis=0), table_ref[...])):
         out_ref[:, 2 * c, :] = message[:, :128]
         out_ref[:, 2 * c + 1, :] = message[:, 128:]
 
 
 def read_fields(message_ref, table_ref, source_ref, rho_ref, gather_ref, rows_ref):
     tiles = message_ref[...]
-    source = source_ref[...]
-    parts = []
-    for c in range(3):
-        pair = jnp.concatenate([tiles[:, 2 * c, :], tiles[:, 2 * c + 1, :]], axis=1)
-        parts.append(row_blocks(pair, source))
-    across, along_y, along_z = parts
+    pairs = [
+        jnp.concatenate([tiles[:, 2 * c, :], tiles[:, 2 * c + 1, :]], axis=1) for c in range(3)
+    ]
+    across, along_y, along_z = row_blocks(pairs, source_ref[...])
     after = [*along_y[1:], moved(along_y[0], -1)]
     before = [moved(along_y[3], 1), *along_y[:3]]
-    table = table_ref[...]
-    joined = to_modes([s - 0.5 * (a - b) for s, a, b in zip(across, after, before)], table)
-    third = to_modes(along_z, table)
+    across = [s - 0.5 * (a - b) for s, a, b in zip(across, after, before)]
+    joined, third = to_modes([across, along_z], table_ref[...])
     zero = jnp.zeros_like(third[:8])
     above = jnp.concatenate([third[8:], zero], axis=0)
     below = jnp.concatenate([zero, third[:-8]], axis=0)
@@ -287,7 +295,7 @@
     rows_ref[...] = rows
 
 
-def first_solve(gather_ref, rows_ref, edge_ref, rho_ref, scale_ref, weights_ref, table_ref, source_ref,
+def first_solve(place_ref, gather_ref, rows_ref, rho_ref, scale_ref, weights_ref, table_ref, source_ref,
                 out_ref, residual_ref, waves_ref, aligned_ref):
     rho = rho_ref[...]
     power = rho * rho
@@ -300,13 +308,13 @@
     upward = gathered[:, 0:8] + power * under + over
     downward = gathered[:, 8:16] + under + power * over
     low, high = incoming(upward, downward, weights_ref[...])
-    mine = edge_ref[...]
+    mine = lax.broadcasted_iota(jnp.int32, under.shape, 0) == place_ref[0]
     rows = rows_ref[...]
     rows = jnp.concatenate(
         [
-            rows[:8] + jnp.sum(mine * under, axis=0),
+            rows[:8] + jnp.sum(jnp.where(mine, under, 0.0), axis=0),
             rows[8:56],
-            rows[56:] + jnp.sum(mine * over, axis=0),
+            rows[56:] + jnp.sum(jnp.where(mine, over, 0.0), axis=0),
         ],
         axis=0,
     )
@@ -324,7 +332,7 @@
     applied = applied_rows(slots, beta_x_ref[...], beta_y_ref[...], beta_z_ref[...])
     slots_ref[...] = slots
     applied_ref[...] = applied
-    message = to_message(applied, table)
+    (message,) = to_messages(applied, table)
     curvature = total(slots[8:40] * applied)
     out_ref[:, 0, :] = message[:, :128]
     out_ref[:, 1, :] = message[:, 128:]
@@ -335,7 +343,7 @@
 
 def read_image(message_ref, table_ref, source_ref, rho_ref, gather_ref, rows_ref):
     tiles = message_ref[...]
-    rows = to_modes(row_blocks(from_tiles(tiles, 2), source_ref[...]), table_ref[...])
+    (rows,) = to_modes(row_blocks([from_tiles(tiles, 2)], source_ref[...]), table_ref[...])
     sums = jnp.sum(tiles[:, 2, :], axis=0, keepdims=True)
     upward, downward = moments(rows, rho_ref[...])
     gather_ref[0:8] = upward
@@ -389,16 +397,23 @@
         next_ref[2, y] = provisional_ref[2, y] - 0.5 * (fz + bz)
 
 
-def run(kernel, outs, *arrays):
-    shapes = [jax.ShapeDtypeStruct(shape, jnp.float32) for shape in outs]
+def run(kernel, outs, *arrays, last=False):
     whole = pl.BlockSpec(memory_space=pltpu.VMEM)
+    scalar = pl.BlockSpec(memory_space=pltpu.SMEM)
+    scalars = [array.ndim == 1 for array in arrays]
+    kept = jax.ShapeDtypeStruct if last else pltpu.VMEM
     return pl.pallas_call(
         kernel,
-        out_shape=shapes,
-        in_specs=[whole] * len(arrays),
+        out_shape=[kept(shape, jnp.float32) for shape in outs],
+        in_specs=[scalar if small else whole for small in scalars],
         out_specs=[whole] * len(outs),
-        name=kernel.__name__,
-    )(*arrays)
+        compiler_params=pltpu.CompilerParams(vmem_limit_bytes=8 << 20),
+    )(
+        *[
+            array if small else pltpu.with_memory_space_constraint(array, pltpu.VMEM)
+            for array, small in zip(arrays, scalars)
+        ]
+    )
 
 
 def rim_slots():
@@ -472,12 +487,6 @@
     minus_z = jnp.where(layer == 0, 0.0, 2.0 / (density + under))
     betas = (beta_x, beta_y, jnp.stack([plus_z, minus_z]))
 
-    normal_x = provisional[0]
-    forward_x = jnp.concatenate([normal_x[:, :, 1:], -normal_x[:, :, -1:]], axis=2)
-    backward_x = jnp.concatenate([-normal_x[:, :, :1], normal_x[:, :, :-1]], axis=2)
-    source_x = -0.5 * (forward_x - backward_x)
-    fields = jnp.stack([source_x, provisional[1], provisional[2]])
-
     part_x = NX // rows_devices
     plain_x = cosine_table(NX).reshape(rows_devices, part_x, NX).transpose(1, 0, 2).reshape(NX, NX)
     plain_y = cosine_table(total_rows).T.reshape(rows_devices, rows, total_rows)
@@ -497,13 +506,12 @@
     rho = 1.0 / (1.0 + shift + root)
     scale = 1.0 / root
     weights = wave_weights(col_index, rho, cols_devices)
-    here = jnp.arange(cols_devices, dtype=jnp.int32) == col_index
-    edge = jnp.broadcast_to(here.astype(jnp.float32)[:, None, None], (cols_devices, part_x, total_rows))
+    place = col_index.astype(jnp.int32).reshape(1)
 
     modes_shape = (64, total_rows)
     wide = (rows_devices, 8, 128)
     narrow = (rows_devices, 4, 128)
-    (message,) = run(send_fields, [wide], fields, table_x)
+    (message,) = run(send_fields, [wide], provisional, table_x)
     message = exchange(message, "py")
     gather, modes = run(
         read_fields, [(32, total_rows), modes_shape], message, table_y, row_source, rho
@@ -512,7 +520,7 @@
     message, residual, waves, aligned = run(
         first_solve,
         [narrow, modes_shape, (16, total_rows), (1, 128)],
-        gather, modes, edge, rho, scale, weights, table_y, rim_source,
+        place, gather, modes, rho, scale, weights, table_y, rim_source,
     )
     message = exchange(message, "py")
     message, first, applied = run(
@@ -538,6 +546,7 @@
         finish,
         [velocity.shape, fraction.shape],
         parts, scalars, first, second, *betas, provisional,
+        last=True,
     )
     return next_velocity, pressure
 

time: 218 us -> 190 us (0.87)
  Pallas kernels: 27.2 us -> 11 us
  blocking collectives: 108 us -> 101 us
  local copies, waits for them, and re-layouts: 7.54 us -> 3.94 us
  other arithmetic: 8.7 us -> 5.16 us
  waiting for transfers between devices: 26.1 us -> 29 us
    pallas_call x9, Pallas kernels: 27.2 us -> 11 us  [run(): pl.pallas_call(kernel, out_shape=[kept(shape, jnp.float32) for shape in o...]
    all_to_all x4, blocking collectives: 65.7 us -> 61.4 us  [exchange(): lax.all_to_all(message, axis, split_axis=0, concat_axis=0, tiled=True)]
    all_gather x2, blocking collectives: 42.4 us -> 39.8 us  [on_device(): gather = lax.all_gather(gather, 'pz')]
  transfers between devices with their start and end apart: 6 -> 6, of which waited for: 3 -> 3; matrix products, arithmetic and copies ran while one was open for 3% -> 1% of each run, Pallas kernels for 0% -> 0%
where the time goes in v3:
time: 190 us; the launch traced here: 189 us
  blocking collectives  101 us (53%)
  starting transfers between devices  37.9 us (20%)
  waiting for transfers between devices  29 us (15%)
  Pallas kernels  11 us (6%)
  other arithmetic  5.16 us (3%)
  local copies, waits for them, and re-layouts  3.94 us (2%)
    all_to_all x4, blocking collectives, exchange(): lax.all_to_all(message, axis, split_axis=0, concat_axis=0, tiled=True)  61.4 us
    all_gather x2, blocking collectives, on_device(): gather = lax.all_gather(gather, 'pz')  39.8 us
    all_to_all x2, waiting for transfers between devices, exchange(): lax.all_to_all(message, axis, split_axis=0, concat_axis=0, tiled=True)  25.5 us
    ppermute x4, starting transfers between devices, shifted_pair(): return (lax.ppermute(tail, axis, up), lax.ppermute(head, axis, down))  20 us
    all_to_all x2, starting transfers between devices, exchange(): lax.all_to_all(message, axis, split_axis=0, concat_axis=0, tiled=True)  17.8 us
    pallas_call x9, Pallas kernels, run(): pl.pallas_call(kernel, out_shape=[kept(shape, jnp.float32) for shape in o...  11 us
  transfers between devices with their start and end apart: 6, of which 3 were waited for; matrix products, arithmetic and copies ran while one was open for 1% of the time, Pallas kernels for 0%

profile of v3, /device:TPU:1, one launch (start us, length us, event | category | flops | bytes accessed | tf_op | source)
XLA Modules:
  0.0 189.3 jit_solution(18333090198072655720)
XLA Ops:
  1.6 1.1 slice_bitcast_fusion.1
  2.7 4.5 %collective-permute-start.3 = (f32[10,4,512]{2,0,1:T(8,128)S(1)}, f32[10,4,512]{2,0,1:T(8,128)S(1)}, u32[]{:S(2)}, u32[]{:S(2)}) collective-permute-start(f32[10,4,512]{2,0,1:T(8,128)S(1)} %pad_maximum_fusion.12), channel_id=1, source_target_pairs={{0,1},{1,2},{2,3},{3,4},{4,5},{5,6},{6,7},{7,8},{8,9},{9,10},{10,1... | collective-permute-start | bytes 245768 | tf_op jit(solution)/shard_map/ppermute | solution.py:85
  7.4 13.0 %collective-permute-start.2 = (f32[10,4,512]{2,0,1:T(8,128)S(1)}, f32[10,4,512]{2,0,1:T(8,128)S(1)}, u32[]{:S(2)}, u32[]{:S(2)}) collective-permute-start(f32[10,4,512]{2,0,1:T(8,128)S(1)} %pad_maximum_fusion.11), channel_id=1, source_target_pairs={{1,0},{2,1},{3,2},{4,3},{5,4},{6,5},{7,6},{8,7},{9,8},{10,9},{11,1... | collective-permute-start | bytes 245768 | tf_op jit(solution)/shard_map/ppermute | solution.py:85
  20.4 1.3 collective-permute-start.1
  21.7 1.3 collective-permute-start
  26.1 3.5 %collective-permute-done = f32[10,8,512]{2,1,0:T(8,128)S(1)} collective-permute-done((f32[10,8,512]{2,1,0:T(8,128)S(1)}, f32[10,8,512]{2,1,0:T(8,128)S(1)}, u32[]{:S(2)}, u32[]{:S(2)}) %collective-permute-start) | collective-permute-done | bytes 163872 | tf_op jit(solution)/shard_map/ppermute | solution.py:85
  29.6 3.1 %fusion.6.provisional_ref = f32[3,4,8,512]{3,2,1,0:T(8,128)S(1)} fusion(f32[3,4,8,512]{3,2,1,0:T(8,128)S(1)} %copy-done.4, f32[3,4,3,512]{3,2,1,0:T(4,128)S(1)} %get-tuple-element.65, f32[3,4,3,512]{3,2,1,0:T(4,128)S(1)} %get-tuple-element.66, f32[3,3,8,512]{3,2,1,0:T(8,128)S(1)} %bitcast.55, f32[3,3,8,512]{3,2,1,0:T(8,128)S(1)} %bitcast.57, ...), kind=kLoop, calls=%fused_computation.14 | loop fusion | flops 19611648 | bytes 4688128 | tf_op jit(solution)/shard_map/add | solution.py:69
  32.7 1.9 %shard_map.104 = f32[64,8,128]{2,1,0:T(8,128)} custom-call(f32[3,4,8,512]{3,2,1,0:T(8,128)S(1)} %fusion.6.provisional_ref, f32[512,512]{1,0:T(8,128)S(1)} %copy-done), custom_call_target="tpu_custom_call" | custom-call | tf_op jit(solution)/shard_map/pallas_call | solution.py:405
  34.6 13.2 %all-to-all-start = ((f32[64,8,128]{2,1,0:T(8,128)}), f32[64,8,128]{2,1,0:T(8,128)S(1)}, u32[]{:S(2)}, u32[]{:S(2)}) async-start(f32[64,8,128]{2,1,0:T(8,128)} %shard_map.104), calls=%async_computation | async-start | bytes 524288 | tf_op jit(solution)/shard_map/all_to_all | solution.py:101
  48.1 13.8 %all-to-all-done.message_ref = f32[64,8,128]{2,1,0:T(8,128)S(1)} async-done(((f32[64,8,128]{2,1,0:T(8,128)}), f32[64,8,128]{2,1,0:T(8,128)S(1)}, u32[]{:S(2)}, u32[]{:S(2)}) %all-to-all-start) | async-done | bytes 262176 | tf_op jit(solution)/shard_map/all_to_all | solution.py:101
  61.9 1.0 shard_map.105
  62.8 21.0 %all-gather = f32[512,256]{1,0:T(8,128)S(1)} all-gather(f32[32,256]{1,0:T(8,128)S(1)} %get-tuple-element.17), channel_id=2, replica_groups=mesh['py'=64,'pz'=16] {'pz'}, dimensions={0}, use_global_device_ids=true | all-gather | bytes 557056 | tf_op jit(solution)/shard_map/all_gather | solution.py:519
  84.5 1.9 %shard_map.106 = (f32[64,4,128]{2,1,0:T(4,128)}, f32[64,256]{1,0:T(8,128)S(1)}, f32[16,256]{1,0:T(8,128)S(1)}, f32[1,128]{1,0:T(1,128)S(1)}) custom-call(s32[1]{0:T(128)} %bitcast.place_ref, f32[16,32,256]{2,1,0:T(8,128)S(1)} %bitcast.52, f32[64,256]{1,0:T(8,128)S(1)} %get-tuple-element.18.rows_ref, f32[8,256]{1,0:T(8,128)S(1)} %get-tuple-element.58.rho_ref, ...), custom_call_target="tpu_custom_call" | custom-call | tf_op jit(solution)/shard_map/pallas_call | solution.py:405
  86.5 4.6 %all-to-all-start.1 = ((f32[64,4,128]{2,1,0:T(4,128)}), f32[64,4,128]{2,1,0:T(4,128)S(1)}, u32[]{:S(2)}, u32[]{:S(2)}) async-start(f32[64,4,128]{2,1,0:T(4,128)} %get-tuple-element.19), calls=%async_computation.1 | async-start | bytes 262144 | tf_op jit(solution)/shard_map/all_to_all | solution.py:101
  91.2 11.7 %all-to-all-done.1.message_ref = f32[64,4,128]{2,1,0:T(4,128)S(1)} async-done(((f32[64,4,128]{2,1,0:T(4,128)}), f32[64,4,128]{2,1,0:T(4,128)S(1)}, u32[]{:S(2)}, u32[]{:S(2)}) %all-to-all-start.1) | async-done | bytes 131104 | tf_op jit(solution)/shard_map/all_to_all | solution.py:101
  102.9 2.1 %shard_map.107 = (f32[64,4,128]{2,1,0:T(4,128)S(1)}, f32[64,512]{1,0:T(8,128)S(1)}, f32[32,512]{1,0:T(8,128)S(1)}) custom-call(f32[64,4,128]{2,1,0:T(4,128)S(1)} %all-to-all-done.1.message_ref, f32[1,128]{1,0:T(1,128)S(1)} %get-tuple-element.20.aligned_ref, f32[512,512]{1,0:T(8,128)S(1)} %copy-done, f32[4,8,512]{2,1,0:T(8,128)S(1)} %concatenate.72.beta_x_ref, ...), custom_call_target="tpu_custom_call" | custom-call | tf_op jit(solution)/shard_map/pallas_call | solution.py:405
  104.9 15.6 %all_to_all.30.message_ref = f32[64,4,128]{2,1,0:T(4,128)S(1)} all-to-all(f32[64,4,128]{2,1,0:T(4,128)S(1)} %get-tuple-element.21), channel_id=1, replica_groups=mesh['py'=64,'pz'=16] {'py'}, dimensions={0} | all-to-all | bytes 262144 | tf_op jit(solution)/shard_map/all_to_all | solution.py:101
  121.2 18.8 %all-gather.1 = f32[384,256]{1,0:T(8,128)S(1)} all-gather(f32[24,256]{1,0:T(8,128)S(1)} %get-tuple-element.22), channel_id=3, replica_groups=mesh['py'=64,'pz'=16] {'pz'}, dimensions={0}, use_global_device_ids=true | all-gather | bytes 417792 | tf_op jit(solution)/shard_map/all_gather | solution.py:533
  140.0 1.3 shard_map.109
  141.3 15.6 %all_to_all.31.message_ref = f32[64,4,128]{2,1,0:T(4,128)S(1)} all-to-all(f32[64,4,128]{2,1,0:T(4,128)S(1)} %get-tuple-element.26), channel_id=1, replica_groups=mesh['py'=64,'pz'=16] {'py'}, dimensions={0} | all-to-all | bytes 262144 | tf_op jit(solution)/shard_map/all_to_all | solution.py:101
  156.8 1.0 shard_map.110
  157.9 15.0 %all_to_all.32.parts_ref = f32[64,1,128]{2,1,0:T(1,128)S(1)} all-to-all(f32[64,1,128]{2,1,0:T(1,128)S(1)} %get-tuple-element.29), channel_id=1, replica_groups=mesh['py'=64,'pz'=16] {'py'}, dimensions={0} | all-to-all | bytes 65536 | tf_op jit(solution)/shard_map/all_to_all | solution.py:101
  172.9 15.2 %all_to_all.33.parts_ref = f32[16,1,128]{2,1,0:T(1,128)S(1)} all-to-all(f32[16,1,128]{2,1,0:T(1,128)S(1)} %shard_map.111), channel_id=1, replica_groups=mesh['py'=64,'pz'=16] {'pz'}, dimensions={0} | all-to-all | bytes 16384 | tf_op jit(solution)/shard_map/all_to_all | solution.py:101
  188.2 1.1 shard_map.112
  (72 shorter events, 5.7 us)
Async XLA Ops:
  2.7 22.8 %collective-permute-start.3 = (f32[10,4,512]{2,0,1:T(8,128)S(1)}, f32[10,4,512]{2,0,1:T(8,128)S(1)}, u32[]{:S(2)}, u32[]{:S(2)}) collective-permute-start(f32[10,4,512]{2,0,1:T(8,128)S(1)} %pad_maximum_fusion.12), channel_id=1, source_target_pairs={{0,1},{1,2},{2,3},{3,4},{4,5},{5,6},{6,7},{7,8},{8,9},{9,10},{10,1... | collective-permute-start | bytes 245768 | tf_op jit(solution)/shard_map/ppermute | solution.py:85
  7.3 13.0 %copy-start.4 = (f32[3,4,8,512]{3,2,1,0:T(8,128)S(1)}, f32[3,4,8,512]{3,2,1,0:T(8,128)}, u32[]{:S(2)}) copy-start(f32[3,4,8,512]{3,2,1,0:T(8,128)} %param.9) | copy-start | bytes 589828
  7.3 13.0 %copy-start.5 = (f32[4,8,512]{2,1,0:T(8,128)S(1)}, f32[4,8,512]{2,1,0:T(8,128)}, u32[]{:S(2)}) copy-start(f32[4,8,512]{2,1,0:T(8,128)} %param.10) | copy-start | bytes 196612
  7.4 18.2 %collective-permute-start.2 = (f32[10,4,512]{2,0,1:T(8,128)S(1)}, f32[10,4,512]{2,0,1:T(8,128)S(1)}, u32[]{:S(2)}, u32[]{:S(2)}) collective-permute-start(f32[10,4,512]{2,0,1:T(8,128)S(1)} %pad_maximum_fusion.11), channel_id=1, source_target_pairs={{1,0},{2,1},{3,2},{4,3},{5,4},{6,5},{7,6},{8,7},{9,8},{10,9},{11,1... | collective-permute-start | bytes 245768 | tf_op jit(solution)/shard_map/ppermute | solution.py:85
  20.4 5.6 %collective-permute-start.1 = (f32[10,8,512]{2,1,0:T(8,128)S(1)}, f32[10,8,512]{2,1,0:T(8,128)S(1)}, u32[]{:S(2)}, u32[]{:S(2)}) collective-permute-start(f32[10,8,512]{2,1,0:T(8,128)S(1)} %pad_maximum_fusion.10), channel_id=1, source_target_pairs={{0,16},{16,32},{32,48},{48,64},{64,80},{80,96},{96,112},{112,128},... | collective-permute-start | bytes 491528 | tf_op jit(solution)/shard_map/ppermute | solution.py:85
  21.7 7.8 %collective-permute-start = (f32[10,8,512]{2,1,0:T(8,128)S(1)}, f32[10,8,512]{2,1,0:T(8,128)S(1)}, u32[]{:S(2)}, u32[]{:S(2)}) collective-permute-start(f32[10,8,512]{2,1,0:T(8,128)S(1)} %pad_maximum_fusion.9), channel_id=1, source_target_pairs={{16,0},{32,16},{48,32},{64,48},{80,64},{96,80},{112,96},{128,112},... | collective-permute-start | bytes 491528 | tf_op jit(solution)/shard_map/ppermute | solution.py:85
  23.3 0.7 copy-start.6
  24.6 0.8 copy-start.7
  29.6 3.1 %copy-start = (f32[512,512]{1,0:T(8,128)S(1)}, f32[512,512]{1,0:T(8,128)}, u32[]{:S(2)}) copy-start(f32[512,512]{1,0:T(8,128)} %constant.161.clone.table_ref) | copy-start | bytes 3145732
  34.6 27.2 %all-to-all-start = ((f32[64,8,128]{2,1,0:T(8,128)}), f32[64,8,128]{2,1,0:T(8,128)S(1)}, u32[]{:S(2)}, u32[]{:S(2)}) async-start(f32[64,8,128]{2,1,0:T(8,128)} %shard_map.104), calls=%async_computation | async-start | bytes 524288 | tf_op jit(solution)/shard_map/all_to_all | solution.py:101
  48.0 13.8 %copy-start.1 = (f32[256,256]{1,0:T(8,128)S(1)}, f32[256,256]{1,0:T(8,128)}, u32[]{:S(2)}) copy-start(f32[256,256]{1,0:T(8,128)} %constant.162.clone.table_ref) | copy-start | bytes 786436
  48.0 13.8 %copy-start.3 = (s32[1,256]{1,0:T(1,128)S(1)}, s32[1,256]{1,0:T(1,128)}, u32[]{:S(2)}) copy-start(s32[1,256]{1,0:T(1,128)} %constant.163.clone.source_ref) | copy-start | bytes 3076
  83.8 0.7 copy-start.2
  86.5 16.4 %all-to-all-start.1 = ((f32[64,4,128]{2,1,0:T(4,128)}), f32[64,4,128]{2,1,0:T(4,128)S(1)}, u32[]{:S(2)}, u32[]{:S(2)}) async-start(f32[64,4,128]{2,1,0:T(4,128)} %get-tuple-element.19), calls=%async_computation.1 | async-start | bytes 262144 | tf_op jit(solution)/shard_map/all_to_all | solution.py:101

commit v4 on v3

--- a/solution.py
+++ b/solution.py
@@ -4,7 +4,7 @@
 from jax import lax
 from jax.experimental import pallas as pl
 from jax.experimental.pallas import tpu as pltpu
-from jax.sharding import PartitionSpec as P
+from jax.sharding import Mesh, PartitionSpec as P
 
 NX = 512
 
@@ -147,8 +147,8 @@
 
 def to_messages(rows, table_x):
     spectral = dot_nt(table_x, rows)
-    devices = spectral.shape[0] // 8
-    blocks = [spectral[devices * k : devices * k + devices] for k in range(8)]
+    devices = spectral.shape[0] // 4
+    blocks = [spectral[devices * k : devices * k + devices] for k in range(4)]
     return [
         jnp.concatenate([block[:, 32 * c : 32 * c + 32] for block in blocks], axis=1)
         for c in range(rows.shape[0] // 32)
@@ -167,16 +167,26 @@
 def to_modes(fields, table_y):
     cells = [jnp.concatenate(blocks, axis=0).T for blocks in fields]
     modes = dot(jnp.concatenate(cells, axis=0), table_y)
-    return [modes[64 * c : 64 * c + 64] for c in range(len(fields))]
-
-
-def moments(rows, rho):
-    upward = rows[0:8]
-    for z in range(1, 8):
-        upward = rho * upward + rows[8 * z : 8 * z + 8]
-    downward = rows[56:64]
-    for z in range(6, -1, -1):
-        downward = rho * downward + rows[8 * z : 8 * z + 8]
+    layers = [
+        jnp.concatenate([modes[4 * r : 4 * r + 4, :128], modes[4 * r : 4 * r + 4, 128:]], axis=0)
+        for r in range(16 * len(fields))
+    ]
+    return [layers[16 * c : 16 * c + 16] for c in range(len(fields))]
+
+
+def from_layers(layers):
+    return jnp.concatenate(
+        [jnp.concatenate([layer[:4], layer[4:]], axis=1) for layer in layers], axis=0
+    )
+
+
+def moments(layers, rho):
+    upward = layers[0]
+    for layer in layers[1:]:
+        upward = rho * upward + layer
+    downward = layers[-1]
+    for layer in layers[-2::-1]:
+        downward = rho * downward + layer
     return upward, downward
 
 
@@ -186,34 +196,40 @@
     return low, high
 
 
-def solved(rows, low, high, rho, scale):
+def solved(layers, low, high, rho, scale):
     inverse = 1.0 / rho
-    cells = [rows[8 * z : 8 * z + 8] for z in range(8)]
     wave = low * inverse
     forward = [wave]
-    for z in range(8):
-        wave = rho * wave + cells[z]
+    for layer in layers:
+        wave = rho * wave + layer
         forward.append(wave)
     forward.append(rho * wave)
     wave = high
     backward = [high * inverse, high]
-    for z in range(7, -1, -1):
-        wave = rho * (wave + cells[z])
+    for layer in layers[::-1]:
+        wave = rho * (wave + layer)
         backward.append(wave)
     backward = backward[::-1]
-    return jnp.concatenate([scale * (f + b) for f, b in zip(forward, backward)], axis=0)
-
-
-def to_rims(modes, table_y, source):
-    rows = dot_nt(table_y, modes)
+    return [scale * (f + b) for f, b in zip(forward, backward)]
+
+
+def layers_total(left, right):
+    product = left[0] * right[0]
+    for one, other in zip(left[1:], right[1:]):
+        product = product + one * other
+    return total(product)
+
+
+def send_rims(out_ref, layers, table_y, source):
+    rows = dot_nt(table_y, from_layers(layers))
     devices = rows.shape[0] // 4
     blocks = [rows[devices * y : devices * y + devices] for y in range(4)]
     blocks = [moved(blocks[3], 1), *blocks, moved(blocks[0], -1)]
-    return picked(jnp.concatenate(blocks, axis=1), source)
+    into_tiles(out_ref, picked(jnp.concatenate(blocks, axis=1), source))
 
 
 def from_rims(message, table_x):
-    stacked = jnp.concatenate([message[:, 64 * k : 64 * k + 64] for k in range(8)], axis=0)
+    stacked = jnp.concatenate([message[:, 64 * k : 64 * k + 64] for k in range(4)], axis=0)
     return dot(stacked.T, table_x)
 
 
@@ -268,38 +284,38 @@
     rows = [-0.5 * (after - before)]
     rows += [provisional_ref[c].reshape(32, NX) for c in (1, 2)]
     for c, message in enumerate(to_messages(jnp.concatenate(rows, axis=0), table_ref[...])):
-        out_ref[:, 2 * c, :] = message[:, :128]
-        out_ref[:, 2 * c + 1, :] = message[:, 128:]
-
-
-def read_fields(message_ref, table_ref, source_ref, rho_ref, gather_ref, rows_ref):
+        out_ref[:, c, :] = message
+    out_ref[:, 3, :] = jnp.zeros_like(message)
+
+
+def read_fields(message_ref, table_ref, source_ref, rho_ref, gather_ref, layers_ref):
     tiles = message_ref[...]
-    pairs = [
-        jnp.concatenate([tiles[:, 2 * c, :], tiles[:, 2 * c + 1, :]], axis=1) for c in range(3)
-    ]
+    pairs = [jnp.concatenate([tiles[:, c, :], tiles[:, c + 4, :]], axis=1) for c in range(3)]
     across, along_y, along_z = row_blocks(pairs, source_ref[...])
     after = [*along_y[1:], moved(along_y[0], -1)]
     before = [moved(along_y[3], 1), *along_y[:3]]
     across = [s - 0.5 * (a - b) for s, a, b in zip(across, after, before)]
     joined, third = to_modes([across, along_z], table_ref[...])
-    zero = jnp.zeros_like(third[:8])
-    above = jnp.concatenate([third[8:], zero], axis=0)
-    below = jnp.concatenate([zero, third[:-8]], axis=0)
-    rows = joined - 0.5 * (above - below)
-    rho = rho_ref[...]
-    upward, downward = moments(rows, rho)
-    gather_ref[0:8] = upward
-    gather_ref[8:16] = downward
-    gather_ref[16:24] = third[0:8]
-    gather_ref[24:32] = third[56:64]
-    rows_ref[...] = rows
-
-
-def first_solve(place_ref, gather_ref, rows_ref, rho_ref, scale_ref, weights_ref, table_ref, source_ref,
+    zero = jnp.zeros_like(third[0])
+    above = [*third[1:], zero]
+    below = [zero, *third[:-1]]
+    layers = [j - 0.5 * (a - b) for j, a, b in zip(joined, above, below)]
+    upward, downward = moments(layers, rho_ref[...])
+    for device in range(gather_ref.shape[0]):
+        gather_ref[device, 0:8] = upward
+        gather_ref[device, 8:16] = downward
+        gather_ref[device, 16:24] = third[0]
+        gather_ref[device, 24:32] = third[-1]
+    for z, layer in enumerate(layers):
+        layers_ref[z] = layer
+
+
+def first_solve(place_ref, gather_ref, layers_ref, rho_ref, scale_ref, weights_ref, table_ref, source_ref,
                 out_ref, residual_ref, waves_ref, aligned_ref):
     rho = rho_ref[...]
-    power = rho * rho
-    power = power * power * power * rho
+    square = rho * rho
+    fourth = square * square
+    power = fourth * fourth * fourth * square * rho
     gathered = gather_ref[...]
     first, last = gathered[:, 16:24], gathered[:, 24:32]
     zero = jnp.zeros_like(first[:1])
@@ -309,65 +325,61 @@
     downward = gathered[:, 8:16] + under + power * over
     low, high = incoming(upward, downward, weights_ref[...])
     mine = lax.broadcasted_iota(jnp.int32, under.shape, 0) == place_ref[0]
-    rows = rows_ref[...]
-    rows = jnp.concatenate(
-        [
-            rows[:8] + jnp.sum(jnp.where(mine, under, 0.0), axis=0),
-            rows[8:56],
-            rows[56:] + jnp.sum(jnp.where(mine, over, 0.0), axis=0),
-        ],
-        axis=0,
-    )
-    modes = solved(rows, low, high, rho, scale_ref[...])
-    aligned_ref[...] = lane_row([total(rows * modes[8:72])])
-    residual_ref[...] = rows
-    waves_ref[0:8] = low
-    waves_ref[8:16] = high
-    into_tiles(out_ref, to_rims(modes, table_ref[...], source_ref[...]))
+    layers = [layers_ref[z] for z in range(16)]
+    layers[0] = layers[0] + jnp.sum(jnp.where(mine, under, 0.0), axis=0)
+    layers[15] = layers[15] + jnp.sum(jnp.where(mine, over, 0.0), axis=0)
+    modes = solved(layers, low, high, rho, scale_ref[...])
+    aligned_ref[...] = lane_row([layers_total(layers, modes[1:-1])])
+    for z, layer in enumerate(layers):
+        residual_ref[z] = layer
+    waves_ref[0] = low
+    waves_ref[1] = high
+    send_rims(out_ref, modes, table_ref[...], source_ref[...])
 
 
 def first_image(message_ref, aligned_ref, table_ref, beta_x_ref, beta_y_ref, beta_z_ref, out_ref, slots_ref, applied_ref):
     table = table_ref[...]
-    slots = from_rims(from_tiles(message_ref[...], 4), table)
+    slots = from_rims(from_tiles(message_ref[...], 2), table)
     applied = applied_rows(slots, beta_x_ref[...], beta_y_ref[...], beta_z_ref[...])
     slots_ref[...] = slots
     applied_ref[...] = applied
     (message,) = to_messages(applied, table)
     curvature = total(slots[8:40] * applied)
-    out_ref[:, 0, :] = message[:, :128]
-    out_ref[:, 1, :] = message[:, 128:]
+    out_ref[:, 0, :] = message
     row = lane_row([aligned_ref[...][:, :1], curvature])
-    out_ref[:, 2, :] = jnp.broadcast_to(row, (message.shape[0], 128))
-    out_ref[:, 3, :] = jnp.zeros((message.shape[0], 128), jnp.float32)
-
-
-def read_image(message_ref, table_ref, source_ref, rho_ref, gather_ref, rows_ref):
+    out_ref[:, 1, :] = jnp.broadcast_to(row, message.shape)
+
+
+def read_image(message_ref, table_ref, source_ref, rho_ref, gather_ref, layers_ref):
     tiles = message_ref[...]
-    (rows,) = to_modes(row_blocks([from_tiles(tiles, 2)], source_ref[...]), table_ref[...])
-    sums = jnp.sum(tiles[:, 2, :], axis=0, keepdims=True)
-    upward, downward = moments(rows, rho_ref[...])
-    gather_ref[0:8] = upward
-    gather_ref[8:16] = downward
-    gather_ref[16:24] = jnp.broadcast_to(jnp.concatenate([sums, sums], axis=1), (8, 256))
-    rows_ref[...] = rows
-
-
-def second_solve(gather_ref, rows_ref, residual_ref, waves_ref, rho_ref, scale_ref, weights_ref, table_ref, source_ref,
+    pair = jnp.concatenate([tiles[:, 0, :], tiles[:, 2, :]], axis=1)
+    (layers,) = to_modes(row_blocks([pair], source_ref[...]), table_ref[...])
+    sums = jnp.sum(tiles[:, 1, :] + tiles[:, 3, :], axis=0, keepdims=True)
+    upward, downward = moments(layers, rho_ref[...])
+    sums = jnp.broadcast_to(sums, upward.shape)
+    for device in range(gather_ref.shape[0]):
+        gather_ref[device, 0:8] = upward
+        gather_ref[device, 8:16] = downward
+        gather_ref[device, 16:24] = sums
+    for z, layer in enumerate(layers):
+        layers_ref[z] = layer
+
+
+def second_solve(gather_ref, layers_ref, residual_ref, waves_ref, rho_ref, scale_ref, weights_ref, table_ref, source_ref,
                  out_ref, scalars_ref):
     gathered = gather_ref[...]
-    sums = jnp.sum(gathered[:, 16:17, :128], axis=0)
+    sums = jnp.sum(gathered[:, 16:24], axis=0)[:1]
     aligned, curvature = sums[:, 0:1], sums[:, 1:2]
     step = aligned / curvature
     low, high = incoming(gathered[:, 0:8], gathered[:, 8:16], weights_ref[...])
-    waves = waves_ref[...]
-    rows = residual_ref[...] - step * rows_ref[...]
-    modes = solved(rows, waves[0:8] - step * low, waves[8:16] - step * high, rho_ref[...], scale_ref[...])
-    scalars_ref[...] = lane_row([total(rows * modes[8:72]), aligned, curvature])
-    into_tiles(out_ref, to_rims(modes, table_ref[...], source_ref[...]))
+    layers = [residual_ref[z] - step * layers_ref[z] for z in range(16)]
+    modes = solved(layers, waves_ref[0] - step * low, waves_ref[1] - step * high, rho_ref[...], scale_ref[...])
+    scalars_ref[...] = lane_row([layers_total(layers, modes[1:-1]), aligned, curvature])
+    send_rims(out_ref, modes, table_ref[...], source_ref[...])
 
 
 def second_image(message_ref, scalars_ref, applied_ref, table_ref, beta_x_ref, beta_y_ref, beta_z_ref, slots_ref, out_ref):
-    slots = from_rims(from_tiles(message_ref[...], 4), table_ref[...])
+    slots = from_rims(from_tiles(message_ref[...], 2), table_ref[...])
     slots_ref[...] = slots
     bent = total(slots[8:40] * applied_rows(slots, beta_x_ref[...], beta_y_ref[...], beta_z_ref[...]))
     crossed = total(slots[8:40] * applied_ref[...])
@@ -421,17 +433,21 @@
     places += [(y + 1, z + 1) for y in range(4) for z in range(8)]
     places += [(5, z + 1) for z in range(8)]
     places += [(y + 1, 0) for y in range(4)] + [(y + 1, 9) for y in range(4)]
-    lanes = [[(y * 10 + z) * 8 + k for y, z in places] + [-1] * (64 - len(places)) for k in range(8)]
+    lanes = [
+        [(y * 18 + 8 * core + z) * 4 + k for y, z in places] + [-1] * (64 - len(places))
+        for core in range(2)
+        for k in range(4)
+    ]
     return np.array(lanes, np.int32).reshape(1, -1)
 
 
-def wave_weights(index, rho, count):
+def wave_weights(index, rho, count, size):
     block = jnp.arange(count, dtype=jnp.int32)
-    period = 16 * count
-    behind = 8 * (index - block) - 7 + jnp.where(block < index, 0, period)
-    ahead = 8 * (block - index) - 7 + jnp.where(block > index, 0, period)
-    mirrored_low = 8 * (index + block) + 1
-    mirrored_high = period - 15 - 8 * (index + block)
+    period = 2 * size * count
+    behind = size * (index - block) - size + 1 + jnp.where(block < index, 0, period)
+    ahead = size * (block - index) - size + 1 + jnp.where(block > index, 0, period)
+    mirrored_low = size * (index + block) + 1
+    mirrored_high = period - 2 * size + 1 - size * (index + block)
     exponents = jnp.stack([behind, mirrored_low, mirrored_high, ahead]).astype(jnp.float32)
     log_rho = jnp.log(rho)
     powers = jnp.exp(exponents[:, :, None, None] * log_rho)
@@ -441,10 +457,14 @@
 def on_device(velocity, fraction, wall_flags):
     rows, cols = (fraction.shape[0], fraction.shape[1])
     rows_devices = lax.axis_size("py")
-    cols_devices = lax.axis_size("pz")
+    chips = lax.axis_size("px")
+    cores = lax.axis_size("core")
+    cols_devices = chips * cores
     total_rows = rows * rows_devices
     row_index = lax.axis_index("py")
-    col_index = lax.axis_index("pz")
+    chip_index = lax.axis_index("px")
+    core_index = lax.axis_index("core")
+    col_index = chip_index * cores + core_index
 
     def y_layers(part):
         return part.reshape(9, cols, NX)
@@ -457,7 +477,7 @@
         lanes = jnp.transpose(velocity[:, :, first : first + 3], (0, 2, 1, 3)).reshape(9, rows, NX)
         return jnp.concatenate([lanes, fraction[:, only][None]], axis=0)
 
-    z_low, z_high = shifted_pair(z_layers(0, 0), z_layers(cols - 3, cols - 1), "pz")
+    z_low, z_high = shifted_pair(z_layers(0, 0), z_layers(cols - 3, cols - 1), ("px", "core"))
 
     def unlayered(z_rim):
         return jnp.transpose(z_rim[:9].reshape(3, 3, rows, NX), (0, 2, 1, 3))
@@ -487,61 +507,66 @@
     minus_z = jnp.where(layer == 0, 0.0, 2.0 / (density + under))
     betas = (beta_x, beta_y, jnp.stack([plus_z, minus_z]))
 
-    part_x = NX // rows_devices
-    plain_x = cosine_table(NX).reshape(rows_devices, part_x, NX).transpose(1, 0, 2).reshape(NX, NX)
+    peers = rows_devices * cores
+    part_x = NX // peers
+    plain_x = cosine_table(NX).reshape(peers, part_x, NX).transpose(1, 0, 2).reshape(NX, NX)
     plain_y = cosine_table(total_rows).T.reshape(rows_devices, rows, total_rows)
     plain_y = plain_y.transpose(1, 0, 2).reshape(total_rows, total_rows)
     table_x = jnp.asarray(plain_x, dtype=jnp.float32)
     table_y = jnp.asarray(plain_y, dtype=jnp.float32)
     inner = np.arange(256)
-    row_source = jnp.asarray((inner % 8 * 32 + inner // 64 * 8 + inner // 8 % 8)[None].astype(np.int32))
+    row_source = jnp.asarray(
+        (inner // 32 % 2 * 128 + inner % 4 * 32 + inner // 64 * 8 + inner // 4 % 8)[None].astype(np.int32)
+    )
     rim_source = jnp.asarray(rim_slots())
 
     half_x = lax.dynamic_slice(
-        jnp.asarray(half_eigenvalue(NX), dtype=jnp.float32), (row_index * part_x,), (part_x,)
+        jnp.asarray(half_eigenvalue(NX), dtype=jnp.float32), ((row_index * cores + core_index) * part_x,), (part_x,)
     )
     half_y = jnp.asarray(half_eigenvalue(total_rows), dtype=jnp.float32)
-    shift = compressibility + half_x[:, None] + half_y[None, :]
+    shift = compressibility + half_x[None, :, None] + half_y.reshape(2, 1, 128)
+    shift = shift.reshape(8, 128)
     root = jnp.sqrt(shift * (shift + 2.0))
     rho = 1.0 / (1.0 + shift + root)
     scale = 1.0 / root
-    weights = wave_weights(col_index, rho, cols_devices)
-    place = col_index.astype(jnp.int32).reshape(1)
-
-    modes_shape = (64, total_rows)
-    wide = (rows_devices, 8, 128)
-    narrow = (rows_devices, 4, 128)
-    (message,) = run(send_fields, [wide], provisional, table_x)
-    message = exchange(message, "py")
-    gather, modes = run(
-        read_fields, [(32, total_rows), modes_shape], message, table_y, row_source, rho
-    )
-    gather = lax.all_gather(gather, "pz")
+    size = cols * cores
+    weights = wave_weights(chip_index, rho, chips, size)
+    place = chip_index.astype(jnp.int32).reshape(1)
+
+    across = ("py", "core")
+    layers_shape = (size, 8, 128)
+    rims_shape = (rows_devices, 4, 128)
+    (message,) = run(send_fields, [(peers, 4, 128)], provisional, table_x)
+    message = exchange(message, across).reshape(rows_devices, 8, 128)
+    gather, layers = run(
+        read_fields, [(chips, 32, 128), layers_shape], message, table_y, row_source, rho
+    )
+    gather = exchange(gather, "px")
     message, residual, waves, aligned = run(
         first_solve,
-        [narrow, modes_shape, (16, total_rows), (1, 128)],
-        place, gather, modes, rho, scale, weights, table_y, rim_source,
-    )
-    message = exchange(message, "py")
+        [rims_shape, layers_shape, (2, 8, 128), (1, 128)],
+        place, gather, layers, rho, scale, weights, table_y, rim_source,
+    )
+    message = exchange(message.reshape(peers, 2, 128), across)
     message, first, applied = run(
-        first_image, [narrow, (64, NX), (32, NX)], message, aligned, table_x, *betas
-    )
-    message = exchange(message, "py")
-    gather, modes = run(
-        read_image, [(24, total_rows), modes_shape], message, table_y, row_source, rho
-    )
-    gather = lax.all_gather(gather, "pz")
+        first_image, [(peers, 2, 128), (64, NX), (32, NX)], message, aligned, table_x, *betas
+    )
+    message = exchange(message, across).reshape(rows_devices, 4, 128)
+    gather, layers = run(
+        read_image, [(chips, 24, 128), layers_shape], message, table_y, row_source, rho
+    )
+    gather = exchange(gather, "px")
     message, scalars = run(
         second_solve,
-        [narrow, (1, 128)],
-        gather, modes, residual, waves, rho, scale, weights, table_y, rim_source,
-    )
-    message = exchange(message, "py")
+        [rims_shape, (1, 128)],
+        gather, layers, residual, waves, rho, scale, weights, table_y, rim_source,
+    )
+    message = exchange(message.reshape(peers, 2, 128), across)
     second, parts = run(
-        second_image, [(64, NX), (rows_devices, 1, 128)], message, scalars, applied, table_x, *betas
-    )
-    (parts,) = run(add_parts, [(cols_devices, 1, 128)], exchange(parts, "py"))
-    parts = exchange(parts, "pz")
+        second_image, [(64, NX), (peers, 1, 128)], message, scalars, applied, table_x, *betas
+    )
+    (parts,) = run(add_parts, [(chips, 1, 128)], exchange(parts, across))
+    parts = exchange(parts, "px")
     next_velocity, pressure = run(
         finish,
         [velocity.shape, fraction.shape],
@@ -552,8 +577,14 @@
 
 
 def solution(mesh):
-    in_specs = (P(None, "py", "pz", None), P("py", "pz", None), P(None, "py", "pz"))
-    out_specs = (P(None, "py", "pz", None), P("py", "pz", None))
+    rows = mesh.shape["py"]
+    split = Mesh(mesh.devices.reshape(rows, -1, 2), ("py", "px", "core"))
+    wide = P(None, "py", ("px", "core"), None)
+    flat = P("py", ("px", "core"), None)
     return jax.shard_map(
-        on_device, mesh=mesh, in_specs=in_specs, out_specs=out_specs, check_vma=False
-    )
+        on_device,
+        mesh=split,
+        in_specs=(wide, flat, P(None, "py", ("px", "core"))),
+        out_specs=(wide, flat),
+        check_vma=False,
+    )

time: 190 us -> 185 us (0.974)
  blocking collectives: 101 us -> 72.2 us
  starting transfers between devices: 37.9 us -> 50.4 us
  waiting for transfers between devices: 29 us -> 38.4 us
    all_gather x2 -> x0, blocking collectives: 39.8 us -> none  [on_device(): gather = lax.all_gather(gather, 'pz')]
    all_to_all x2 -> x3, starting transfers between devices: 17.8 us -> 30.4 us  [exchange(): lax.all_to_all(message, axis, split_axis=0, concat_axis=0, tiled=True)]
    all_to_all x4 -> x5, blocking collectives: 61.4 us -> 72.2 us  [exchange(): lax.all_to_all(message, axis, split_axis=0, concat_axis=0, tiled=True)]
    all_to_all x2 -> x3, waiting for transfers between devices: 25.5 us -> 35.7 us  [exchange(): lax.all_to_all(message, axis, split_axis=0, concat_axis=0, tiled=True)]
  transfers between devices with their start and end apart: 6 -> 7, of which waited for: 3 -> 4; matrix products, arithmetic and copies ran while one was open for 1% -> 1% of each run, Pallas kernels for 0% -> 0%
where the time goes in v4:
time: 185 us; the launch traced here: 184 us
  blocking collectives  72.2 us (39%)
  starting transfers between devices  50.4 us (27%)
  waiting for transfers between devices  38.4 us (21%)
  Pallas kernels  11.7 us (6%)
  other arithmetic  5.13 us (3%)
  local copies, waits for them, and re-layouts  4.7 us (3%)
    all_to_all x5, blocking collectives, exchange(): lax.all_to_all(message, axis, split_axis=0, concat_axis=0, tiled=True)  72.2 us
    all_to_all x3, waiting for transfers between devices, exchange(): lax.all_to_all(message, axis, split_axis=0, concat_axis=0, tiled=True)  35.7 us
    all_to_all x3, starting transfers between devices, exchange(): lax.all_to_all(message, axis, split_axis=0, concat_axis=0, tiled=True)  30.4 us
    ppermute x4, starting transfers between devices, shifted_pair(): return (lax.ppermute(tail, axis, up), lax.ppermute(head, axis, down))  20 us
    pallas_call x9, Pallas kernels, run(): pl.pallas_call(kernel, out_shape=[kept(shape, jnp.float32) for shape in o...  11.7 us
  transfers between devices with their start and end apart: 7, of which 4 were waited for; matrix products, arithmetic and copies ran while one was open for 1% of the time, Pallas kernels for 0%

profile of v4, /device:TPU:1, one launch (start us, length us, event | category | flops | bytes accessed | tf_op | source)
XLA Modules:
  0.0 183.8 jit_solution(12587775170939399046)
XLA Ops:
  2.7 4.5 %collective-permute-start.3 = (f32[10,4,512]{2,0,1:T(8,128)S(1)}, f32[10,4,512]{2,0,1:T(8,128)S(1)}, u32[]{:S(2)}, u32[]{:S(2)}) collective-permute-start(f32[10,4,512]{2,0,1:T(8,128)S(1)} %pad_maximum_fusion.12), channel_id=1, source_target_pairs={{0,1},{1,2},{2,3},{3,4},{4,5},{5,6},{6,7},{7,8},{8,9},{9,10},{10,1... | collective-permute-start | bytes 245768 | tf_op jit(solution)/shard_map/ppermute | solution.py:85
  7.4 13.0 %collective-permute-start.2 = (f32[10,4,512]{2,0,1:T(8,128)S(1)}, f32[10,4,512]{2,0,1:T(8,128)S(1)}, u32[]{:S(2)}, u32[]{:S(2)}) collective-permute-start(f32[10,4,512]{2,0,1:T(8,128)S(1)} %pad_maximum_fusion.11), channel_id=1, source_target_pairs={{1,0},{2,1},{3,2},{4,3},{5,4},{6,5},{7,6},{8,7},{9,8},{10,9},{11,1... | collective-permute-start | bytes 245768 | tf_op jit(solution)/shard_map/ppermute | solution.py:85
  20.4 1.3 collective-permute-start.1
  21.7 1.3 collective-permute-start
  26.8 2.7 %collective-permute-done = f32[10,8,512]{2,1,0:T(8,128)S(1)} collective-permute-done((f32[10,8,512]{2,1,0:T(8,128)S(1)}, f32[10,8,512]{2,1,0:T(8,128)S(1)}, u32[]{:S(2)}, u32[]{:S(2)}) %collective-permute-start) | collective-permute-done | bytes 163872 | tf_op jit(solution)/shard_map/ppermute | solution.py:85
  29.6 3.1 %fusion.6.provisional_ref = f32[3,4,8,512]{3,2,1,0:T(8,128)S(1)} fusion(f32[3,4,8,512]{3,2,1,0:T(8,128)S(1)} %copy-done.4, f32[3,4,3,512]{3,2,1,0:T(4,128)S(1)} %get-tuple-element.64, f32[3,4,3,512]{3,2,1,0:T(4,128)S(1)} %get-tuple-element.65, f32[3,3,8,512]{3,2,1,0:T(8,128)S(1)} %bitcast.59, f32[3,3,8,512]{3,2,1,0:T(8,128)S(1)} %bitcast.61, ...), kind=kLoop, calls=%fused_computation.13 | loop fusion | flops 19611648 | bytes 4688128 | tf_op jit(solution)/shard_map/add | solution.py:69
  32.7 2.0 %shard_map.104 = f32[128,4,128]{2,1,0:T(4,128)} custom-call(f32[3,4,8,512]{3,2,1,0:T(8,128)S(1)} %fusion.6.provisional_ref, f32[512,512]{1,0:T(8,128)S(1)} %copy-done), custom_call_target="tpu_custom_call" | custom-call | tf_op jit(solution)/shard_map/pallas_call | solution.py:417
  34.7 14.3 %all-to-all-start = ((f32[128,4,128]{2,1,0:T(4,128)}), f32[128,4,128]{2,1,0:T(4,128)S(1)}, u32[]{:S(2)}, u32[]{:S(2)}) async-start(f32[128,4,128]{2,1,0:T(4,128)} %shard_map.104), calls=%async_computation | async-start | bytes 524288 | tf_op jit(solution)/shard_map/all_to_all | solution.py:101
  49.1 15.1 %all-to-all-done = f32[128,4,128]{2,1,0:T(4,128)S(1)} async-done(((f32[128,4,128]{2,1,0:T(4,128)}), f32[128,4,128]{2,1,0:T(4,128)S(1)}, u32[]{:S(2)}, u32[]{:S(2)}) %all-to-all-start) | async-done | bytes 262176 | tf_op jit(solution)/shard_map/all_to_all | solution.py:101
  64.2 1.7 shard_map.105
  65.9 8.8 %all-to-all-start.1 = ((f32[8,32,128]{2,1,0:T(8,128)}), f32[8,32,128]{2,1,0:T(8,128)S(1)}, u32[]{:S(2)}, u32[]{:S(2)}) async-start(f32[8,32,128]{2,1,0:T(8,128)} %get-tuple-element.17), calls=%async_computation.1 | async-start | bytes 262144 | tf_op jit(solution)/shard_map/all_to_all | solution.py:101
  74.7 7.9 %all-to-all-done.1.gather_ref = f32[8,32,128]{2,1,0:T(8,128)S(1)} async-done(((f32[8,32,128]{2,1,0:T(8,128)}), f32[8,32,128]{2,1,0:T(8,128)S(1)}, u32[]{:S(2)}, u32[]{:S(2)}) %all-to-all-start.1) | async-done | bytes 131104 | tf_op jit(solution)/shard_map/all_to_all | solution.py:101
  83.3 1.8 shard_map.106
  85.0 7.3 %all-to-all-start.2 = ((f32[128,2,128]{2,1,0:T(2,128)}), f32[128,2,128]{2,1,0:T(2,128)S(1)}, u32[]{:S(2)}, u32[]{:S(2)}) async-start(f32[128,2,128]{2,1,0:T(2,128)} %bitcast.26), calls=%async_computation.2 | async-start | bytes 262144 | tf_op jit(solution)/shard_map/all_to_all | solution.py:101
  92.4 12.7 %all-to-all-done.2.message_ref = f32[128,2,128]{2,1,0:T(2,128)S(1)} async-done(((f32[128,2,128]{2,1,0:T(2,128)}), f32[128,2,128]{2,1,0:T(2,128)S(1)}, u32[]{:S(2)}, u32[]{:S(2)}) %all-to-all-start.2) | async-done | bytes 131104 | tf_op jit(solution)/shard_map/all_to_all | solution.py:101
  105.2 2.1 %shard_map.107 = (f32[128,2,128]{2,1,0:T(2,128)S(1)}, f32[64,512]{1,0:T(8,128)S(1)}, f32[32,512]{1,0:T(8,128)S(1)}) custom-call(f32[128,2,128]{2,1,0:T(2,128)S(1)} %all-to-all-done.2.message_ref, f32[1,128]{1,0:T(1,128)S(1)} %get-tuple-element.20.aligned_ref, f32[512,512]{1,0:T(8,128)S(1)} %copy-done, f32[4,8,512]{2,1,0:T(8,128)S(1)} %concatenate.72.beta_x_ref, ...), custom_call_target="tpu_custom_call" | custom-call | tf_op jit(solution)/shard_map/pallas_call | solution.py:417
  107.3 17.7 %all_to_all.40 = f32[128,2,128]{2,1,0:T(2,128)S(1)} all-to-all(f32[128,2,128]{2,1,0:T(2,128)S(1)} %get-tuple-element.21), channel_id=1, replica_groups=mesh['py'=64,'px'=8,'core'=2] {'py','core'}, dimensions={0} | all-to-all | bytes 262144 | tf_op jit(solution)/shard_map/all_to_all | solution.py:101
  125.7 9.9 %all_to_all.41.gather_ref = f32[8,24,128]{2,1,0:T(8,128)S(1)} all-to-all(f32[8,24,128]{2,1,0:T(8,128)S(1)} %get-tuple-element.22), channel_id=1, replica_groups=mesh['py'=64,'px'=8,'core'=2] {'px'}, dimensions={0} | all-to-all | bytes 196608 | tf_op jit(solution)/shard_map/all_to_all | solution.py:101
  135.7 1.2 shard_map.109
  136.8 19.1 %all_to_all.42.message_ref = f32[128,2,128]{2,1,0:T(2,128)S(1)} all-to-all(f32[128,2,128]{2,1,0:T(2,128)S(1)} %bitcast.57), channel_id=1, replica_groups=mesh['py'=64,'px'=8,'core'=2] {'py','core'}, dimensions={0} | all-to-all | bytes 262144 | tf_op jit(solution)/shard_map/all_to_all | solution.py:101
  156.0 1.1 shard_map.110
  157.1 16.5 %all_to_all.43.parts_ref = f32[128,1,128]{2,1,0:T(1,128)S(1)} all-to-all(f32[128,1,128]{2,1,0:T(1,128)S(1)} %get-tuple-element.29), channel_id=1, replica_groups=mesh['py'=64,'px'=8,'core'=2] {'py','core'}, dimensions={0} | all-to-all | bytes 131072 | tf_op jit(solution)/shard_map/all_to_all | solution.py:101
  173.7 8.9 %all_to_all.44.parts_ref = f32[8,1,128]{2,1,0:T(1,128)S(1)} all-to-all(f32[8,1,128]{2,1,0:T(1,128)S(1)} %shard_map.111), channel_id=1, replica_groups=mesh['py'=64,'px'=8,'core'=2] {'px'}, dimensions={0} | all-to-all | bytes 8192 | tf_op jit(solution)/shard_map/all_to_all | solution.py:101
  182.6 1.1 shard_map.112
  (77 shorter events, 7.6 us)
Async XLA Ops:
  2.7 23.5 %collective-permute-start.3 = (f32[10,4,512]{2,0,1:T(8,128)S(1)}, f32[10,4,512]{2,0,1:T(8,128)S(1)}, u32[]{:S(2)}, u32[]{:S(2)}) collective-permute-start(f32[10,4,512]{2,0,1:T(8,128)S(1)} %pad_maximum_fusion.12), channel_id=1, source_target_pairs={{0,1},{1,2},{2,3},{3,4},{4,5},{5,6},{6,7},{7,8},{8,9},{9,10},{10,1... | collective-permute-start | bytes 245768 | tf_op jit(solution)/shard_map/ppermute | solution.py:85
  7.3 13.0 %copy-start.4 = (f32[3,4,8,512]{3,2,1,0:T(8,128)S(1)}, f32[3,4,8,512]{3,2,1,0:T(8,128)}, u32[]{:S(2)}) copy-start(f32[3,4,8,512]{3,2,1,0:T(8,128)} %param.9) | copy-start | bytes 589828
  7.3 13.0 %copy-start.5 = (f32[4,8,512]{2,1,0:T(8,128)S(1)}, f32[4,8,512]{2,1,0:T(8,128)}, u32[]{:S(2)}) copy-start(f32[4,8,512]{2,1,0:T(8,128)} %param.10) | copy-start | bytes 196612
  7.4 19.0 %collective-permute-start.2 = (f32[10,4,512]{2,0,1:T(8,128)S(1)}, f32[10,4,512]{2,0,1:T(8,128)S(1)}, u32[]{:S(2)}, u32[]{:S(2)}) collective-permute-start(f32[10,4,512]{2,0,1:T(8,128)S(1)} %pad_maximum_fusion.11), channel_id=1, source_target_pairs={{1,0},{2,1},{3,2},{4,3},{5,4},{6,5},{7,6},{8,7},{9,8},{10,9},{11,1... | collective-permute-start | bytes 245768 | tf_op jit(solution)/shard_map/ppermute | solution.py:85
  20.4 6.4 %collective-permute-start.1 = (f32[10,8,512]{2,1,0:T(8,128)S(1)}, f32[10,8,512]{2,1,0:T(8,128)S(1)}, u32[]{:S(2)}, u32[]{:S(2)}) collective-permute-start(f32[10,8,512]{2,1,0:T(8,128)S(1)} %pad_maximum_fusion.10), channel_id=1, source_target_pairs={{0,16},{16,32},{32,48},{48,64},{64,80},{80,96},{96,112},{112,128},... | collective-permute-start | bytes 491528 | tf_op jit(solution)/shard_map/ppermute | solution.py:85
  21.7 7.8 %collective-permute-start = (f32[10,8,512]{2,1,0:T(8,128)S(1)}, f32[10,8,512]{2,1,0:T(8,128)S(1)}, u32[]{:S(2)}, u32[]{:S(2)}) collective-permute-start(f32[10,8,512]{2,1,0:T(8,128)S(1)} %pad_maximum_fusion.9), channel_id=1, source_target_pairs={{16,0},{32,16},{48,32},{64,48},{80,64},{96,80},{112,96},{128,112},... | collective-permute-start | bytes 491528 | tf_op jit(solution)/shard_map/ppermute | solution.py:85
  23.3 0.7 copy-start.6
  25.5 0.7 copy-start.7
  29.6 3.1 %copy-start = (f32[512,512]{1,0:T(8,128)S(1)}, f32[512,512]{1,0:T(8,128)}, u32[]{:S(2)}) copy-start(f32[512,512]{1,0:T(8,128)} %constant.170.clone.table_ref) | copy-start | bytes 3145732
  34.7 29.5 %copy-start.1 = (f32[256,256]{1,0:T(8,128)S(1)}, f32[256,256]{1,0:T(8,128)}, u32[]{:S(2)}) copy-start(f32[256,256]{1,0:T(8,128)} %constant.171.clone.table_ref) | copy-start | bytes 786436
  34.7 29.5 %all-to-all-start = ((f32[128,4,128]{2,1,0:T(4,128)}), f32[128,4,128]{2,1,0:T(4,128)S(1)}, u32[]{:S(2)}, u32[]{:S(2)}) async-start(f32[128,4,128]{2,1,0:T(4,128)} %shard_map.104), calls=%async_computation | async-start | bytes 524288 | tf_op jit(solution)/shard_map/all_to_all | solution.py:101
  49.1 15.1 %copy-start.3 = (s32[1,256]{1,0:T(1,128)S(1)}, s32[1,256]{1,0:T(1,128)}, u32[]{:S(2)}) copy-start(s32[1,256]{1,0:T(1,128)} %constant.172.clone.source_ref) | copy-start | bytes 3076
  65.9 16.7 %all-to-all-start.1 = ((f32[8,32,128]{2,1,0:T(8,128)}), f32[8,32,128]{2,1,0:T(8,128)S(1)}, u32[]{:S(2)}, u32[]{:S(2)}) async-start(f32[8,32,128]{2,1,0:T(8,128)} %get-tuple-element.17), calls=%async_computation.1 | async-start | bytes 262144 | tf_op jit(solution)/shard_map/all_to_all | solution.py:101
  82.6 0.7 copy-start.2
  85.0 20.1 %all-to-all-start.2 = ((f32[128,2,128]{2,1,0:T(2,128)}), f32[128,2,128]{2,1,0:T(2,128)S(1)}, u32[]{:S(2)}, u32[]{:S(2)}) async-start(f32[128,2,128]{2,1,0:T(2,128)} %bitcast.26), calls=%async_computation.2 | async-start | bytes 262144 | tf_op jit(solution)/shard_map/all_to_all | solution.py:101

commit v5 on v4

--- a/solution.py
+++ b/solution.py
@@ -32,9 +32,12 @@
         13.0 / 12.0 * (slope_three - 2.0 * slope_four + slope_five) ** 2
         + 0.25 * (3.0 * slope_three - 4.0 * slope_four + slope_five) ** 2
     )
-    alpha_one = 0.1 / (weno_epsilon + smooth_one) ** 2
-    alpha_two = 0.6 / (weno_epsilon + smooth_two) ** 2
-    alpha_three = 0.3 / (weno_epsilon + smooth_three) ** 2
+    scale_one = weno_epsilon + smooth_one
+    scale_two = weno_epsilon + smooth_two
+    scale_three = weno_epsilon + smooth_three
+    alpha_one = 0.1 * (scale_two * scale_three) ** 2
+    alpha_two = 0.6 * (scale_one * scale_three) ** 2
+    alpha_three = 0.3 * (scale_one * scale_two) ** 2
     weight_sum = alpha_one + alpha_two + alpha_three
     blended = alpha_one * (slope_one / 3.0 - 7.0 * slope_two / 6.0 + 11.0 * slope_three / 6.0)
     blended = blended + alpha_two * (-slope_two / 6.0 + 5.0 * slope_three / 6.0 + slope_four / 3.0)
@@ -47,13 +50,12 @@
 def upwind_derivative(padded, direction_axis, advecting):
     length = padded.shape[direction_axis] - 6
     differences = jnp.diff(padded, axis=direction_axis)
+    rightward = advecting > 0
 
     def window(offset):
         return lax.slice_in_dim(differences, offset, offset + length, axis=direction_axis)
 
-    lower_side = weno_blend(window(0), window(1), window(2), window(3), window(4))
-    upper_side = weno_blend(window(5), window(4), window(3), window(2), window(1))
-    return jnp.where(advecting > 0, lower_side, upper_side)
+    return weno_blend(*[jnp.where(rightward, window(k), window(5 - k)) for k in range(5)])
 
 
 def predicted(center, along_x, along_y, along_z, fraction):
@@ -70,9 +72,8 @@
 
 
 def wall_ghosts(velocity, wall_flags):
-    tangential = 2.0 * wall_flags.astype(jnp.float32) - 1.0
-    normal = -jnp.ones_like(tangential)
-    mirror_signs = jnp.stack([normal, tangential, tangential])
+    component = lax.broadcasted_iota(jnp.int32, (3, *wall_flags.shape), 0)
+    mirror_signs = jnp.where((component == 0) | (wall_flags[None] == 0), -1.0, 1.0)
     lower_ghost = velocity[..., :3][..., ::-1] * mirror_signs[:, 0, :, :, None]
     upper_ghost = velocity[..., -3:][..., ::-1] * mirror_signs[:, 1, :, :, None]
     return jnp.concatenate([lower_ghost, velocity, upper_ghost], axis=-1)
@@ -288,10 +289,55 @@
     out_ref[:, 3, :] = jnp.zeros_like(message)
 
 
+def prepare(place_ref, half_x_ref, half_y_ref, fraction_ref, y_low_ref, y_high_ref, z_low_ref, z_high_ref,
+            beta_x_ref, beta_y_ref, beta_z_ref, rho_ref, scale_ref, weights_ref):
+    row, chip, core = place_ref[0], place_ref[1], place_ref[2]
+
+    def density_of(part):
+        return 1.0 + (heavy_density - 1.0) * part
+
+    cells = [density_of(fraction_ref[y]) for y in range(4)]
+    under, over = density_of(z_low_ref[...]), density_of(z_high_ref[...])
+    lane = lax.broadcasted_iota(jnp.int32, cells[0].shape, 1)
+    layer = lax.broadcasted_iota(jnp.int32, cells[0].shape, 0)
+    first_z = (layer == 0) & (chip == 0) & (core == 0)
+    last_z = (layer == 7) & (chip == weights_ref.shape[1] - 1) & (core == 1)
+    for y, own in enumerate(cells):
+        beta_x_ref[y] = jnp.where(lane == NX - 1, 0.0, 2.0 / (own + rolled(own, -1, 1)))
+        above = jnp.where(layer == 7, over[y : y + 1], rolled(own, -1, 0))
+        below = jnp.where(layer == 0, under[y : y + 1], rolled(own, 1, 0))
+        beta_z_ref[0, y] = jnp.where(last_z, 0.0, 2.0 / (own + above))
+        beta_z_ref[1, y] = jnp.where(first_z, 0.0, 2.0 / (own + below))
+    column = [density_of(y_low_ref[...]), *cells, density_of(y_high_ref[...])]
+    for y in range(5):
+        wall = (lane >= 0) & (row == (0 if y == 0 else 63)) if y in (0, 4) else lane < 0
+        beta_y_ref[y] = jnp.where(wall, 0.0, 2.0 / (column[y + 1] + column[y]))
+    mode = lax.broadcasted_iota(jnp.int32, rho_ref.shape, 0) % 4
+    half_x = jnp.zeros(rho_ref.shape, jnp.float32)
+    for k in range(4):
+        half_x = jnp.where(mode == k, half_x_ref[(row * 2 + core) * 4 + k], half_x)
+    shift = compressibility + half_x + half_y_ref[...]
+    root = jnp.sqrt(shift * (shift + 2.0))
+    rho = 1.0 / (1.0 + shift + root)
+    rho_ref[...] = rho
+    scale_ref[...] = 1.0 / root
+    log_rho = jnp.log(rho)
+    count, size = weights_ref.shape[1], 16
+    period = 2 * size * count
+    norm = 1.0 / (1.0 - jnp.exp(period * log_rho))
+    for block in range(count):
+        behind = size * (chip - block) - size + 1 + jnp.where(block < chip, 0, period)
+        ahead = size * (block - chip) - size + 1 + jnp.where(block > chip, 0, period)
+        low = size * (chip + block) + 1
+        high = period - 2 * size + 1 - size * (chip + block)
+        for side, exponent in enumerate((behind, low, high, ahead)):
+            weights_ref[side, block] = jnp.exp(exponent.astype(jnp.float32) * log_rho) * norm
+
+
 def read_fields(message_ref, table_ref, source_ref, rho_ref, gather_ref, layers_ref):
     tiles = message_ref[...]
     pairs = [jnp.concatenate([tiles[:, c, :], tiles[:, c + 4, :]], axis=1) for c in range(3)]
-    across, along_y, along_z = row_blocks(pairs, source_ref[...])
+    across, along_y, along_z = row_blocks(pairs, source_ref[:, :256])
     after = [*along_y[1:], moved(along_y[0], -1)]
     before = [moved(along_y[3], 1), *along_y[:3]]
     across = [s - 0.5 * (a - b) for s, a, b in zip(across, after, before)]
@@ -334,7 +380,7 @@
         residual_ref[z] = layer
     waves_ref[0] = low
     waves_ref[1] = high
-    send_rims(out_ref, modes, table_ref[...], source_ref[...])
+    send_rims(out_ref, modes, table_ref[...], source_ref[:, 256:])
 
 
 def first_image(message_ref, aligned_ref, table_ref, beta_x_ref, beta_y_ref, beta_z_ref, out_ref, slots_ref, applied_ref):
@@ -353,7 +399,7 @@
 def read_image(message_ref, table_ref, source_ref, rho_ref, gather_ref, layers_ref):
     tiles = message_ref[...]
     pair = jnp.concatenate([tiles[:, 0, :], tiles[:, 2, :]], axis=1)
-    (layers,) = to_modes(row_blocks([pair], source_ref[...]), table_ref[...])
+    (layers,) = to_modes(row_blocks([pair], source_ref[:, :256]), table_ref[...])
     sums = jnp.sum(tiles[:, 1, :] + tiles[:, 3, :], axis=0, keepdims=True)
     upward, downward = moments(layers, rho_ref[...])
     sums = jnp.broadcast_to(sums, upward.shape)
@@ -375,7 +421,7 @@
     layers = [residual_ref[z] - step * layers_ref[z] for z in range(16)]
     modes = solved(layers, waves_ref[0] - step * low, waves_ref[1] - step * high, rho_ref[...], scale_ref[...])
     scalars_ref[...] = lane_row([layers_total(layers, modes[1:-1]), aligned, curvature])
-    send_rims(out_ref, modes, table_ref[...], source_ref[...])
+    send_rims(out_ref, modes, table_ref[...], source_ref[:, 256:])
 
 
 def second_image(message_ref, scalars_ref, applied_ref, table_ref, beta_x_ref, beta_y_ref, beta_z_ref, slots_ref, out_ref):
@@ -441,19 +487,6 @@
     return np.array(lanes, np.int32).reshape(1, -1)
 
 
-def wave_weights(index, rho, count, size):
-    block = jnp.arange(count, dtype=jnp.int32)
-    period = 2 * size * count
-    behind = size * (index - block) - size + 1 + jnp.where(block < index, 0, period)
-    ahead = size * (block - index) - size + 1 + jnp.where(block > index, 0, period)
-    mirrored_low = size * (index + block) + 1
-    mirrored_high = period - 2 * size + 1 - size * (index + block)
-    exponents = jnp.stack([behind, mirrored_low, mirrored_high, ahead]).astype(jnp.float32)
-    log_rho = jnp.log(rho)
-    powers = jnp.exp(exponents[:, :, None, None] * log_rho)
-    return powers / (1.0 - jnp.exp(period * log_rho))
-
-
 def on_device(velocity, fraction, wall_flags):
     rows, cols = (fraction.shape[0], fraction.shape[1])
     rows_devices = lax.axis_size("py")
@@ -464,7 +497,6 @@
     row_index = lax.axis_index("py")
     chip_index = lax.axis_index("px")
     core_index = lax.axis_index("core")
-    col_index = chip_index * cores + core_index
 
     def y_layers(part):
         return part.reshape(9, cols, NX)
@@ -490,62 +522,45 @@
         fraction,
     )
 
-    def density_of(part):
-        return 1.0 + (heavy_density - 1.0) * part
-
-    density = density_of(fraction)
-    inner_x = 2.0 / (density[:, :, 1:] + density[:, :, :-1])
-    beta_x = jnp.concatenate([inner_x, jnp.zeros_like(density[:, :, :1])], axis=2)
-    along_y = jnp.concatenate([density_of(y_low[9:]), density, density_of(y_high[9:])], axis=0)
-    face = row_index * rows + jnp.arange(rows + 1, dtype=jnp.int32)[:, None, None]
-    wall = (face == 0) | (face == total_rows)
-    beta_y = jnp.where(wall, 0.0, 2.0 / (along_y[1:] + along_y[:-1]))
-    over = jnp.concatenate([density[:, 1:], density_of(z_high[9][:, None])], axis=1)
-    under = jnp.concatenate([density_of(z_low[9][:, None]), density[:, :-1]], axis=1)
-    layer = col_index * cols + jnp.arange(cols, dtype=jnp.int32)[None, :, None]
-    plus_z = jnp.where(layer == cols_devices * cols - 1, 0.0, 2.0 / (density + over))
-    minus_z = jnp.where(layer == 0, 0.0, 2.0 / (density + under))
-    betas = (beta_x, beta_y, jnp.stack([plus_z, minus_z]))
-
     peers = rows_devices * cores
     part_x = NX // peers
     plain_x = cosine_table(NX).reshape(peers, part_x, NX).transpose(1, 0, 2).reshape(NX, NX)
+    table_x = jnp.asarray(plain_x, dtype=jnp.float32)
+    (message,) = run(send_fields, [(peers, 4, 128)], provisional, table_x)
+
+    places = jnp.stack([row_index, chip_index, core_index]).astype(jnp.int32)
+
     plain_y = cosine_table(total_rows).T.reshape(rows_devices, rows, total_rows)
     plain_y = plain_y.transpose(1, 0, 2).reshape(total_rows, total_rows)
-    table_x = jnp.asarray(plain_x, dtype=jnp.float32)
     table_y = jnp.asarray(plain_y, dtype=jnp.float32)
     inner = np.arange(256)
-    row_source = jnp.asarray(
-        (inner // 32 % 2 * 128 + inner % 4 * 32 + inner // 64 * 8 + inner // 4 % 8)[None].astype(np.int32)
-    )
-    rim_source = jnp.asarray(rim_slots())
-
-    half_x = lax.dynamic_slice(
-        jnp.asarray(half_eigenvalue(NX), dtype=jnp.float32), ((row_index * cores + core_index) * part_x,), (part_x,)
-    )
-    half_y = jnp.asarray(half_eigenvalue(total_rows), dtype=jnp.float32)
-    shift = compressibility + half_x[None, :, None] + half_y.reshape(2, 1, 128)
-    shift = shift.reshape(8, 128)
-    root = jnp.sqrt(shift * (shift + 2.0))
-    rho = 1.0 / (1.0 + shift + root)
-    scale = 1.0 / root
+    row_source = inner // 32 % 2 * 128 + inner % 4 * 32 + inner // 64 * 8 + inner // 4 % 8
+    sources = jnp.asarray(np.concatenate([row_source[None].astype(np.int32), rim_slots()], axis=1))
+
+    half_x = jnp.asarray(half_eigenvalue(NX), dtype=jnp.float32)
+    half_y = half_eigenvalue(total_rows).reshape(2, 1, 128)
+    half_y = jnp.asarray(np.broadcast_to(half_y, (2, 4, 128)).reshape(8, 128), dtype=jnp.float32)
     size = cols * cores
-    weights = wave_weights(chip_index, rho, chips, size)
-    place = chip_index.astype(jnp.int32).reshape(1)
+    *betas, rho, scale, weights = run(
+        prepare,
+        [(rows, cols, NX), (rows + 1, cols, NX), (2, rows, cols, NX), (8, 128), (8, 128), (4, chips, 8, 128)],
+        places, half_x, half_y, fraction, y_low[9], y_high[9], z_low[9], z_high[9],
+    )
+    place = places[1:2]
 
     across = ("py", "core")
     layers_shape = (size, 8, 128)
     rims_shape = (rows_devices, 4, 128)
-    (message,) = run(send_fields, [(peers, 4, 128)], provisional, table_x)
-    message = exchange(message, across).reshape(rows_devices, 8, 128)
+    message = exchange(message, across)
+    message = message.reshape(rows_devices, 8, 128)
     gather, layers = run(
-        read_fields, [(chips, 32, 128), layers_shape], message, table_y, row_source, rho
+        read_fields, [(chips, 32, 128), layers_shape], message, table_y, sources, rho
     )
     gather = exchange(gather, "px")
     message, residual, waves, aligned = run(
         first_solve,
         [rims_shape, layers_shape, (2, 8, 128), (1, 128)],
-        place, gather, layers, rho, scale, weights, table_y, rim_source,
+        place, gather, layers, rho, scale, weights, table_y, sources,
     )
     message = exchange(message.reshape(peers, 2, 128), across)
     message, first, applied = run(
@@ -553,20 +568,20 @@
     )
     message = exchange(message, across).reshape(rows_devices, 4, 128)
     gather, layers = run(
-        read_image, [(chips, 24, 128), layers_shape], message, table_y, row_source, rho
+        read_image, [(chips, 24, 128), layers_shape], message, table_y, sources, rho
     )
     gather = exchange(gather, "px")
     message, scalars = run(
         second_solve,
         [rims_shape, (1, 128)],
-        gather, layers, residual, waves, rho, scale, weights, table_y, rim_source,
+        gather, layers, residual, waves, rho, scale, weights, table_y, sources,
     )
     message = exchange(message.reshape(peers, 2, 128), across)
     second, parts = run(
-        second_image, [(64, NX), (peers, 1, 128)], message, scalars, applied, table_x, *betas
-    )
-    (parts,) = run(add_parts, [(chips, 1, 128)], exchange(parts, across))
-    parts = exchange(parts, "px")
+        second_image, [(64, NX), (rows_devices, 1, 128)], message, scalars, applied, table_x, *betas
+    )
+    (parts,) = run(add_parts, [(cols_devices, 1, 128)], exchange(parts, "py"))
+    parts = exchange(parts, ("px", "core"))
     next_velocity, pressure = run(
         finish,
         [velocity.shape, fraction.shape],

time: 185 us -> 177 us (0.957)
  blocking collectives: 72.2 us -> 107 us
  waiting for transfers between devices: 38.4 us -> 13.8 us
  starting transfers between devices: 50.4 us -> 38.6 us
  other arithmetic: 5.13 us -> 2.62 us
    all_to_all x5 -> x7, blocking collectives: 72.2 us -> 107 us  [exchange(): lax.all_to_all(message, axis, split_axis=0, concat_axis=0, tiled=True)]
    all_to_all x3 -> x1, waiting for transfers between devices: 35.7 us -> 13.8 us  [exchange(): lax.all_to_all(message, axis, split_axis=0, concat_axis=0, tiled=True)]
    all_to_all x3 -> x1, starting transfers between devices: 30.4 us -> 15.3 us  [exchange(): lax.all_to_all(message, axis, split_axis=0, concat_axis=0, tiled=True)]
    ppermute x4, starting transfers between devices: 20 us -> 23.3 us  [shifted_pair(): return (lax.ppermute(tail, axis, up), lax.ppermute(head, axis, down))]
    ppermute x4, waiting for transfers between devices: 2.75 us -> 0.01 us  [shifted_pair(): return (lax.ppermute(tail, axis, up), lax.ppermute(head, axis, down))]
    pallas_call x9 -> x10, Pallas kernels: 11.7 us -> 11.1 us  [run(): pl.pallas_call(kernel, out_shape=[kept(shape, jnp.float32) for shape in o...]
  transfers between devices with their start and end apart: 7 -> 5, of which waited for: 4 -> 1; matrix products, arithmetic and copies ran while one was open for 1% -> 1% of each run, Pallas kernels for 0% -> 0%
where the time goes in v5:
time: 177 us
  blocking collectives  107 us (60%)
  starting transfers between devices  38.6 us (22%)
  waiting for transfers between devices  13.8 us (8%)
  Pallas kernels  11.1 us (6%)
  local copies, waits for them, and re-layouts  2.86 us (2%)
  other arithmetic  2.62 us (1%)
    all_to_all x7, blocking collectives, exchange(): lax.all_to_all(message, axis, split_axis=0, concat_axis=0, tiled=True)  107 us
    ppermute x4, starting transfers between devices, shifted_pair(): return (lax.ppermute(tail, axis, up), lax.ppermute(head, axis, down))  23.3 us
    all_to_all x1, starting transfers between devices, exchange(): lax.all_to_all(message, axis, split_axis=0, concat_axis=0, tiled=True)  15.3 us
    all_to_all x1, waiting for transfers between devices, exchange(): lax.all_to_all(message, axis, split_axis=0, concat_axis=0, tiled=True)  13.8 us
    pallas_call x10, Pallas kernels, run(): pl.pallas_call(kernel, out_shape=[kept(shape, jnp.float32) for shape in o...  11.1 us
  transfers between devices with their start and end apart: 5, of which 1 were waited for; matrix products, arithmetic and copies ran while one was open for 1% of the time, Pallas kernels for 0%

profile of v5, /device:TPU:1, one launch (start us, length us, event | category | flops | bytes accessed | tf_op | source)
XLA Modules:
  0.0 176.8 jit_solution(11274386560664100356)
XLA Ops:
  0.6 1.0 fusion.21
  1.7 1.4 collective-permute-start
  3.2 4.8 %collective-permute-start.1 = (f32[10,8,512]{2,1,0:T(8,128)S(1)}, f32[10,8,512]{2,1,0:T(8,128)S(1)}, u32[]{:S(2)}, u32[]{:S(2)}) collective-permute-start(f32[10,8,512]{2,1,0:T(8,128)S(1)} %pad_maximum_fusion.10), channel_id=1, source_target_pairs={{0,16},{16,32},{32,48},{48,64},{64,80},{80,96},{96,112},{112,128},... | collective-permute-start | bytes 491528 | tf_op jit(solution)/shard_map/ppermute | solution.py:86
  8.1 4.3 %collective-permute-start.3 = (f32[10,4,512]{2,1,0:T(4,128)S(1)}, f32[10,4,512]{2,1,0:T(4,128)S(1)}, u32[]{:S(2)}, u32[]{:S(2)}) collective-permute-start(f32[10,4,512]{2,1,0:T(4,128)S(1)} %pad_maximum_fusion.12), channel_id=1, source_target_pairs={{0,1},{1,2},{2,3},{3,4},{4,5},{5,6},{6,7},{7,8},{8,9},{9,10},{10,1... | collective-permute-start | bytes 245768 | tf_op jit(solution)/shard_map/ppermute | solution.py:86
  12.5 12.8 %collective-permute-start.2 = (f32[10,4,512]{2,1,0:T(4,128)S(1)}, f32[10,4,512]{2,1,0:T(4,128)S(1)}, u32[]{:S(2)}, u32[]{:S(2)}) collective-permute-start(f32[10,4,512]{2,1,0:T(4,128)S(1)} %pad_maximum_fusion.11), channel_id=1, source_target_pairs={{1,0},{2,1},{3,2},{4,3},{5,4},{6,5},{7,6},{8,7},{9,8},{10,9},{11,1... | collective-permute-start | bytes 245768 | tf_op jit(solution)/shard_map/ppermute | solution.py:86
  27.3 1.8 %fusion.6.provisional_ref = f32[3,4,8,512]{3,2,1,0:T(8,128)S(1)} fusion(f32[3,4,8,512]{3,2,1,0:T(8,128)S(1)} %copy-done.6, f32[3,4,3,512]{3,2,1,0:T(4,128)S(1)} %bitcast.64, f32[3,4,3,512]{3,2,1,0:T(4,128)S(1)} %bitcast.66, f32[3,3,8,512]{3,2,1,0:T(8,128)S(1)} %bitcast.62, f32[3,3,8,512]{3,2,1,0:T(8,128)S(1)} %bitcast.60, ...), kind=kLoop, calls=%fused_computation.16 | loop fusion | flops 11943936 | bytes 4688128 | tf_op jit(solution)/shard_map/add | solution.py:71
  29.1 2.0 %shard_map.95 = f32[128,4,128]{2,1,0:T(4,128)} custom-call(f32[3,4,8,512]{3,2,1,0:T(8,128)S(1)} %fusion.6.provisional_ref, f32[512,512]{1,0:T(8,128)S(1)} %copy-done), custom_call_target="tpu_custom_call" | custom-call | tf_op jit(solution)/shard_map/pallas_call | solution.py:463
  31.0 15.3 %all-to-all-start = ((f32[128,4,128]{2,1,0:T(4,128)}), f32[128,4,128]{2,1,0:T(4,128)S(1)}, u32[]{:S(2)}, u32[]{:S(2)}) async-start(f32[128,4,128]{2,1,0:T(4,128)} %shard_map.95), calls=%async_computation | async-start | bytes 524288 | tf_op jit(solution)/shard_map/all_to_all | solution.py:102
  47.1 0.7 shard_map.96
  47.8 13.8 %all-to-all-done = f32[128,4,128]{2,1,0:T(4,128)S(1)} async-done(((f32[128,4,128]{2,1,0:T(4,128)}), f32[128,4,128]{2,1,0:T(4,128)S(1)}, u32[]{:S(2)}, u32[]{:S(2)}) %all-to-all-start) | async-done | bytes 262176 | tf_op jit(solution)/shard_map/all_to_all | solution.py:102
  61.6 1.0 shard_map.97
  62.6 14.5 %all_to_all.40.gather_ref = f32[8,32,128]{2,1,0:T(8,128)S(1)} all-to-all(f32[8,32,128]{2,1,0:T(8,128)S(1)} %get-tuple-element.24), channel_id=1, replica_groups=mesh['py'=64,'px'=8,'core'=2] {'px'}, dimensions={0} | all-to-all | bytes 262144 | tf_op jit(solution)/shard_map/all_to_all | solution.py:102
  77.0 1.1 shard_map.98
  78.1 19.5 %all_to_all.41.message_ref = f32[128,2,128]{2,1,0:T(2,128)S(1)} all-to-all(f32[128,2,128]{2,1,0:T(2,128)S(1)} %bitcast.58), channel_id=1, replica_groups=mesh['py'=64,'px'=8,'core'=2] {'py','core'}, dimensions={0} | all-to-all | bytes 262144 | tf_op jit(solution)/shard_map/all_to_all | solution.py:102
  97.6 2.1 %shard_map.99 = (f32[128,2,128]{2,1,0:T(2,128)S(1)}, f32[64,512]{1,0:T(8,128)S(1)}, f32[32,512]{1,0:T(8,128)S(1)}) custom-call(f32[128,2,128]{2,1,0:T(2,128)S(1)} %all_to_all.41.message_ref, f32[1,128]{1,0:T(1,128)S(1)} %get-tuple-element.29.aligned_ref, f32[512,512]{1,0:T(8,128)S(1)} %copy-done, f32[4,8,512]{2,1,0:T(8,128)S(1)} %get-tuple-element.30.beta_x_ref, ...), custom_call_target="tpu_custom_call" | custom-call | tf_op jit(solution)/shard_map/pallas_call | solution.py:463
  99.8 17.9 %all_to_all.42 = f32[128,2,128]{2,1,0:T(2,128)S(1)} all-to-all(f32[128,2,128]{2,1,0:T(2,128)S(1)} %get-tuple-element.33), channel_id=1, replica_groups=mesh['py'=64,'px'=8,'core'=2] {'py','core'}, dimensions={0} | all-to-all | bytes 262144 | tf_op jit(solution)/shard_map/all_to_all | solution.py:102
  117.7 0.7 shard_map.100
  118.4 9.9 %all_to_all.43.gather_ref = f32[8,24,128]{2,1,0:T(8,128)S(1)} all-to-all(f32[8,24,128]{2,1,0:T(8,128)S(1)} %get-tuple-element.34), channel_id=1, replica_groups=mesh['py'=64,'px'=8,'core'=2] {'px'}, dimensions={0} | all-to-all | bytes 196608 | tf_op jit(solution)/shard_map/all_to_all | solution.py:102
  128.3 1.2 shard_map.101
  129.5 19.1 %all_to_all.44.message_ref = f32[128,2,128]{2,1,0:T(2,128)S(1)} all-to-all(f32[128,2,128]{2,1,0:T(2,128)S(1)} %bitcast.57), channel_id=1, replica_groups=mesh['py'=64,'px'=8,'core'=2] {'py','core'}, dimensions={0} | all-to-all | bytes 262144 | tf_op jit(solution)/shard_map/all_to_all | solution.py:102
  148.6 1.1 shard_map.102
  149.7 14.7 %all_to_all.45.parts_ref = f32[64,1,128]{2,1,0:T(1,128)S(1)} all-to-all(f32[64,1,128]{2,1,0:T(1,128)S(1)} %get-tuple-element.41), channel_id=1, replica_groups=mesh['py'=64,'px'=8,'core'=2] {'py'}, dimensions={0} | all-to-all | bytes 65536 | tf_op jit(solution)/shard_map/all_to_all | solution.py:102
  164.4 11.2 %all_to_all.46.parts_ref = f32[16,1,128]{2,1,0:T(1,128)S(1)} all-to-all(f32[16,1,128]{2,1,0:T(1,128)S(1)} %shard_map.103), channel_id=1, replica_groups=mesh['py'=64,'px'=8,'core'=2] {'px','core'}, dimensions={0} | all-to-all | bytes 16384 | tf_op jit(solution)/shard_map/all_to_all | solution.py:102
  175.6 1.1 shard_map.104
  (60 shorter events, 2.7 us)
Async XLA Ops:
  0.6 1.1 copy-start.2
  1.7 6.2 %copy-start.6 = (f32[3,4,8,512]{3,2,1,0:T(8,128)S(1)}, f32[3,4,8,512]{3,2,1,0:T(8,128)}, u32[]{:S(2)}) copy-start(f32[3,4,8,512]{3,2,1,0:T(8,128)} %param.8) | copy-start | bytes 589828
  1.7 25.4 %collective-permute-start = (f32[10,8,512]{2,1,0:T(8,128)S(1)}, f32[10,8,512]{2,1,0:T(8,128)S(1)}, u32[]{:S(2)}, u32[]{:S(2)}) collective-permute-start(f32[10,8,512]{2,1,0:T(8,128)S(1)} %pad_maximum_fusion.9), channel_id=1, source_target_pairs={{16,0},{32,16},{48,32},{64,48},{80,64},{96,80},{112,96},{128,112},... | collective-permute-start | bytes 491528 | tf_op jit(solution)/shard_map/ppermute | solution.py:86
  3.2 23.9 %collective-permute-start.1 = (f32[10,8,512]{2,1,0:T(8,128)S(1)}, f32[10,8,512]{2,1,0:T(8,128)S(1)}, u32[]{:S(2)}, u32[]{:S(2)}) collective-permute-start(f32[10,8,512]{2,1,0:T(8,128)S(1)} %pad_maximum_fusion.10), channel_id=1, source_target_pairs={{0,16},{16,32},{32,48},{48,64},{64,80},{80,96},{96,112},{112,128},... | collective-permute-start | bytes 491528 | tf_op jit(solution)/shard_map/ppermute | solution.py:86
  8.1 18.7 %collective-permute-start.3 = (f32[10,4,512]{2,1,0:T(4,128)S(1)}, f32[10,4,512]{2,1,0:T(4,128)S(1)}, u32[]{:S(2)}, u32[]{:S(2)}) collective-permute-start(f32[10,4,512]{2,1,0:T(4,128)S(1)} %pad_maximum_fusion.12), channel_id=1, source_target_pairs={{0,1},{1,2},{2,3},{3,4},{4,5},{5,6},{6,7},{7,8},{8,9},{9,10},{10,1... | collective-permute-start | bytes 245768 | tf_op jit(solution)/shard_map/ppermute | solution.py:86
  12.5 14.4 %collective-permute-start.2 = (f32[10,4,512]{2,1,0:T(4,128)S(1)}, f32[10,4,512]{2,1,0:T(4,128)S(1)}, u32[]{:S(2)}, u32[]{:S(2)}) collective-permute-start(f32[10,4,512]{2,1,0:T(4,128)S(1)} %pad_maximum_fusion.11), channel_id=1, source_target_pairs={{1,0},{2,1},{3,2},{4,3},{5,4},{6,5},{7,6},{8,7},{9,8},{10,9},{11,1... | collective-permute-start | bytes 245768 | tf_op jit(solution)/shard_map/ppermute | solution.py:86
  25.6 0.7 copy-start.7
  27.2 1.8 %copy-start = (f32[512,512]{1,0:T(8,128)S(1)}, f32[512,512]{1,0:T(8,128)}, u32[]{:S(2)}) copy-start(f32[512,512]{1,0:T(8,128)} %constant.105.clone.table_ref) | copy-start | bytes 3145732
  31.0 30.6 %copy-start.1 = (f32[256,256]{1,0:T(8,128)S(1)}, f32[256,256]{1,0:T(8,128)}, u32[]{:S(2)}) copy-start(f32[256,256]{1,0:T(8,128)} %constant.106.clone.table_ref) | copy-start | bytes 786436
  31.0 30.6 %all-to-all-start = ((f32[128,4,128]{2,1,0:T(4,128)}), f32[128,4,128]{2,1,0:T(4,128)S(1)}, u32[]{:S(2)}, u32[]{:S(2)}) async-start(f32[128,4,128]{2,1,0:T(4,128)} %shard_map.95), calls=%async_computation | async-start | bytes 524288 | tf_op jit(solution)/shard_map/all_to_all | solution.py:102
  46.4 0.7 copy-start.4
  46.4 0.7 copy-start.5
  47.8 13.8 %copy-start.3 = (s32[1,768]{1,0:T(1,128)S(1)}, s32[1,768]{1,0:T(1,128)}, u32[]{:S(2)}) copy-start(s32[1,768]{1,0:T(1,128)} %constant.107.clone.source_ref) | copy-start | bytes 9220

commit v6 on v5

--- a/solution.py
+++ b/solution.py
@@ -79,11 +79,18 @@
     return jnp.concatenate([lower_ghost, velocity, upper_ghost], axis=-1)
 
 
+def swapped(values, axis, pairs):
+    return lax.ppermute(values, axis, pairs)
+
+
 def shifted_pair(head, tail, axis):
     count = lax.axis_size(axis)
-    up = [(i, i + 1) for i in range(count - 1)]
-    down = [(i + 1, i) for i in range(count - 1)]
-    return lax.ppermute(tail, axis, up), lax.ppermute(head, axis, down)
+    even = (lax.axis_index(axis) & 1) == 0
+    inner = [(i, i + 1) for i in range(0, count, 2)]
+    outer = [(i, i + 1) for i in range(1, count - 1, 2)]
+    one = swapped(jnp.where(even, tail, head), axis, inner + [(j, i) for i, j in inner])
+    two = swapped(jnp.where(even, head, tail), axis, outer + [(j, i) for i, j in outer])
+    return jnp.where(even, two, one), jnp.where(even, one, two)
 
 
 def cosine_table(length):
@@ -146,33 +153,19 @@
         ref[:, t, :] = values[:, 128 * t : 128 * t + 128]
 
 
-def to_messages(rows, table_x):
+def to_message(rows, table_x):
     spectral = dot_nt(table_x, rows)
     devices = spectral.shape[0] // 4
     blocks = [spectral[devices * k : devices * k + devices] for k in range(4)]
+    return jnp.concatenate(blocks, axis=1)
+
+
+def to_layers(blocks, table_y):
+    modes = dot(jnp.concatenate(blocks, axis=0).T, table_y)
     return [
-        jnp.concatenate([block[:, 32 * c : 32 * c + 32] for block in blocks], axis=1)
-        for c in range(rows.shape[0] // 32)
+        jnp.concatenate([modes[4 * r : 4 * r + 4, :128], modes[4 * r : 4 * r + 4, 128:]], axis=0)
+        for r in range(modes.shape[0] // 4)
     ]
-
-
-def row_blocks(messages, source):
-    ordered = picked(jnp.concatenate(messages, axis=0), source)
-    devices = messages[0].shape[0]
-    return [
-        [ordered[devices * c : devices * c + devices, 64 * y : 64 * y + 64] for y in range(4)]
-        for c in range(len(messages))
-    ]
-
-
-def to_modes(fields, table_y):
-    cells = [jnp.concatenate(blocks, axis=0).T for blocks in fields]
-    modes = dot(jnp.concatenate(cells, axis=0), table_y)
-    layers = [
-        jnp.concatenate([modes[4 * r : 4 * r + 4, :128], modes[4 * r : 4 * r + 4, 128:]], axis=0)
-        for r in range(16 * len(fields))
-    ]
-    return [layers[16 * c : 16 * c + 16] for c in range(len(fields))]
 
 
 def from_layers(layers):
@@ -282,11 +275,20 @@
     lane = lax.broadcasted_iota(jnp.int32, normal.shape, 1)
     after = jnp.where(lane == NX - 1, -normal, rolled(normal, -1, 1))
     before = jnp.where(lane == 0, -normal, rolled(normal, 1, 1))
-    rows = [-0.5 * (after - before)]
-    rows += [provisional_ref[c].reshape(32, NX) for c in (1, 2)]
-    for c, message in enumerate(to_messages(jnp.concatenate(rows, axis=0), table_ref[...])):
-        out_ref[:, c, :] = message
-    out_ref[:, 3, :] = jnp.zeros_like(message)
+    across = -0.5 * (after - before)
+    along_y = [provisional_ref[1, y] for y in range(4)]
+    along_z = [provisional_ref[2, y] for y in range(4)]
+    zero = jnp.zeros_like(along_y[0])
+    layer = lax.broadcasted_iota(jnp.int32, zero.shape, 0)
+    rows = []
+    for y in range(4):
+        rise = (along_y[y + 1] if y < 3 else zero) - (along_y[y - 1] if y > 0 else zero)
+        above = jnp.where(layer == 7, 0.0, rolled(along_z[y], -1, 0))
+        below = jnp.where(layer == 0, 0.0, rolled(along_z[y], 1, 0))
+        rows.append(across[8 * y : 8 * y + 8] - 0.5 * rise - 0.5 * (above - below))
+    rows += [along_y[0], along_y[3]]
+    rows += [part[:1] for part in along_z] + [part[7:] for part in along_z] + [zero]
+    into_tiles(out_ref, to_message(jnp.concatenate(rows, axis=0), table_ref[...]))
 
 
 def prepare(place_ref, half_x_ref, half_y_ref, fraction_ref, y_low_ref, y_high_ref, z_low_ref, z_high_ref,
@@ -336,22 +338,20 @@
 
 def read_fields(message_ref, table_ref, source_ref, rho_ref, gather_ref, layers_ref):
     tiles = message_ref[...]
-    pairs = [jnp.concatenate([tiles[:, c, :], tiles[:, c + 4, :]], axis=1) for c in range(3)]
-    across, along_y, along_z = row_blocks(pairs, source_ref[:, :256])
-    after = [*along_y[1:], moved(along_y[0], -1)]
-    before = [moved(along_y[3], 1), *along_y[:3]]
-    across = [s - 0.5 * (a - b) for s, a, b in zip(across, after, before)]
-    joined, third = to_modes([across, along_z], table_ref[...])
-    zero = jnp.zeros_like(third[0])
-    above = [*third[1:], zero]
-    below = [zero, *third[:-1]]
-    layers = [j - 0.5 * (a - b) for j, a, b in zip(joined, above, below)]
+    ordered = picked(from_tiles(tiles, 4), source_ref[:, 768:])
+    blocks = [ordered[:, 128 * y : 128 * y + 128] for y in range(4)]
+    blocks[0] = blocks[0] + 0.5 * moved(ordered[:, 640:768], 1)
+    blocks[3] = blocks[3] - 0.5 * moved(ordered[:, 512:640], -1)
+    layers = to_layers([block[:, :80] for block in blocks], table_ref[...])
+    layers, edges = layers[:16], layers[16:]
+    layers[7] = layers[7] - 0.5 * edges[2]
+    layers[8] = layers[8] + 0.5 * edges[1]
     upward, downward = moments(layers, rho_ref[...])
     for device in range(gather_ref.shape[0]):
         gather_ref[device, 0:8] = upward
         gather_ref[device, 8:16] = downward
-        gather_ref[device, 16:24] = third[0]
-        gather_ref[device, 24:32] = third[-1]
+        gather_ref[device, 16:24] = edges[0]
+        gather_ref[device, 24:32] = edges[3]
     for z, layer in enumerate(layers):
         layers_ref[z] = layer
 
@@ -380,7 +380,7 @@
         residual_ref[z] = layer
     waves_ref[0] = low
     waves_ref[1] = high
-    send_rims(out_ref, modes, table_ref[...], source_ref[:, 256:])
+    send_rims(out_ref, modes, table_ref[...], source_ref[:, 256:768])
 
 
 def first_image(message_ref, aligned_ref, table_ref, beta_x_ref, beta_y_ref, beta_z_ref, out_ref, slots_ref, applied_ref):
@@ -389,7 +389,7 @@
     applied = applied_rows(slots, beta_x_ref[...], beta_y_ref[...], beta_z_ref[...])
     slots_ref[...] = slots
     applied_ref[...] = applied
-    (message,) = to_messages(applied, table)
+    message = to_message(applied, table)
     curvature = total(slots[8:40] * applied)
     out_ref[:, 0, :] = message
     row = lane_row([aligned_ref[...][:, :1], curvature])
@@ -399,7 +399,8 @@
 def read_image(message_ref, table_ref, source_ref, rho_ref, gather_ref, layers_ref):
     tiles = message_ref[...]
     pair = jnp.concatenate([tiles[:, 0, :], tiles[:, 2, :]], axis=1)
-    (layers,) = to_modes(row_blocks([pair], source_ref[:, :256]), table_ref[...])
+    ordered = picked(pair, source_ref[:, :256])
+    layers = to_layers([ordered[:, 64 * y : 64 * y + 64] for y in range(4)], table_ref[...])
     sums = jnp.sum(tiles[:, 1, :] + tiles[:, 3, :], axis=0, keepdims=True)
     upward, downward = moments(layers, rho_ref[...])
     sums = jnp.broadcast_to(sums, upward.shape)
@@ -421,7 +422,7 @@
     layers = [residual_ref[z] - step * layers_ref[z] for z in range(16)]
     modes = solved(layers, waves_ref[0] - step * low, waves_ref[1] - step * high, rho_ref[...], scale_ref[...])
     scalars_ref[...] = lane_row([layers_total(layers, modes[1:-1]), aligned, curvature])
-    send_rims(out_ref, modes, table_ref[...], source_ref[:, 256:])
+    send_rims(out_ref, modes, table_ref[...], source_ref[:, 256:768])
 
 
 def second_image(message_ref, scalars_ref, applied_ref, table_ref, beta_x_ref, beta_y_ref, beta_z_ref, slots_ref, out_ref):
@@ -487,6 +488,21 @@
     return np.array(lanes, np.int32).reshape(1, -1)
 
 
+def field_slots():
+    def lane(core, k, row):
+        return core * 256 + k * 64 + row
+
+    lanes = []
+    for y in range(4):
+        lanes += [lane(z // 8, k, 8 * y + z % 8) for z in range(16) for k in range(4)]
+        for core, row in ((0, 48), (0, 52), (1, 48), (1, 52)):
+            lanes += [lane(core, k, row + y) for k in range(4)]
+        lanes += [-1] * 48
+    for row in (32, 40):
+        lanes += [lane(z // 8, k, row + z % 8) for z in range(16) for k in range(4)] + [-1] * 64
+    return np.array(lanes, np.int32).reshape(1, -1)
+
+
 def on_device(velocity, fraction, wall_flags):
     rows, cols = (fraction.shape[0], fraction.shape[1])
     rows_devices = lax.axis_size("py")
@@ -526,7 +542,7 @@
     part_x = NX // peers
     plain_x = cosine_table(NX).reshape(peers, part_x, NX).transpose(1, 0, 2).reshape(NX, NX)
     table_x = jnp.asarray(plain_x, dtype=jnp.float32)
-    (message,) = run(send_fields, [(peers, 4, 128)], provisional, table_x)
+    (message,) = run(send_fields, [(peers, 2, 128)], provisional, table_x)
 
     places = jnp.stack([row_index, chip_index, core_index]).astype(jnp.int32)
 
@@ -535,7 +551,7 @@
     table_y = jnp.asarray(plain_y, dtype=jnp.float32)
     inner = np.arange(256)
     row_source = inner // 32 % 2 * 128 + inner % 4 * 32 + inner // 64 * 8 + inner // 4 % 8
-    sources = jnp.asarray(np.concatenate([row_source[None].astype(np.int32), rim_slots()], axis=1))
+    sources = jnp.asarray(np.concatenate([row_source[None].astype(np.int32), rim_slots(), field_slots()], axis=1))
 
     half_x = jnp.asarray(half_eigenvalue(NX), dtype=jnp.float32)
     half_y = half_eigenvalue(total_rows).reshape(2, 1, 128)
@@ -552,7 +568,7 @@
     layers_shape = (size, 8, 128)
     rims_shape = (rows_devices, 4, 128)
     message = exchange(message, across)
-    message = message.reshape(rows_devices, 8, 128)
+    message = message.reshape(rows_devices, 4, 128)
     gather, layers = run(
         read_fields, [(chips, 32, 128), layers_shape], message, table_y, sources, rho
     )

time: 177 us -> 174 us (0.983)
  starting transfers between devices: 38.6 us -> 34.6 us
    ppermute x4, starting transfers between devices: 23.3 us -> 20.7 us  [swapped(): return lax.ppermute(values, axis, pairs)]
    all_to_all x1, waiting for transfers between devices: 13.8 us -> 11.3 us  [exchange(): lax.all_to_all(message, axis, split_axis=0, concat_axis=0, tiled=True)]
    ppermute x4, waiting for transfers between devices: 0.01 us -> 2.34 us  [swapped(): return lax.ppermute(values, axis, pairs)]
  transfers between devices with their start and end apart: 5 -> 5, of which waited for: 1 -> 2; matrix products, arithmetic and copies ran while one was open for 1% -> 1% of each run, Pallas kernels for 0% -> 0%
where the time goes in v6:
time: 174 us; the launch traced here: 173 us
  blocking collectives  107 us (61%)
  starting transfers between devices  34.6 us (20%)
  waiting for transfers between devices  13.6 us (8%)
  Pallas kernels  11 us (6%)
  local copies, waits for them, and re-layouts  2.86 us (2%)
  other arithmetic  2.66 us (2%)
    all_to_all x7, blocking collectives, exchange(): lax.all_to_all(message, axis, split_axis=0, concat_axis=0, tiled=True)  107 us
    ppermute x4, starting transfers between devices, swapped(): return lax.ppermute(values, axis, pairs)  20.7 us
    all_to_all x1, starting transfers between devices, exchange(): lax.all_to_all(message, axis, split_axis=0, concat_axis=0, tiled=True)  13.9 us
    all_to_all x1, waiting for transfers between devices, exchange(): lax.all_to_all(message, axis, split_axis=0, concat_axis=0, tiled=True)  11.3 us
    pallas_call x10, Pallas kernels, run(): pl.pallas_call(kernel, out_shape=[kept(shape, jnp.float32) for shape in o...  11 us
  transfers between devices with their start and end apart: 5, of which 2 were waited for; matrix products, arithmetic and copies ran while one was open for 1% of the time, Pallas kernels for 0%

profile of v6, /device:TPU:1, one launch (start us, length us, event | category | flops | bytes accessed | tf_op | source)
XLA Modules:
  0.0 173.2 jit_solution(2453189886985907268)
XLA Ops:
  0.6 1.0 fusion.25
  1.8 4.3 %collective-permute-start = (f32[10,8,512]{2,1,0:T(8,128)S(1)}, f32[10,8,512]{2,1,0:T(8,128)S(1)}, u32[]{:S(2)}, u32[]{:S(2)}) collective-permute-start(f32[10,8,512]{2,1,0:T(8,128)S(1)} %get-tuple-element.46), channel_id=1, source_target_pairs={{0,16},{32,48},{64,80},{96,112},{128,144},{160,176},{192,208},{224... | collective-permute-start | bytes 491528 | tf_op jit(solution)/shard_map/ppermute | solution.py:83
  6.9 13.8 %collective-permute-start.2 = (f32[10,4,512]{2,1,0:T(4,128)S(1)}, f32[10,4,512]{2,1,0:T(4,128)S(1)}, u32[]{:S(2)}, u32[]{:S(2)}) collective-permute-start(f32[10,4,512]{2,1,0:T(4,128)S(1)} %get-tuple-element.62), channel_id=1, source_target_pairs={{0,1},{2,3},{4,5},{6,7},{8,9},{10,11},{12,13},{14,15},{1,0},{3,2},... | collective-permute-start | bytes 245768 | tf_op jit(solution)/shard_map/ppermute | solution.py:83
  20.8 1.9 %collective-permute-start.3 = (f32[10,4,512]{2,1,0:T(4,128)S(1)}, f32[10,4,512]{2,1,0:T(4,128)S(1)}, u32[]{:S(2)}, u32[]{:S(2)}) collective-permute-start(f32[10,4,512]{2,1,0:T(4,128)S(1)} %get-tuple-element.63), channel_id=1, source_target_pairs={{1,2},{3,4},{5,6},{7,8},{9,10},{11,12},{13,14},{2,1},{4,3},{6,5},{... | collective-permute-start | bytes 245768 | tf_op jit(solution)/shard_map/ppermute | solution.py:83
  24.2 2.3 %collective-permute-done.3 = f32[10,4,512]{2,1,0:T(4,128)S(1)} collective-permute-done((f32[10,4,512]{2,1,0:T(4,128)S(1)}, f32[10,4,512]{2,1,0:T(4,128)S(1)}, u32[]{:S(2)}, u32[]{:S(2)}) %collective-permute-start.3) | collective-permute-done | bytes 81952 | tf_op jit(solution)/shard_map/ppermute | solution.py:83
  27.0 1.8 %fusion.6.provisional_ref = f32[3,4,8,512]{3,2,1,0:T(8,128)S(1)} fusion(f32[3,4,8,512]{3,2,1,0:T(8,128)S(1)} %copy-done.6, f32[3,4,3,512]{3,2,1,0:T(4,128)S(1)} %bitcast.66, f32[3,4,3,512]{3,2,1,0:T(4,128)S(1)} %bitcast.68, f32[3,3,8,512]{3,2,1,0:T(8,128)S(1)} %bitcast.64, f32[3,3,8,512]{3,2,1,0:T(8,128)S(1)} %bitcast.62, ...), kind=kLoop, calls=%fused_computation.16 | loop fusion | flops 11943936 | bytes 4688128 | tf_op jit(solution)/shard_map/add | solution.py:71
  28.8 1.8 %shard_map.95 = f32[128,2,128]{2,1,0:T(2,128)} custom-call(f32[3,4,8,512]{3,2,1,0:T(8,128)S(1)} %fusion.6.provisional_ref, f32[512,512]{1,0:T(8,128)S(1)} %copy-done), custom_call_target="tpu_custom_call" | custom-call | tf_op jit(solution)/shard_map/pallas_call | solution.py:464
  30.6 13.9 %all-to-all-start = ((f32[128,2,128]{2,1,0:T(2,128)}), f32[128,2,128]{2,1,0:T(2,128)S(1)}, u32[]{:S(2)}, u32[]{:S(2)}) async-start(f32[128,2,128]{2,1,0:T(2,128)} %shard_map.95), calls=%async_computation | async-start | bytes 262144 | tf_op jit(solution)/shard_map/all_to_all | solution.py:109
  45.3 0.7 shard_map.96
  46.0 11.3 %all-to-all-done = f32[128,2,128]{2,1,0:T(2,128)S(1)} async-done(((f32[128,2,128]{2,1,0:T(2,128)}), f32[128,2,128]{2,1,0:T(2,128)S(1)}, u32[]{:S(2)}, u32[]{:S(2)}) %all-to-all-start) | async-done | bytes 131104 | tf_op jit(solution)/shard_map/all_to_all | solution.py:109
  57.3 1.1 shard_map.97
  58.4 15.2 %all_to_all.40.gather_ref = f32[8,32,128]{2,1,0:T(8,128)S(1)} all-to-all(f32[8,32,128]{2,1,0:T(8,128)S(1)} %get-tuple-element.24), channel_id=1, replica_groups=mesh['py'=64,'px'=8,'core'=2] {'px'}, dimensions={0} | all-to-all | bytes 262144 | tf_op jit(solution)/shard_map/all_to_all | solution.py:109
  73.6 1.1 shard_map.98
  74.7 19.5 %all_to_all.41.message_ref = f32[128,2,128]{2,1,0:T(2,128)S(1)} all-to-all(f32[128,2,128]{2,1,0:T(2,128)S(1)} %bitcast.60), channel_id=1, replica_groups=mesh['py'=64,'px'=8,'core'=2] {'py','core'}, dimensions={0} | all-to-all | bytes 262144 | tf_op jit(solution)/shard_map/all_to_all | solution.py:109
  94.2 2.1 %shard_map.99 = (f32[128,2,128]{2,1,0:T(2,128)S(1)}, f32[64,512]{1,0:T(8,128)S(1)}, f32[32,512]{1,0:T(8,128)S(1)}) custom-call(f32[128,2,128]{2,1,0:T(2,128)S(1)} %all_to_all.41.message_ref, f32[1,128]{1,0:T(1,128)S(1)} %get-tuple-element.29.aligned_ref, f32[512,512]{1,0:T(8,128)S(1)} %copy-done, f32[4,8,512]{2,1,0:T(8,128)S(1)} %get-tuple-element.30.beta_x_ref, ...), custom_call_target="tpu_custom_call" | custom-call | tf_op jit(solution)/shard_map/pallas_call | solution.py:464
  96.3 17.7 %all_to_all.42 = f32[128,2,128]{2,1,0:T(2,128)S(1)} all-to-all(f32[128,2,128]{2,1,0:T(2,128)S(1)} %get-tuple-element.33), channel_id=1, replica_groups=mesh['py'=64,'px'=8,'core'=2] {'py','core'}, dimensions={0} | all-to-all | bytes 262144 | tf_op jit(solution)/shard_map/all_to_all | solution.py:109
  114.1 0.7 shard_map.100
  114.8 9.9 %all_to_all.43.gather_ref = f32[8,24,128]{2,1,0:T(8,128)S(1)} all-to-all(f32[8,24,128]{2,1,0:T(8,128)S(1)} %get-tuple-element.34), channel_id=1, replica_groups=mesh['py'=64,'px'=8,'core'=2] {'px'}, dimensions={0} | all-to-all | bytes 196608 | tf_op jit(solution)/shard_map/all_to_all | solution.py:109
  124.7 1.2 shard_map.101
  125.9 19.1 %all_to_all.44.message_ref = f32[128,2,128]{2,1,0:T(2,128)S(1)} all-to-all(f32[128,2,128]{2,1,0:T(2,128)S(1)} %bitcast.59), channel_id=1, replica_groups=mesh['py'=64,'px'=8,'core'=2] {'py','core'}, dimensions={0} | all-to-all | bytes 262144 | tf_op jit(solution)/shard_map/all_to_all | solution.py:109
  145.0 1.1 shard_map.102
  146.1 14.7 %all_to_all.45.parts_ref = f32[64,1,128]{2,1,0:T(1,128)S(1)} all-to-all(f32[64,1,128]{2,1,0:T(1,128)S(1)} %get-tuple-element.41), channel_id=1, replica_groups=mesh['py'=64,'px'=8,'core'=2] {'py'}, dimensions={0} | all-to-all | bytes 65536 | tf_op jit(solution)/shard_map/all_to_all | solution.py:109
  160.9 11.2 %all_to_all.46.parts_ref = f32[16,1,128]{2,1,0:T(1,128)S(1)} all-to-all(f32[16,1,128]{2,1,0:T(1,128)S(1)} %shard_map.103), channel_id=1, replica_groups=mesh['py'=64,'px'=8,'core'=2] {'px','core'}, dimensions={0} | all-to-all | bytes 16384 | tf_op jit(solution)/shard_map/all_to_all | solution.py:109
  172.0 1.1 shard_map.104
  (58 shorter events, 3.5 us)
Async XLA Ops:
  0.6 1.1 copy-start.2
  1.7 5.0 %copy-start.6 = (f32[3,4,8,512]{3,2,1,0:T(8,128)S(1)}, f32[3,4,8,512]{3,2,1,0:T(8,128)}, u32[]{:S(2)}) copy-start(f32[3,4,8,512]{3,2,1,0:T(8,128)} %param.8) | copy-start | bytes 589828
  1.8 25.0 %collective-permute-start = (f32[10,8,512]{2,1,0:T(8,128)S(1)}, f32[10,8,512]{2,1,0:T(8,128)S(1)}, u32[]{:S(2)}, u32[]{:S(2)}) collective-permute-start(f32[10,8,512]{2,1,0:T(8,128)S(1)} %get-tuple-element.46), channel_id=1, source_target_pairs={{0,16},{32,48},{64,80},{96,112},{128,144},{160,176},{192,208},{224... | collective-permute-start | bytes 491528 | tf_op jit(solution)/shard_map/ppermute | solution.py:83
  6.0 20.8 %collective-permute-start.1 = (f32[10,8,512]{2,1,0:T(8,128)S(1)}, f32[10,8,512]{2,1,0:T(8,128)S(1)}, u32[]{:S(2)}, u32[]{:S(2)}) collective-permute-start(f32[10,8,512]{2,1,0:T(8,128)S(1)} %get-tuple-element.47), channel_id=1, source_target_pairs={{16,32},{48,64},{80,96},{112,128},{144,160},{176,192},{208,224},{2... | collective-permute-start | bytes 491528 | tf_op jit(solution)/shard_map/ppermute | solution.py:83
  6.9 17.2 %collective-permute-start.2 = (f32[10,4,512]{2,1,0:T(4,128)S(1)}, f32[10,4,512]{2,1,0:T(4,128)S(1)}, u32[]{:S(2)}, u32[]{:S(2)}) collective-permute-start(f32[10,4,512]{2,1,0:T(4,128)S(1)} %get-tuple-element.62), channel_id=1, source_target_pairs={{0,1},{2,3},{4,5},{6,7},{8,9},{10,11},{12,13},{14,15},{1,0},{3,2},... | collective-permute-start | bytes 245768 | tf_op jit(solution)/shard_map/ppermute | solution.py:83
  20.8 5.8 %collective-permute-start.3 = (f32[10,4,512]{2,1,0:T(4,128)S(1)}, f32[10,4,512]{2,1,0:T(4,128)S(1)}, u32[]{:S(2)}, u32[]{:S(2)}) collective-permute-start(f32[10,4,512]{2,1,0:T(4,128)S(1)} %get-tuple-element.63), channel_id=1, source_target_pairs={{1,2},{3,4},{5,6},{7,8},{9,10},{11,12},{13,14},{2,1},{4,3},{6,5},{... | collective-permute-start | bytes 245768 | tf_op jit(solution)/shard_map/ppermute | solution.py:83
  22.9 0.7 copy-start.7
  27.0 1.8 %copy-start = (f32[512,512]{1,0:T(8,128)S(1)}, f32[512,512]{1,0:T(8,128)}, u32[]{:S(2)}) copy-start(f32[512,512]{1,0:T(8,128)} %constant.110.clone.table_ref) | copy-start | bytes 3145732
  30.6 26.7 %copy-start.1 = (f32[256,256]{1,0:T(8,128)S(1)}, f32[256,256]{1,0:T(8,128)}, u32[]{:S(2)}) copy-start(f32[256,256]{1,0:T(8,128)} %constant.111.clone.table_ref) | copy-start | bytes 786436
  30.6 26.7 %all-to-all-start = ((f32[128,2,128]{2,1,0:T(2,128)}), f32[128,2,128]{2,1,0:T(2,128)S(1)}, u32[]{:S(2)}, u32[]{:S(2)}) async-start(f32[128,2,128]{2,1,0:T(2,128)} %shard_map.95), calls=%async_computation | async-start | bytes 262144 | tf_op jit(solution)/shard_map/all_to_all | solution.py:109
  44.6 0.7 copy-start.4
  44.6 0.7 copy-start.5
  45.3 12.0 %copy-start.3 = (s32[1,1536]{1,0:T(1,128)S(1)}, s32[1,1536]{1,0:T(1,128)}, u32[]{:S(2)}) copy-start(s32[1,1536]{1,0:T(1,128)} %constant.112.clone.source_ref) | copy-start | bytes 18436

commit v7 on v6

--- a/solution.py
+++ b/solution.py
@@ -16,7 +16,6 @@
 compressibility = 0.001
 mean_inverse = 0.5
 weno_epsilon = 1e-06
-highest = lax.Precision.HIGHEST
 
 
 def weno_blend(slope_one, slope_two, slope_three, slope_four, slope_five):
@@ -88,8 +87,8 @@
     even = (lax.axis_index(axis) & 1) == 0
     inner = [(i, i + 1) for i in range(0, count, 2)]
     outer = [(i, i + 1) for i in range(1, count - 1, 2)]
+    two = swapped(jnp.where(even, head, tail), axis, outer + [(j, i) for i, j in outer])
     one = swapped(jnp.where(even, tail, head), axis, inner + [(j, i) for i, j in inner])
-    two = swapped(jnp.where(even, head, tail), axis, outer + [(j, i) for i, j in outer])
     return jnp.where(even, two, one), jnp.where(even, one, two)
 
 
@@ -109,16 +108,37 @@
     return lax.all_to_all(message, axis, split_axis=0, concat_axis=0, tiled=True)
 
 
-def dot(left, right):
-    return lax.dot_general(
-        left, right, (((1,), (0,)), ((), ())), precision=highest, preferred_element_type=jnp.float32
-    )
-
-
-def dot_nt(left, right):
-    return lax.dot_general(
-        left, right, (((1,), (1,)), ((), ())), precision=highest, preferred_element_type=jnp.float32
-    )
+def pieces_of(values):
+    parts = []
+    for _ in range(3):
+        parts.append(values.astype(jnp.bfloat16))
+        values = values - parts[-1].astype(jnp.float32)
+    return parts
+
+
+def dot(left, table_ref):
+    parts = pieces_of(left)
+    count = left.shape[0]
+    total = None
+    for order in (2, 1, 0):
+        stacked = jnp.concatenate(parts[: 3 - order], axis=0)
+        term = jnp.dot(stacked, table_ref[order], preferred_element_type=jnp.float32)
+        for piece in range(3 - order):
+            block = term[count * piece : count * piece + count]
+            total = block if total is None else total + block
+    return total
+
+
+def dot_nt(table_ref, right):
+    parts = pieces_of(right)
+    total = None
+    for order in (2, 1, 0):
+        for part in parts[: 3 - order]:
+            term = lax.dot_general(
+                table_ref[order], part, (((1,), (1,)), ((), ())), preferred_element_type=jnp.float32
+            )
+            total = term if total is None else total + term
+    return total
 
 
 def rolled(values, shift, axis):
@@ -134,14 +154,10 @@
 def picked(values, source):
     lane = lax.broadcasted_iota(jnp.int32, (values.shape[1], source.shape[1]), 0)
     chosen = jnp.where(lane == source, 1.0, 0.0).astype(jnp.bfloat16)
-    total = None
-    rest = values
-    for _ in range(3):
-        piece = rest.astype(jnp.bfloat16)
-        rest = rest - piece.astype(jnp.float32)
-        term = jnp.dot(piece, chosen, preferred_element_type=jnp.float32)
-        total = term if total is None else total + term
-    return total
+    count = values.shape[0]
+    stacked = jnp.concatenate(pieces_of(values), axis=0)
+    ordered = jnp.dot(stacked, chosen, preferred_element_type=jnp.float32)
+    return ordered[:count] + ordered[count : 2 * count] + ordered[2 * count :]
 
 
 def from_tiles(tiles, count):
@@ -270,7 +286,9 @@
     return row
 
 
-def send_fields(provisional_ref, table_ref, out_ref):
+def send_fields(provisional_ref, table_ref, out_ref, pieces_ref):
+    for order, part in enumerate(pieces_of(table_ref[...])):
+        pieces_ref[order] = part
     normal = provisional_ref[0].reshape(32, NX)
     lane = lax.broadcasted_iota(jnp.int32, normal.shape, 1)
     after = jnp.where(lane == NX - 1, -normal, rolled(normal, -1, 1))
@@ -288,12 +306,14 @@
         rows.append(across[8 * y : 8 * y + 8] - 0.5 * rise - 0.5 * (above - below))
     rows += [along_y[0], along_y[3]]
     rows += [part[:1] for part in along_z] + [part[7:] for part in along_z] + [zero]
-    into_tiles(out_ref, to_message(jnp.concatenate(rows, axis=0), table_ref[...]))
-
-
-def prepare(place_ref, half_x_ref, half_y_ref, fraction_ref, y_low_ref, y_high_ref, z_low_ref, z_high_ref,
-            beta_x_ref, beta_y_ref, beta_z_ref, rho_ref, scale_ref, weights_ref):
+    into_tiles(out_ref, to_message(jnp.concatenate(rows, axis=0), pieces_ref))
+
+
+def prepare(place_ref, half_x_ref, half_y_ref, table_ref, fraction_ref, y_low_ref, y_high_ref, z_low_ref, z_high_ref,
+            beta_x_ref, beta_y_ref, beta_z_ref, rho_ref, scale_ref, weights_ref, pieces_ref):
     row, chip, core = place_ref[0], place_ref[1], place_ref[2]
+    for order, part in enumerate(pieces_of(table_ref[...])):
+        pieces_ref[order] = part
 
     def density_of(part):
         return 1.0 + (heavy_density - 1.0) * part
@@ -342,7 +362,7 @@
     blocks = [ordered[:, 128 * y : 128 * y + 128] for y in range(4)]
     blocks[0] = blocks[0] + 0.5 * moved(ordered[:, 640:768], 1)
     blocks[3] = blocks[3] - 0.5 * moved(ordered[:, 512:640], -1)
-    layers = to_layers([block[:, :80] for block in blocks], table_ref[...])
+    layers = to_layers([block[:, :80] for block in blocks], table_ref)
     layers, edges = layers[:16], layers[16:]
     layers[7] = layers[7] - 0.5 * edges[2]
     layers[8] = layers[8] + 0.5 * edges[1]
@@ -380,11 +400,11 @@
         residual_ref[z] = layer
     waves_ref[0] = low
     waves_ref[1] = high
-    send_rims(out_ref, modes, table_ref[...], source_ref[:, 256:768])
+    send_rims(out_ref, modes, table_ref, source_ref[:, 256:768])
 
 
 def first_image(message_ref, aligned_ref, table_ref, beta_x_ref, beta_y_ref, beta_z_ref, out_ref, slots_ref, applied_ref):
-    table = table_ref[...]
+    table = table_ref
     slots = from_rims(from_tiles(message_ref[...], 2), table)
     applied = applied_rows(slots, beta_x_ref[...], beta_y_ref[...], beta_z_ref[...])
     slots_ref[...] = slots
@@ -400,7 +420,7 @@
     tiles = message_ref[...]
     pair = jnp.concatenate([tiles[:, 0, :], tiles[:, 2, :]], axis=1)
     ordered = picked(pair, source_ref[:, :256])
-    layers = to_layers([ordered[:, 64 * y : 64 * y + 64] for y in range(4)], table_ref[...])
+    layers = to_layers([ordered[:, 64 * y : 64 * y + 64] for y in range(4)], table_ref)
     sums = jnp.sum(tiles[:, 1, :] + tiles[:, 3, :], axis=0, keepdims=True)
     upward, downward = moments(layers, rho_ref[...])
     sums = jnp.broadcast_to(sums, upward.shape)
@@ -422,11 +442,11 @@
     layers = [residual_ref[z] - step * layers_ref[z] for z in range(16)]
     modes = solved(layers, waves_ref[0] - step * low, waves_ref[1] - step * high, rho_ref[...], scale_ref[...])
     scalars_ref[...] = lane_row([layers_total(layers, modes[1:-1]), aligned, curvature])
-    send_rims(out_ref, modes, table_ref[...], source_ref[:, 256:768])
+    send_rims(out_ref, modes, table_ref, source_ref[:, 256:768])
 
 
 def second_image(message_ref, scalars_ref, applied_ref, table_ref, beta_x_ref, beta_y_ref, beta_z_ref, slots_ref, out_ref):
-    slots = from_rims(from_tiles(message_ref[...], 2), table_ref[...])
+    slots = from_rims(from_tiles(message_ref[...], 2), table_ref)
     slots_ref[...] = slots
     bent = total(slots[8:40] * applied_rows(slots, beta_x_ref[...], beta_y_ref[...], beta_z_ref[...]))
     crossed = total(slots[8:40] * applied_ref[...])
@@ -463,7 +483,7 @@
     kept = jax.ShapeDtypeStruct if last else pltpu.VMEM
     return pl.pallas_call(
         kernel,
-        out_shape=[kept(shape, jnp.float32) for shape in outs],
+        out_shape=[kept(shape, jnp.bfloat16 if shape[0] == 3 and not last else jnp.float32) for shape in outs],
         in_specs=[scalar if small else whole for small in scalars],
         out_specs=[whole] * len(outs),
         compiler_params=pltpu.CompilerParams(vmem_limit_bytes=8 << 20),
@@ -542,7 +562,7 @@
     part_x = NX // peers
     plain_x = cosine_table(NX).reshape(peers, part_x, NX).transpose(1, 0, 2).reshape(NX, NX)
     table_x = jnp.asarray(plain_x, dtype=jnp.float32)
-    (message,) = run(send_fields, [(peers, 2, 128)], provisional, table_x)
+    message, table_x = run(send_fields, [(peers, 2, 128), (3, NX, NX)], provisional, table_x)
 
     places = jnp.stack([row_index, chip_index, core_index]).astype(jnp.int32)
 
@@ -557,10 +577,10 @@
     half_y = half_eigenvalue(total_rows).reshape(2, 1, 128)
     half_y = jnp.asarray(np.broadcast_to(half_y, (2, 4, 128)).reshape(8, 128), dtype=jnp.float32)
     size = cols * cores
-    *betas, rho, scale, weights = run(
+    *betas, rho, scale, weights, table_y = run(
         prepare,
-        [(rows, cols, NX), (rows + 1, cols, NX), (2, rows, cols, NX), (8, 128), (8, 128), (4, chips, 8, 128)],
-        places, half_x, half_y, fraction, y_low[9], y_high[9], z_low[9], z_high[9],
+        [(rows, cols, NX), (rows + 1, cols, NX), (2, rows, cols, NX), (8, 128), (8, 128), (4, chips, 8, 128), (3, total_rows, total_rows)],
+        places, half_x, half_y, table_y, fraction, y_low[9], y_high[9], z_low[9], z_high[9],
     )
     place = places[1:2]
 

time: 174 us -> 177 us (1.017)
  transfers between devices with their start and end apart: 5 -> 5, of which waited for: 2 -> 2; matrix products, arithmetic and copies ran while one was open for 1% -> 2% of each run, Pallas kernels for 0% -> 0%
where the time goes in v7:
time: 177 us; the launch traced here: 176 us
  blocking collectives  108 us (61%)
  starting transfers between devices  35.7 us (20%)
  waiting for transfers between devices  15.1 us (9%)
  Pallas kernels  9.62 us (5%)
  local copies, waits for them, and re-layouts  4.28 us (2%)
  other arithmetic  2.66 us (2%)
    all_to_all x7, blocking collectives, exchange(): lax.all_to_all(message, axis, split_axis=0, concat_axis=0, tiled=True)  108 us
    ppermute x4, starting transfers between devices, swapped(): return lax.ppermute(values, axis, pairs)  20.5 us
    all_to_all x1, starting transfers between devices, exchange(): lax.all_to_all(message, axis, split_axis=0, concat_axis=0, tiled=True)  15.1 us
    all_to_all x1, waiting for transfers between devices, exchange(): lax.all_to_all(message, axis, split_axis=0, concat_axis=0, tiled=True)  11.9 us
    pallas_call x10, Pallas kernels, run(): pl.pallas_call(kernel, out_shape=[kept(shape, jnp.bfloat16 if shape[0] ==...  9.62 us
  transfers between devices with their start and end apart: 5, of which 2 were waited for; matrix products, arithmetic and copies ran while one was open for 2% of the time, Pallas kernels for 0%

profile of v7, /device:TPU:1, one launch (start us, length us, event | category | flops | bytes accessed | tf_op | source)
XLA Modules:
  0.0 176.1 jit_solution(14928862495996503136)
XLA Ops:
  0.7 1.0 fusion.27
  1.6 1.1 slice_bitcast_fusion.1
  2.9 16.0 %collective-permute-start.2 = (f32[10,4,512]{2,1,0:T(4,128)S(1)}, f32[10,4,512]{2,1,0:T(4,128)S(1)}, u32[]{:S(2)}, u32[]{:S(2)}) collective-permute-start(f32[10,4,512]{2,1,0:T(4,128)S(1)} %get-tuple-element.68), channel_id=1, source_target_pairs={{0,1},{2,3},{4,5},{6,7},{8,9},{10,11},{12,13},{14,15},{1,0},{3,2},... | collective-permute-start | bytes 245768 | tf_op jit(solution)/shard_map/ppermute | solution.py:82
  18.9 1.9 %collective-permute-start.3 = (f32[10,4,512]{2,1,0:T(4,128)S(1)}, f32[10,4,512]{2,1,0:T(4,128)S(1)}, u32[]{:S(2)}, u32[]{:S(2)}) collective-permute-start(f32[10,4,512]{2,1,0:T(4,128)S(1)} %get-tuple-element.69), channel_id=1, source_target_pairs={{1,2},{3,4},{5,6},{7,8},{9,10},{11,12},{13,14},{2,1},{4,3},{6,5},{... | collective-permute-start | bytes 245768 | tf_op jit(solution)/shard_map/ppermute | solution.py:82
  21.6 1.0 fusion.25
  22.6 1.9 %collective-permute-start = (f32[10,8,512]{2,1,0:T(8,128)S(1)}, f32[10,8,512]{2,1,0:T(8,128)S(1)}, u32[]{:S(2)}, u32[]{:S(2)}) collective-permute-start(f32[10,8,512]{2,1,0:T(8,128)S(1)} %get-tuple-element.52), channel_id=1, source_target_pairs={{0,16},{32,48},{64,80},{96,112},{128,144},{160,176},{192,208},{224... | collective-permute-start | bytes 491528 | tf_op jit(solution)/shard_map/ppermute | solution.py:82
  26.4 3.2 %collective-permute-done = f32[10,8,512]{2,1,0:T(8,128)S(1)} collective-permute-done((f32[10,8,512]{2,1,0:T(8,128)S(1)}, f32[10,8,512]{2,1,0:T(8,128)S(1)}, u32[]{:S(2)}, u32[]{:S(2)}) %collective-permute-start) | collective-permute-done | bytes 163872 | tf_op jit(solution)/shard_map/ppermute | solution.py:82
  29.8 1.8 %fusion.6.provisional_ref = f32[3,4,8,512]{3,2,1,0:T(8,128)S(1)} fusion(f32[3,4,8,512]{3,2,1,0:T(8,128)S(1)} %copy-done.6, f32[3,4,3,512]{3,2,1,0:T(4,128)S(1)} %bitcast.66, f32[3,4,3,512]{3,2,1,0:T(4,128)S(1)} %bitcast.68, f32[3,3,8,512]{3,2,1,0:T(8,128)S(1)} %bitcast.62, f32[3,3,8,512]{3,2,1,0:T(8,128)S(1)} %bitcast.64, ...), kind=kLoop, calls=%fused_computation.16 | loop fusion | flops 11943936 | bytes 4688128 | tf_op jit(solution)/shard_map/add | solution.py:70
  31.6 1.8 %shard_map.95 = (f32[128,2,128]{2,1,0:T(2,128)}, bf16[3,512,512]{2,1,0:T(8,128)(2,1)S(1)}) custom-call(f32[3,4,8,512]{3,2,1,0:T(8,128)S(1)} %fusion.6.provisional_ref, f32[512,512]{1,0:T(8,128)S(1)} %copy-done), custom_call_target="tpu_custom_call" | custom-call | tf_op jit(solution)/shard_map/pallas_call | solution.py:484
  33.5 15.1 %all-to-all-start = ((f32[128,2,128]{2,1,0:T(2,128)}), f32[128,2,128]{2,1,0:T(2,128)S(1)}, u32[]{:S(2)}, u32[]{:S(2)}) async-start(f32[128,2,128]{2,1,0:T(2,128)} %get-tuple-element.26), calls=%async_computation | async-start | bytes 262144 | tf_op jit(solution)/shard_map/all_to_all | solution.py:108
  48.7 0.8 shard_map.96
  49.4 11.9 %all-to-all-done = f32[128,2,128]{2,1,0:T(2,128)S(1)} async-done(((f32[128,2,128]{2,1,0:T(2,128)}), f32[128,2,128]{2,1,0:T(2,128)S(1)}, u32[]{:S(2)}, u32[]{:S(2)}) %all-to-all-start) | async-done | bytes 131104 | tf_op jit(solution)/shard_map/all_to_all | solution.py:108
  62.1 15.4 %all_to_all.40.gather_ref = f32[8,32,128]{2,1,0:T(8,128)S(1)} all-to-all(f32[8,32,128]{2,1,0:T(8,128)S(1)} %get-tuple-element.29), channel_id=1, replica_groups=mesh['py'=64,'px'=8,'core'=2] {'px'}, dimensions={0} | all-to-all | bytes 262144 | tf_op jit(solution)/shard_map/all_to_all | solution.py:108
  77.5 0.9 shard_map.98
  78.4 19.5 %all_to_all.41.message_ref = f32[128,2,128]{2,1,0:T(2,128)S(1)} all-to-all(f32[128,2,128]{2,1,0:T(2,128)S(1)} %bitcast.60), channel_id=1, replica_groups=mesh['py'=64,'px'=8,'core'=2] {'py','core'}, dimensions={0} | all-to-all | bytes 262144 | tf_op jit(solution)/shard_map/all_to_all | solution.py:108
  97.9 1.8 %shard_map.99 = (f32[128,2,128]{2,1,0:T(2,128)S(1)}, f32[64,512]{1,0:T(8,128)S(1)}, f32[32,512]{1,0:T(8,128)S(1)}) custom-call(f32[128,2,128]{2,1,0:T(2,128)S(1)} %all_to_all.41.message_ref, f32[1,128]{1,0:T(1,128)S(1)} %get-tuple-element.34.aligned_ref, bf16[3,512,512]{2,1,0:T(8,128)(2,1)S(1)} %get-tuple-element.35.table_ref, ...), custom_call_target="tpu_custom_call" | custom-call | tf_op jit(solution)/shard_map/pallas_call | solution.py:484
  99.7 17.9 %all_to_all.42 = f32[128,2,128]{2,1,0:T(2,128)S(1)} all-to-all(f32[128,2,128]{2,1,0:T(2,128)S(1)} %get-tuple-element.39), channel_id=1, replica_groups=mesh['py'=64,'px'=8,'core'=2] {'py','core'}, dimensions={0} | all-to-all | bytes 262144 | tf_op jit(solution)/shard_map/all_to_all | solution.py:108
  118.2 9.9 %all_to_all.43.gather_ref = f32[8,24,128]{2,1,0:T(8,128)S(1)} all-to-all(f32[8,24,128]{2,1,0:T(8,128)S(1)} %get-tuple-element.40), channel_id=1, replica_groups=mesh['py'=64,'px'=8,'core'=2] {'px'}, dimensions={0} | all-to-all | bytes 196608 | tf_op jit(solution)/shard_map/all_to_all | solution.py:108
  128.1 1.0 shard_map.101
  129.1 19.1 %all_to_all.44.message_ref = f32[128,2,128]{2,1,0:T(2,128)S(1)} all-to-all(f32[128,2,128]{2,1,0:T(2,128)S(1)} %bitcast.59), channel_id=1, replica_groups=mesh['py'=64,'px'=8,'core'=2] {'py','core'}, dimensions={0} | all-to-all | bytes 262144 | tf_op jit(solution)/shard_map/all_to_all | solution.py:108
  148.2 0.8 shard_map.102
  149.1 14.7 %all_to_all.45.parts_ref = f32[64,1,128]{2,1,0:T(1,128)S(1)} all-to-all(f32[64,1,128]{2,1,0:T(1,128)S(1)} %get-tuple-element.47), channel_id=1, replica_groups=mesh['py'=64,'px'=8,'core'=2] {'py'}, dimensions={0} | all-to-all | bytes 65536 | tf_op jit(solution)/shard_map/all_to_all | solution.py:108
  163.8 11.2 %all_to_all.46.parts_ref = f32[16,1,128]{2,1,0:T(1,128)S(1)} all-to-all(f32[16,1,128]{2,1,0:T(1,128)S(1)} %shard_map.103), channel_id=1, replica_groups=mesh['py'=64,'px'=8,'core'=2] {'px','core'}, dimensions={0} | all-to-all | bytes 16384 | tf_op jit(solution)/shard_map/all_to_all | solution.py:108
  175.0 1.1 shard_map.104
  (58 shorter events, 4.2 us)
Async XLA Ops:
  0.6 24.7 %copy-start.1 = (f32[4,8,512]{2,1,0:T(8,128)S(1)}, f32[4,8,512]{2,1,0:T(8,128)}, u32[]{:S(2)}) copy-start(f32[4,8,512]{2,1,0:T(8,128)} %fraction_ref.1) | copy-start | bytes 196612
  0.6 24.6 %copy-start.6 = (f32[3,4,8,512]{3,2,1,0:T(8,128)S(1)}, f32[3,4,8,512]{3,2,1,0:T(8,128)}, u32[]{:S(2)}) copy-start(f32[3,4,8,512]{3,2,1,0:T(8,128)} %param.8) | copy-start | bytes 589828
  2.7 22.7 %copy-start.7 = (s32[2,4,8]{2,1,0:T(4,128)S(1)}, s32[2,4,8]{2,1,0:T(4,128)}, u32[]{:S(2)}) copy-start(s32[2,4,8]{2,1,0:T(4,128)} %param.10) | copy-start | bytes 772
  2.9 23.3 %collective-permute-start.2 = (f32[10,4,512]{2,1,0:T(4,128)S(1)}, f32[10,4,512]{2,1,0:T(4,128)S(1)}, u32[]{:S(2)}, u32[]{:S(2)}) collective-permute-start(f32[10,4,512]{2,1,0:T(4,128)S(1)} %get-tuple-element.68), channel_id=1, source_target_pairs={{0,1},{2,3},{4,5},{6,7},{8,9},{10,11},{12,13},{14,15},{1,0},{3,2},... | collective-permute-start | bytes 245768 | tf_op jit(solution)/shard_map/ppermute | solution.py:82
  18.9 7.3 %collective-permute-start.3 = (f32[10,4,512]{2,1,0:T(4,128)S(1)}, f32[10,4,512]{2,1,0:T(4,128)S(1)}, u32[]{:S(2)}, u32[]{:S(2)}) collective-permute-start(f32[10,4,512]{2,1,0:T(4,128)S(1)} %get-tuple-element.69), channel_id=1, source_target_pairs={{1,2},{3,4},{5,6},{7,8},{9,10},{11,12},{13,14},{2,1},{4,3},{6,5},{... | collective-permute-start | bytes 245768 | tf_op jit(solution)/shard_map/ppermute | solution.py:82
  22.6 7.0 %collective-permute-start = (f32[10,8,512]{2,1,0:T(8,128)S(1)}, f32[10,8,512]{2,1,0:T(8,128)S(1)}, u32[]{:S(2)}, u32[]{:S(2)}) collective-permute-start(f32[10,8,512]{2,1,0:T(8,128)S(1)} %get-tuple-element.52), channel_id=1, source_target_pairs={{0,16},{32,48},{64,80},{96,112},{128,144},{160,176},{192,208},{224... | collective-permute-start | bytes 491528 | tf_op jit(solution)/shard_map/ppermute | solution.py:82
  24.5 5.1 %collective-permute-start.1 = (f32[10,8,512]{2,1,0:T(8,128)S(1)}, f32[10,8,512]{2,1,0:T(8,128)S(1)}, u32[]{:S(2)}, u32[]{:S(2)}) collective-permute-start(f32[10,8,512]{2,1,0:T(8,128)S(1)} %get-tuple-element.53), channel_id=1, source_target_pairs={{16,32},{48,64},{80,96},{112,128},{144,160},{176,192},{208,224},{2... | collective-permute-start | bytes 491528 | tf_op jit(solution)/shard_map/ppermute | solution.py:82
  29.8 1.8 %copy-start = (f32[512,512]{1,0:T(8,128)S(1)}, f32[512,512]{1,0:T(8,128)}, u32[]{:S(2)}) copy-start(f32[512,512]{1,0:T(8,128)} %constant.110.clone.table_ref) | copy-start | bytes 3145732
  31.6 17.0 %copy-start.2 = (f32[256,256]{1,0:T(8,128)S(1)}, f32[256,256]{1,0:T(8,128)}, u32[]{:S(2)}) copy-start(f32[256,256]{1,0:T(8,128)} %constant.111.clone.table_ref) | copy-start | bytes 786436
  31.6 17.0 %copy-start.4 = (f32[8,128]{1,0:T(8,128)S(1)}, f32[8,128]{1,0:T(8,128)}, u32[]{:S(2)}) copy-start(f32[8,128]{1,0:T(8,128)} %constant.114.clone.half_y_ref) | copy-start | bytes 12292
  31.6 17.0 %copy-start.5 = (f32[512]{0:T(512)S(1)}, f32[512]{0:T(512)}, u32[]{:S(2)}) copy-start(f32[512]{0:T(512)} %constant.113.clone.half_x_ref) | copy-start | bytes 6148
  31.6 29.7 %copy-start.3 = (s32[1,1536]{1,0:T(1,128)S(1)}, s32[1,1536]{1,0:T(1,128)}, u32[]{:S(2)}) copy-start(s32[1,1536]{1,0:T(1,128)} %constant.112.clone.source_ref) | copy-start | bytes 18436
  33.5 27.9 %all-to-all-start = ((f32[128,2,128]{2,1,0:T(2,128)}), f32[128,2,128]{2,1,0:T(2,128)S(1)}, u32[]{:S(2)}, u32[]{:S(2)}) async-start(f32[128,2,128]{2,1,0:T(2,128)} %get-tuple-element.26), calls=%async_computation | async-start | bytes 262144 | tf_op jit(solution)/shard_map/all_to_all | solution.py:108

commit v8 on v7

--- a/solution.py
+++ b/solution.py
@@ -82,13 +82,13 @@
     return lax.ppermute(values, axis, pairs)
 
 
-def shifted_pair(head, tail, axis):
+def shifted_pair(one, two, axis):
     count = lax.axis_size(axis)
     even = (lax.axis_index(axis) & 1) == 0
     inner = [(i, i + 1) for i in range(0, count, 2)]
     outer = [(i, i + 1) for i in range(1, count - 1, 2)]
-    two = swapped(jnp.where(even, head, tail), axis, outer + [(j, i) for i, j in outer])
-    one = swapped(jnp.where(even, tail, head), axis, inner + [(j, i) for i, j in inner])
+    one = swapped(one, axis, inner + [(j, i) for i, j in inner])
+    two = swapped(two, axis, outer + [(j, i) for i, j in outer])
     return jnp.where(even, two, one), jnp.where(even, one, two)
 
 
@@ -284,6 +284,21 @@
     for index, value in enumerate(values):
         row = jnp.where(lane == index, value, row)
     return row
+
+
+def rims(odd_ref, velocity_ref, fraction_ref, y_one_ref, y_two_ref, z_one_ref, z_two_ref):
+    odd_y, odd_z = odd_ref[0] == 1, odd_ref[1] == 1
+
+    def place(one_ref, two_ref, index, head, tail, odd):
+        one_ref[index] = jnp.where(odd, head, tail)
+        two_ref[index] = jnp.where(odd, tail, head)
+
+    for c in range(3):
+        for m in range(3):
+            place(y_one_ref, y_two_ref, 3 * c + m, velocity_ref[c, m], velocity_ref[c, m + 1], odd_y)
+            place(z_one_ref, z_two_ref, 3 * c + m, velocity_ref[c, :, m, :], velocity_ref[c, :, m + 5, :], odd_z)
+    place(y_one_ref, y_two_ref, 9, fraction_ref[0], fraction_ref[3], odd_y)
+    place(z_one_ref, z_two_ref, 9, fraction_ref[:, 0, :], fraction_ref[:, 7, :], odd_z)
 
 
 def send_fields(provisional_ref, table_ref, out_ref, pieces_ref):
@@ -534,18 +549,12 @@
     chip_index = lax.axis_index("px")
     core_index = lax.axis_index("core")
 
-    def y_layers(part):
-        return part.reshape(9, cols, NX)
-
-    y_head = jnp.concatenate([y_layers(velocity[:, :3]), fraction[:1]], axis=0)
-    y_tail = jnp.concatenate([y_layers(velocity[:, -3:]), fraction[-1:]], axis=0)
-    y_low, y_high = shifted_pair(y_head, y_tail, "py")
-
-    def z_layers(first, only):
-        lanes = jnp.transpose(velocity[:, :, first : first + 3], (0, 2, 1, 3)).reshape(9, rows, NX)
-        return jnp.concatenate([lanes, fraction[:, only][None]], axis=0)
-
-    z_low, z_high = shifted_pair(z_layers(0, 0), z_layers(cols - 3, cols - 1), ("px", "core"))
+    odd = jnp.stack([row_index & 1, core_index]).astype(jnp.int32)
+    y_one, y_two, z_one, z_two = run(
+        rims, [(10, cols, NX), (10, cols, NX), (10, rows, NX), (10, rows, NX)], odd, velocity, fraction
+    )
+    y_low, y_high = shifted_pair(y_one, y_two, "py")
+    z_low, z_high = shifted_pair(z_one, z_two, ("px", "core"))
 
     def unlayered(z_rim):
         return jnp.transpose(z_rim[:9].reshape(3, 3, rows, NX), (0, 2, 1, 3))

time: 177 us -> 175 us (0.989)
  waiting for transfers between devices: 15.1 us -> 11.9 us
  other arithmetic: 2.66 us -> 5.1 us
    ppermute x4, waiting for transfers between devices: 3.21 us -> 0.01 us  [swapped(): return lax.ppermute(values, axis, pairs)]
    slice x3 -> x0, local copies, waits for them, and re-layouts: 2.72 us -> none  [the longest x1 1 us: on_device(): velocity[:, -3:]]
    pallas_call x10 -> x11, Pallas kernels: 9.62 us -> 10.2 us  [run(): pl.pallas_call(kernel, out_shape=[kept(shape, jnp.bfloat16 if shape[0] ==...]
  transfers between devices with their start and end apart: 5 -> 5, of which waited for: 2 -> 1; matrix products, arithmetic and copies ran while one was open for 2% -> 3% of each run, Pallas kernels for 0% -> 0%
where the time goes in v8:
time: 175 us
  blocking collectives  108 us (62%)
  starting transfers between devices  34.9 us (20%)
  waiting for transfers between devices  11.9 us (7%)
  Pallas kernels  10.2 us (6%)
  other arithmetic  5.1 us (3%)
  local copies, waits for them, and re-layouts  3.92 us (2%)
    all_to_all x7, blocking collectives, exchange(): lax.all_to_all(message, axis, split_axis=0, concat_axis=0, tiled=True)  108 us
    ppermute x4, starting transfers between devices, swapped(): return lax.ppermute(values, axis, pairs)  20.5 us
    all_to_all x1, starting transfers between devices, exchange(): lax.all_to_all(message, axis, split_axis=0, concat_axis=0, tiled=True)  14.4 us
    all_to_all x1, waiting for transfers between devices, exchange(): lax.all_to_all(message, axis, split_axis=0, concat_axis=0, tiled=True)  11.9 us
    pallas_call x11, Pallas kernels, run(): pl.pallas_call(kernel, out_shape=[kept(shape, jnp.bfloat16 if shape[0] ==...  10.2 us
  transfers between devices with their start and end apart: 5, of which 1 were waited for; matrix products, arithmetic and copies ran while one was open for 3% of the time, Pallas kernels for 0%

profile of v8, /device:TPU:1, one launch (start us, length us, event | category | flops | bytes accessed | tf_op | source)
XLA Modules:
  0.0 174.6 jit_solution(12259004853488417192)
XLA Ops:
  0.7 0.9 copy-done
  1.6 0.8 copy-done.3
  3.1 16.0 %collective-permute-start.2 = (f32[10,4,512]{2,1,0:T(4,128)S(1)}, f32[10,4,512]{2,1,0:T(4,128)S(1)}, u32[]{:S(2)}, u32[]{:S(2)}) collective-permute-start(f32[10,4,512]{2,1,0:T(4,128)S(1)} %get-tuple-element.32), channel_id=1, source_target_pairs={{0,1},{2,3},{4,5},{6,7},{8,9},{10,11},{12,13},{14,15},{1,0},{3,2},... | collective-permute-start | bytes 245768 | tf_op jit(solution)/shard_map/ppermute | solution.py:82
  19.1 1.9 %collective-permute-start.3 = (f32[10,4,512]{2,1,0:T(4,128)S(1)}, f32[10,4,512]{2,1,0:T(4,128)S(1)}, u32[]{:S(2)}, u32[]{:S(2)}) collective-permute-start(f32[10,4,512]{2,1,0:T(4,128)S(1)} %get-tuple-element.33), channel_id=1, source_target_pairs={{1,2},{3,4},{5,6},{7,8},{9,10},{11,12},{13,14},{2,1},{4,3},{6,5},{... | collective-permute-start | bytes 245768 | tf_op jit(solution)/shard_map/ppermute | solution.py:82
  21.0 1.9 %collective-permute-start = (f32[10,8,512]{2,1,0:T(8,128)S(1)}, f32[10,8,512]{2,1,0:T(8,128)S(1)}, u32[]{:S(2)}, u32[]{:S(2)}) collective-permute-start(f32[10,8,512]{2,1,0:T(8,128)S(1)} %get-tuple-element.30), channel_id=1, source_target_pairs={{0,16},{32,48},{64,80},{96,112},{128,144},{160,176},{192,208},{224... | collective-permute-start | bytes 491528 | tf_op jit(solution)/shard_map/ppermute | solution.py:82
  23.7 0.9 compare_bitcast_fusion.2
  24.6 0.9 add_divide_fusion
  25.5 0.9 fusion.20
  26.4 0.9 slice_bitcast_fusion.2
  29.2 1.8 %fusion.6.provisional_ref = f32[3,4,8,512]{3,2,1,0:T(8,128)S(1)} fusion(f32[3,4,8,512]{3,2,1,0:T(8,128)S(1)} %copy-done.1, f32[3,4,3,512]{3,2,1,0:T(4,128)S(1)} %get-tuple-element.78, f32[3,4,3,512]{3,2,1,0:T(4,128)S(1)} %get-tuple-element.79, f32[3,3,8,512]{3,2,1,0:T(8,128)S(1)} %bitcast.49, f32[3,3,8,512]{3,2,1,0:T(8,128)S(1)} %bitcast.51, ...), kind=kLoop, calls=%fused_computation.16 | loop fusion | flops 11943936 | bytes 4688128 | tf_op jit(solution)/shard_map/add | solution.py:70
  31.0 1.8 %shard_map.96 = (f32[128,2,128]{2,1,0:T(2,128)}, bf16[3,512,512]{2,1,0:T(8,128)(2,1)S(1)}) custom-call(f32[3,4,8,512]{3,2,1,0:T(8,128)S(1)} %fusion.6.provisional_ref, f32[512,512]{1,0:T(8,128)S(1)} %copy-done.2), custom_call_target="tpu_custom_call" | custom-call | tf_op jit(solution)/shard_map/pallas_call | solution.py:499
  32.8 14.4 %all-to-all-start = ((f32[128,2,128]{2,1,0:T(2,128)}), f32[128,2,128]{2,1,0:T(2,128)S(1)}, u32[]{:S(2)}, u32[]{:S(2)}) async-start(f32[128,2,128]{2,1,0:T(2,128)} %get-tuple-element.34), calls=%async_computation | async-start | bytes 262144 | tf_op jit(solution)/shard_map/all_to_all | solution.py:108
  48.0 11.9 %all-to-all-done = f32[128,2,128]{2,1,0:T(2,128)S(1)} async-done(((f32[128,2,128]{2,1,0:T(2,128)}), f32[128,2,128]{2,1,0:T(2,128)S(1)}, u32[]{:S(2)}, u32[]{:S(2)}) %all-to-all-start) | async-done | bytes 131104 | tf_op jit(solution)/shard_map/all_to_all | solution.py:108
  60.7 15.3 %all_to_all.40.gather_ref = f32[8,32,128]{2,1,0:T(8,128)S(1)} all-to-all(f32[8,32,128]{2,1,0:T(8,128)S(1)} %get-tuple-element.37), channel_id=1, replica_groups=mesh['py'=64,'px'=8,'core'=2] {'px'}, dimensions={0} | all-to-all | bytes 262144 | tf_op jit(solution)/shard_map/all_to_all | solution.py:108
  75.9 0.9 shard_map.99
  76.8 19.5 %all_to_all.41.message_ref = f32[128,2,128]{2,1,0:T(2,128)S(1)} all-to-all(f32[128,2,128]{2,1,0:T(2,128)S(1)} %bitcast.47), channel_id=1, replica_groups=mesh['py'=64,'px'=8,'core'=2] {'py','core'}, dimensions={0} | all-to-all | bytes 262144 | tf_op jit(solution)/shard_map/all_to_all | solution.py:108
  96.3 1.8 %shard_map.100 = (f32[128,2,128]{2,1,0:T(2,128)S(1)}, f32[64,512]{1,0:T(8,128)S(1)}, f32[32,512]{1,0:T(8,128)S(1)}) custom-call(f32[128,2,128]{2,1,0:T(2,128)S(1)} %all_to_all.41.message_ref, f32[1,128]{1,0:T(1,128)S(1)} %get-tuple-element.42.aligned_ref, bf16[3,512,512]{2,1,0:T(8,128)(2,1)S(1)} %get-tuple-element.43.table_ref, ...), custom_call_target="tpu_custom_call" | custom-call | tf_op jit(solution)/shard_map/pallas_call | solution.py:499
  98.1 17.9 %all_to_all.42 = f32[128,2,128]{2,1,0:T(2,128)S(1)} all-to-all(f32[128,2,128]{2,1,0:T(2,128)S(1)} %get-tuple-element.47), channel_id=1, replica_groups=mesh['py'=64,'px'=8,'core'=2] {'py','core'}, dimensions={0} | all-to-all | bytes 262144 | tf_op jit(solution)/shard_map/all_to_all | solution.py:108
  116.6 9.9 %all_to_all.43.gather_ref = f32[8,24,128]{2,1,0:T(8,128)S(1)} all-to-all(f32[8,24,128]{2,1,0:T(8,128)S(1)} %get-tuple-element.48), channel_id=1, replica_groups=mesh['py'=64,'px'=8,'core'=2] {'px'}, dimensions={0} | all-to-all | bytes 196608 | tf_op jit(solution)/shard_map/all_to_all | solution.py:108
  126.5 1.0 shard_map.102
  127.5 19.1 %all_to_all.44.message_ref = f32[128,2,128]{2,1,0:T(2,128)S(1)} all-to-all(f32[128,2,128]{2,1,0:T(2,128)S(1)} %bitcast.46), channel_id=1, replica_groups=mesh['py'=64,'px'=8,'core'=2] {'py','core'}, dimensions={0} | all-to-all | bytes 262144 | tf_op jit(solution)/shard_map/all_to_all | solution.py:108
  147.5 14.7 %all_to_all.45.parts_ref = f32[64,1,128]{2,1,0:T(1,128)S(1)} all-to-all(f32[64,1,128]{2,1,0:T(1,128)S(1)} %get-tuple-element.55), channel_id=1, replica_groups=mesh['py'=64,'px'=8,'core'=2] {'py'}, dimensions={0} | all-to-all | bytes 65536 | tf_op jit(solution)/shard_map/all_to_all | solution.py:108
  162.3 11.2 %all_to_all.46.parts_ref = f32[16,1,128]{2,1,0:T(1,128)S(1)} all-to-all(f32[16,1,128]{2,1,0:T(1,128)S(1)} %shard_map.104), channel_id=1, replica_groups=mesh['py'=64,'px'=8,'core'=2] {'px','core'}, dimensions={0} | all-to-all | bytes 16384 | tf_op jit(solution)/shard_map/all_to_all | solution.py:108
  173.4 1.1 shard_map.105
  (51 shorter events, 6.2 us)
Async XLA Ops:
  0.7 0.9 copy-start
  1.6 0.8 copy-start.3
  2.5 25.9 %copy-start.1 = (f32[3,4,8,512]{3,2,1,0:T(8,128)S(1)}, f32[3,4,8,512]{3,2,1,0:T(8,128)}, u32[]{:S(2)}) copy-start(f32[3,4,8,512]{3,2,1,0:T(8,128)} %velocity_ref.1) | copy-start | bytes 589828
  3.1 25.6 %collective-permute-start.2 = (f32[10,4,512]{2,1,0:T(4,128)S(1)}, f32[10,4,512]{2,1,0:T(4,128)S(1)}, u32[]{:S(2)}, u32[]{:S(2)}) collective-permute-start(f32[10,4,512]{2,1,0:T(4,128)S(1)} %get-tuple-element.32), channel_id=1, source_target_pairs={{0,1},{2,3},{4,5},{6,7},{8,9},{10,11},{12,13},{14,15},{1,0},{3,2},... | collective-permute-start | bytes 245768 | tf_op jit(solution)/shard_map/ppermute | solution.py:82
  19.1 9.6 %collective-permute-start.3 = (f32[10,4,512]{2,1,0:T(4,128)S(1)}, f32[10,4,512]{2,1,0:T(4,128)S(1)}, u32[]{:S(2)}, u32[]{:S(2)}) collective-permute-start(f32[10,4,512]{2,1,0:T(4,128)S(1)} %get-tuple-element.33), channel_id=1, source_target_pairs={{1,2},{3,4},{5,6},{7,8},{9,10},{11,12},{13,14},{2,1},{4,3},{6,5},{... | collective-permute-start | bytes 245768 | tf_op jit(solution)/shard_map/ppermute | solution.py:82
  21.0 8.0 %collective-permute-start = (f32[10,8,512]{2,1,0:T(8,128)S(1)}, f32[10,8,512]{2,1,0:T(8,128)S(1)}, u32[]{:S(2)}, u32[]{:S(2)}) collective-permute-start(f32[10,8,512]{2,1,0:T(8,128)S(1)} %get-tuple-element.30), channel_id=1, source_target_pairs={{0,16},{32,48},{64,80},{96,112},{128,144},{160,176},{192,208},{224... | collective-permute-start | bytes 491528 | tf_op jit(solution)/shard_map/ppermute | solution.py:82
  23.0 6.0 %collective-permute-start.1 = (f32[10,8,512]{2,1,0:T(8,128)S(1)}, f32[10,8,512]{2,1,0:T(8,128)S(1)}, u32[]{:S(2)}, u32[]{:S(2)}) collective-permute-start(f32[10,8,512]{2,1,0:T(8,128)S(1)} %get-tuple-element.31), channel_id=1, source_target_pairs={{16,32},{48,64},{80,96},{112,128},{144,160},{176,192},{208,224},{2... | collective-permute-start | bytes 491528 | tf_op jit(solution)/shard_map/ppermute | solution.py:82
  29.2 1.8 %copy-start.2 = (f32[512,512]{1,0:T(8,128)S(1)}, f32[512,512]{1,0:T(8,128)}, u32[]{:S(2)}) copy-start(f32[512,512]{1,0:T(8,128)} %constant.110.clone.table_ref) | copy-start | bytes 3145732
  31.0 16.3 %copy-start.4 = (f32[4,8,512]{2,1,0:T(8,128)S(1)}, f32[4,8,512]{2,1,0:T(8,128)}, u32[]{:S(2)}) copy-start(f32[4,8,512]{2,1,0:T(8,128)} %fraction_ref.3) | copy-start | bytes 196612
  31.0 16.3 %copy-start.5 = (f32[256,256]{1,0:T(8,128)S(1)}, f32[256,256]{1,0:T(8,128)}, u32[]{:S(2)}) copy-start(f32[256,256]{1,0:T(8,128)} %constant.111.clone.table_ref) | copy-start | bytes 786436
  31.0 16.3 %copy-start.7 = (f32[8,128]{1,0:T(8,128)S(1)}, f32[8,128]{1,0:T(8,128)}, u32[]{:S(2)}) copy-start(f32[8,128]{1,0:T(8,128)} %constant.114.clone.half_y_ref) | copy-start | bytes 12292
  31.0 16.2 %copy-start.8 = (f32[512]{0:T(512)S(1)}, f32[512]{0:T(512)}, u32[]{:S(2)}) copy-start(f32[512]{0:T(512)} %constant.113.clone.half_x_ref) | copy-start | bytes 6148
  31.0 28.9 %copy-start.6 = (s32[1,1536]{1,0:T(1,128)S(1)}, s32[1,1536]{1,0:T(1,128)}, u32[]{:S(2)}) copy-start(s32[1,1536]{1,0:T(1,128)} %constant.112.clone.source_ref) | copy-start | bytes 18436
  32.8 27.1 %all-to-all-start = ((f32[128,2,128]{2,1,0:T(2,128)}), f32[128,2,128]{2,1,0:T(2,128)S(1)}, u32[]{:S(2)}, u32[]{:S(2)}) async-start(f32[128,2,128]{2,1,0:T(2,128)} %get-tuple-element.34), calls=%async_computation | async-start | bytes 262144 | tf_op jit(solution)/shard_map/all_to_all | solution.py:108
